TPU v7x, 32 devices: a whole 2x2x4 slice. The times are simulated.
32 devices in a mesh: grp: 2 (over y), feat: 4 (over z), rows: 4 (over x, core).
Axes of the slice: x: 2, y: 2, z: 4, core: 2. Of those that a mesh axis runs over, the one named last changes fastest.
Arguments:
- tile_values: bfloat16 [3072, 128, 128], P(('grp', 'feat', 'rows')), parts along dimension 0, may hold values from -6 to 6
- tile_row: int32 [3072], P(('grp', 'feat', 'rows')), parts along dimension 0, may hold values from 0 to 7
- tile_block: int32 [3072], P(('grp', 'feat', 'rows')), parts along dimension 0, may hold values from 0 to 47
- tile_count: int32 [3072], P(('grp', 'feat', 'rows')), parts along dimension 0, may hold values from 1 to 16384
- tile_owner: int32 [3072, 1], P(('grp', 'feat', 'rows')), parts along dimension 0, may hold values from 0 to 3, as said below
- cut_index: int32 [31, 49152], P(None, ('grp', 'feat')), parts along dimension 1, may hold values from 0 to 309, as said below
- gradients: bfloat16 [8, 32768], P(None, ('grp', 'feat', 'rows')), parts along dimension 1, may hold values from -6 to 6
Outputs:
- histogram: float32 [8, 32, 49152], P(None, None, ('grp', 'feat', 'rows')), parts along dimension 2
There are 2 independent parts, one for each index of `grp`. A program takes and returns all parts, laid end to end along the dimension named above; each array names one. Nothing has to cross between parts.
Inputs may be any that keep to these rules, and one draw needn't show every extreme that they name: `tile_owner`: at most 48 of the tiles of one device have the same feature group, and in every draw some feature group receives exactly 48 tiles from every device. `cut_index`: each feature's cut indices rise strictly along the first dimension.
All inputs are finite; a program needn't handle non-finite values.
Results may differ from a plain program's by a relative error of at most 0.007.
Values may be sent and summed in bfloat16 or wider, within the bound.
No kernel may reach another device: no remote copies, remote signals or barrier semaphores. Data moves between devices by JAX's collectives and lax.ppermute only.
A program may use at most 64 MiB of HBM per device.

v0:
```python
import math

import jax
import jax.numpy as jnp
from jax import lax
from jax.sharding import PartitionSpec as P


def bin_tiles(hist, values, meta, grads, cuts):
    count = values.shape[0]
    tile = values.shape[1]
    k_out = grads.shape[1]
    levels = cuts.shape[0] + 1
    width = math.gcd(count, 8)
    turns = count // width
    flat_pos = (
        jnp.arange(tile, dtype=jnp.int32)[:, None] * tile
        + jnp.arange(tile, dtype=jnp.int32)[None, :]
    )
    bin_ids = jnp.arange(levels, dtype=jnp.int32)

    def step(carry, x):
        vals, info, grad_rows = x
        vfloat = vals.astype(jnp.float32)
        cut_rows = jnp.take(cuts, info[:, 1], axis=1)
        level = jnp.zeros(vals.shape, jnp.int32)
        for c in range(levels - 1):
            level = level + (vfloat > cut_rows[c][:, None, :]).astype(jnp.int32)
        live = flat_pos[None] < info[:, 0][:, None, None]
        onehot = (
            (level[:, :, None, :] == bin_ids[None, None, :, None]) & live[:, :, None, :]
        ).astype(jnp.bfloat16)
        sums = jnp.einsum("wki,wibj->kbwj", grad_rows, onehot, preferred_element_type=jnp.float32)
        carry = carry.at[:, :, info[:, 1], :].add(sums)
        return (carry, None)

    xs = (
        values.reshape(turns, width, tile, tile),
        meta.reshape(turns, width, 3),
        grads.reshape(turns, width, k_out, tile),
    )
    hist, _ = lax.scan(step, hist, xs)
    return hist


def shards(tile_values, tile_row, tile_block, tile_count, tile_owner, cut_index, gradients):
    owners = lax.axis_size("feat")
    tile_dev = tile_values.shape[0]
    tile = tile_values.shape[1]
    levels = cut_index.shape[0] + 1
    k_out = gradients.shape[0]
    rows_dev = gradients.shape[1]
    row_blocks = rows_dev // tile
    fb_dev = cut_index.shape[1] // tile
    capacity = max(2, 2 * tile_dev // owners)
    slots = owners * capacity
    owner = tile_owner[:, 0]
    hits = (owner[:, None] == jnp.arange(owners, dtype=jnp.int32)[None, :]).astype(jnp.int32)
    before = jnp.cumsum(hits, axis=0) - hits
    rank = jnp.sum(before * hits, axis=1)
    target = owner * capacity + rank
    match = (target[None, :] == jnp.arange(slots, dtype=jnp.int32)[:, None]).astype(jnp.int32)
    source = jnp.sum(match * jnp.arange(tile_dev, dtype=jnp.int32)[None, :], axis=1)
    used = jnp.sum(match, axis=1)
    sent_values = jnp.take(tile_values, source, axis=0).reshape(owners, capacity, tile, tile)
    sent_rows = jnp.take(tile_row, source)
    meta = jnp.stack(
        [jnp.take(tile_count, source) * used, jnp.take(tile_block, source), sent_rows], axis=1
    ).reshape(owners, capacity, 3)
    cuts = ((cut_index.astype(jnp.float32) + (0.5 - 5.0 * (levels - 1))) / 64.0).reshape(
        levels - 1, fb_dev, tile
    )
    hist = jnp.zeros((k_out, levels, fb_dev, tile), jnp.float32)
    sender = jnp.arange(owners, dtype=jnp.int32)[:, None] * row_blocks
    gathered = lax.all_gather(gradients, "feat", axis=1, tiled=True).reshape(
        k_out, owners * row_blocks, tile
    )
    got_values, got_meta = (
        lax.all_to_all(sent_values, "feat", split_axis=0, concat_axis=0, tiled=True),
        lax.all_to_all(meta, "feat", split_axis=0, concat_axis=0, tiled=True),
    )
    number = got_values.shape[0] * got_values.shape[1]
    index = (sender + got_meta[:, :, 2]).reshape(number)
    picked = jnp.transpose(jnp.take(gathered, index, axis=1), (1, 0, 2))
    hist = bin_tiles(
        hist, got_values.reshape(number, tile, tile), got_meta.reshape(number, 3), picked, cuts
    )
    return lax.psum_scatter(
        hist.reshape(k_out, levels, fb_dev * tile).astype(jnp.bfloat16),
        "rows",
        scatter_dimension=2,
        tiled=True,
    ).astype(jnp.float32)


def solution(mesh):
    placed = (
        P(("grp", "feat", "rows"), None, None),
        P(("grp", "feat", "rows")),
        P(("grp", "feat", "rows")),
        P(("grp", "feat", "rows")),
        P(("grp", "feat", "rows"), None),
        P(None, ("grp", "feat")),
        P(None, ("grp", "feat", "rows")),
    )
    return jax.shard_map(
        shards,
        mesh=mesh,
        in_specs=placed,
        out_specs=P(None, None, ("grp", "feat", "rows")),
        check_vma=False,
    )
```

profile of v0, /device:TPU:0, one launch (start us, length us, event | category | flops | bytes accessed | tf_op | source)
XLA Modules:
  0.0 570.7 jit_solution(10430399734683316478)
XLA Ops:
  15.9 6.3 %all-to-all-start = ((s32[4,1,144]{2,1,0:T(1,128)}), s32[4,1,144]{2,1,0:T(1,128)S(1)}, u32[]{:S(2)}, u32[]{:S(2)}) async-start(s32[4,1,144]{2,1,0:T(1,128)} %reshape.324), calls=%async_computation | async-start | bytes 8192 | tf_op jit(solution)/shard_map/all_to_all | solution.py:80
  22.4 8.1 %gather_fusion.1 = bf16[192,128,128]{2,1,0:T(8,128)(2,1)} fusion(bf16[96,128,128]{2,1,0:T(8,128)(2,1)S(1)} %copy-done, s32[1024]{0:T(1024)S(1)} %pad_clamp_fusion.2), kind=kCustom, calls=%fused_computation.4 | custom fusion | bytes 12583680 | tf_op jit(solution)/shard_map/jit(_take)/gather | solution.py:65
  30.4 6.1 %broadcast_select_fusion = bf16[4,48,128,128]{3,2,1,0:T(8,128)(2,1)} fusion(bf16[4,48,128,128]{3,2,1,0:T(8,128)(2,1)} %bitcast.149, pred[4,48]{1,0:T(4,128)(4,1)S(1)} %compare_and_fusion.2), kind=kLoop, calls=%fused_computation.59 | loop fusion | flops 3145728 | bytes 12583104 | tf_op jit(solution)/shard_map/jit(_take)/select_n | solution.py:65
  36.5 5.4 all-to-all-start.1
  44.8 140.9 %all_gather.3 = bf16[8,4096]{1,0:T(8,128)(2,1)S(1)} all-gather(bf16[8,1024]{1,0:T(8,128)(2,1)S(1)} %copy-done.1), channel_id=1, replica_groups=mesh['grp'=2,'feat'=4,'rows'=4] {'feat'}, dimensions={1}, use_global_device_ids=true | all-gather | bytes 81920 | tf_op jit(solution)/shard_map/all_gather | solution.py:75
  190.8 3.5 broadcast_in_dim.51
  194.3 325.4 %while.11 = (s32[]{:T(128)}, f32[8,32,48,128]{3,1,2,0:T(8,128)}, s32[24,8,3]{1,0,2:T(8,128)S(1)}, bf16[24,8,128,128]{3,2,1,0:T(8,128)(2,1)}, f32[31,48,128]{2,0,...) while((s32[]{:T(128)}, f32[8,32,48,128]{3,1,2,0:T(8,128)}, ...), condition=%wide.region_6.8_spmd.clone, body=%wide.region_4.7_spmd.clone.sunk | while | flops 88129608 | bytes 8906009 | solution.py:42
  199.1 3.8 fusion.25
  204.0 3.7 scatter_fusion
  212.5 3.8 fusion.25
  217.5 3.7 scatter_fusion
  223.4 2.6 convert_add_fusion.2
  226.0 3.8 fusion.25
  231.0 3.8 scatter_fusion
  237.0 2.6 convert_add_fusion.2
  239.6 3.8 fusion.25
  244.5 3.9 scatter_fusion
  253.3 3.8 fusion.25
  258.2 3.9 scatter_fusion
  264.4 2.6 convert_add_fusion.2
  267.0 3.8 fusion.25
  271.9 3.9 scatter_fusion
  280.6 3.8 fusion.25
  285.6 3.8 scatter_fusion
  294.2 3.8 fusion.25
  299.1 3.6 scatter_fusion
  304.9 2.6 convert_add_fusion.2
  307.5 3.8 fusion.25
  312.5 3.9 scatter_fusion
  318.5 2.6 convert_add_fusion.2
  321.1 3.8 fusion.25
  326.1 3.9 scatter_fusion
  334.7 3.8 fusion.25
  339.7 3.9 scatter_fusion
  348.4 3.8 fusion.25
  353.3 3.9 scatter_fusion
  362.0 3.8 fusion.25
  367.0 3.8 scatter_fusion
  375.5 3.8 fusion.25
  380.5 3.7 scatter_fusion
  389.0 3.8 fusion.25
  394.0 3.5 scatter_fusion
  402.3 3.8 fusion.25
  407.3 3.6 scatter_fusion
  415.6 3.8 fusion.25
  420.6 3.6 scatter_fusion
  426.4 2.6 convert_add_fusion.2
  429.0 3.8 fusion.25
  434.0 3.6 scatter_fusion
  442.4 3.8 fusion.25
  447.4 3.8 scatter_fusion
  453.3 2.6 convert_add_fusion.2
  455.9 3.8 fusion.25
  460.9 3.8 scatter_fusion
  469.4 3.8 fusion.25
  474.4 4.0 scatter_fusion
  483.2 3.8 fusion.25
  488.2 4.0 scatter_fusion
  496.9 3.8 fusion.25
  501.9 4.0 scatter_fusion
  510.7 3.8 fusion.25
  515.7 4.0 scatter_fusion
  519.7 5.0 copy_bitcast_fusion.1
  524.7 36.7 %reduce-scatter.2.cloned.1.call-done = bf16[8,32,1536]{2,1,0:T(8,128)(2,1)} async-done(((bf16[8,32,6144]{2,1,0:T(8,128)(2,1)}), bf16[8,32,1536]{2,1,0:T(8,128)(2,1)}) %reduce-scatter.2.cloned.1.call-update) | async-done | bytes 786448 | tf_op jit(solution)/shard_map/reduce_scatter | solution.py:88
  (357 shorter events, 142.7 us)
Async XLA Ops:
  6.5 15.8 %copy-start = (bf16[96,128,128]{2,1,0:T(8,128)(2,1)S(1)}, bf16[96,128,128]{2,1,0:T(8,128)(2,1)}, u32[]{:S(2)}) copy-start(bf16[96,128,128]{2,1,0:T(8,128)(2,1)} %param.11) | copy-start | bytes 9437188
  15.9 20.6 %all-to-all-start = ((s32[4,1,144]{2,1,0:T(1,128)}), s32[4,1,144]{2,1,0:T(1,128)S(1)}, u32[]{:S(2)}, u32[]{:S(2)}) async-start(s32[4,1,144]{2,1,0:T(1,128)} %reshape.324), calls=%async_computation | async-start | bytes 8192 | tf_op jit(solution)/shard_map/all_to_all | solution.py:80
  36.5 8.3 %copy-start.1 = (bf16[8,1024]{1,0:T(8,128)(2,1)S(1)}, bf16[8,1024]{1,0:T(8,128)(2,1)}, u32[]{:S(2)}) copy-start(bf16[8,1024]{1,0:T(8,128)(2,1)} %param.17) | copy-start | bytes 49156
  36.5 154.3 %all-to-all-start.1 = ((bf16[4,48,128,128]{3,2,1,0:T(8,128)(2,1)}), bf16[4,48,128,128]{3,2,1,0:T(8,128)(2,1)}, u32[]{:S(2)}, u32[]{:S(2)}) async-start(bf16[4,48,128,128]{3,2,1,0:T(8,128)(2,1)} %broadcast_select_fusion), calls=%async_computation.1 | async-start | bytes 12582912 | tf_op jit(solution)/shard_map/all_to_all | solution.py:79
  41.9 519.5 %reduce-scatter.2.cloned.1.call-start = ((), (), s32[]{:S(2)}) async-start(), calls=%async_computation.3 | async-start | bytes 3932160 | tf_op jit(solution)/shard_map/reduce_scatter | solution.py:88
Sparse Core Ops, SparseCore 0:
  524.8 36.5 reduce-scatter.1
where the time goes:
time: 576 us; the launch traced here: 571 us
  other arithmetic  181 us (31%)
  blocking collectives  141 us (24%)
  local copies, waits for them, and re-layouts  93.1 us (16%)
  matrix products  91.7 us (16%)
  waiting for transfers between devices  36.8 us (6%)
  between operations  13.5 us (2%)
  starting transfers between devices  11.7 us (2%)
    all_gather x1, blocking collectives, shards(): lax.all_gather(gradients, 'feat', axis=1, tiled=True)  141 us
    dot_general x24, matrix products, step(): jnp.einsum('wki,wibj->kbwj', grad_rows, onehot, preferred_element_type=jn...  91.7 us
    scatter-add x24, other arithmetic, step(): carry = carry.at[:, :, info[:, 1], :].add(sums)  91.2 us
    add x24, other arithmetic, step(): level = level + (vfloat > cut_rows[c][:, None, :]).astype(jnp.int32)  62.3 us
    gather x24, local copies, waits for them, and re-layouts, step(): cut_rows = jnp.take(cuts, info[:, 1], axis=1)  40.5 us
    reduce_scatter x1, waiting for transfers between devices, shards(): lax.psum_scatter(hist.reshape(k_out, levels, fb_dev * tile).astype(jnp.bf...  36.7 us
    dot_general x24, local copies, waits for them, and re-layouts, step(): jnp.einsum('wki,wibj->kbwj', grad_rows, onehot, preferred_element_type=jn...  27.8 us
  transfers between devices with their start and end apart: 3, of which 1 were waited for; matrix products, arithmetic and copies ran while one was open for 4% of the time, Pallas kernels for 0%

commit v1 on v0

v1 whole, which is shorter than its diff:
```python
import functools

import jax
import jax.numpy as jnp
from jax import lax
from jax.experimental import pallas as pl
from jax.experimental.pallas import tpu as pltpu
from jax.sharding import PartitionSpec as P

ROWS_G = 16
VMEM = pltpu.VMEM
SMEM = pltpu.SMEM
HBM = pl.ANY
BF16 = jnp.bfloat16
FIELDS = 6


def params(mib):
    return pltpu.CompilerParams(vmem_limit_bytes=mib << 20)


def spec(space):
    return pl.BlockSpec(memory_space=space)


def granules(count, tile):
    per = ROWS_G * tile
    return (count + (per - 1)) // per


def pack_kernel(
    sizes, tile, owner_ref, count_ref, values_ref, head_ref, *rest
):
    outs, (scratch, cursor, sem, value_sem) = rest[: len(sizes)], rest[len(sizes) :]
    owners, tiles = scratch.shape[0], values_ref.shape[0]
    per_tile = tile // ROWS_G
    for o in range(owners):
        cursor[o] = 0

    def place(t, carry):
        o = owner_ref[t]
        at = cursor[o]
        cursor[o] = at + granules(count_ref[t], tile)
        scratch[o, pl.ds(at, per_tile)] = values_ref[t].reshape(per_tile, ROWS_G, tile)
        return carry

    lax.fori_loop(0, tiles, place, 0)
    head = head_ref.shape[0]
    copies = []
    start = 0
    for number, (out, size) in enumerate(zip(outs, sizes)):
        copies.append(
            pltpu.make_async_copy(
                scratch.at[:, pl.ds(start, size)],
                out.at[:, pl.ds(head if number == 0 else 0, size)],
                sem.at[number],
            )
        )
        start += size
    for o in range(owners):
        copies.append(
            pltpu.make_async_copy(
                head_ref, outs[0].at[o, pl.ds(0, head)], value_sem.at[o]
            )
        )
    for copy in copies:
        copy.start()
    for copy in copies:
        copy.wait()


def pack(owner, count, values, head, sizes, room):
    tiles, tile = values.shape[0], values.shape[1]
    owners = room[0]
    extra = [head.shape[0]] + [0] * (len(sizes) - 1)
    return pl.pallas_call(
        functools.partial(pack_kernel, sizes, tile),
        out_shape=[
            jax.ShapeDtypeStruct((owners, size + more, ROWS_G, tile), BF16)
            for size, more in zip(sizes, extra)
        ],
        in_specs=[spec(SMEM), spec(SMEM), spec(VMEM), spec(VMEM)],
        out_specs=[spec(HBM)] * len(sizes),
        scratch_shapes=[
            VMEM((owners, room[1], ROWS_G, tile), BF16),
            SMEM((owners,), jnp.int32),
            pltpu.SemaphoreType.DMA((len(sizes),)),
            pltpu.SemaphoreType.DMA((owners,)),
        ],
        compiler_params=params(24),
        cost_estimate=pl.CostEstimate(flops=0, bytes_accessed=8 << 20, transcendentals=0),
    )(owner, count, values, head)


def list_kernel(tile, row_blocks, window_ref, meta_ref, list_ref, total_ref, cursor):
    me, low, high = window_ref[0], window_ref[1], window_ref[2]
    senders, tiles = meta_ref.shape[0], meta_ref.shape[2]
    per = ROWS_G * tile
    length = high - low
    margin = tile // ROWS_G
    total_ref[1] = 0

    def sender(s, found):
        def clear(o, carry):
            cursor[o] = 0
            return carry

        lax.fori_loop(0, senders, clear, 0)

        def step(t, found):
            o = meta_ref[s, 0, t]
            count = meta_ref[s, 1, t] * tile + meta_ref[s, 2, t]
            at = cursor[o]
            end = at + granules(count, tile)
            cursor[o] = end
            total_ref[1] = jnp.maximum(total_ref[1], end)
            hit = (o == me) & (at < high) & (end > low)

            @pl.when(hit)
            def _():
                list_ref[0, found] = margin + s * length + at - low
                list_ref[1, found] = meta_ref[s, 3, t]
                list_ref[2, found] = s * row_blocks + meta_ref[s, 4, t]
                list_ref[3, found] = jnp.minimum(count, (high - at) * per)
                list_ref[4, found] = jnp.maximum(low - at, 0) * ROWS_G

            return found + hit.astype(jnp.int32)

        return lax.fori_loop(0, tiles, step, found)

    found = lax.fori_loop(0, senders, sender, 0)
    total_ref[0] = found
    list_ref[0, found] = margin
    list_ref[1, found] = 0
    list_ref[2, found] = 0
    list_ref[3, found] = 0
    list_ref[4, found] = 0


def list_tiles(window, meta, tile, row_blocks, room):
    return pl.pallas_call(
        functools.partial(list_kernel, tile, row_blocks),
        out_shape=[
            jax.ShapeDtypeStruct((FIELDS, room), jnp.int32),
            jax.ShapeDtypeStruct((2,), jnp.int32),
        ],
        in_specs=[spec(SMEM), spec(SMEM)],
        out_specs=[spec(SMEM), spec(SMEM)],
        scratch_shapes=[SMEM((meta.shape[0],), jnp.int32)],
        compiler_params=params(1),
        cost_estimate=pl.CostEstimate(flops=0, bytes_accessed=1 << 20, transcendentals=0),
    )(window, meta)


def hist_kernel(
    first, skip, list_ref, total_ref, got_ref, grads_ref, cuts_ref, *rest
):
    if first:
        hist_ref, got, sem = rest
    else:
        before_ref, hist_ref, got, sem = rest
    senders, length = got_ref.shape[0], got_ref.shape[1] - skip
    tile = got_ref.shape[3]
    per_tile = tile // ROWS_G
    levels = cuts_ref.shape[1]
    k_out = hist_ref.shape[2]
    copies = [
        pltpu.make_async_copy(
            got_ref.at[s, pl.ds(skip, length)],
            got.at[pl.ds(per_tile + s * length, length)],
            sem.at[s],
        )
        for s in range(senders)
    ]
    if not first:
        copies.append(pltpu.make_async_copy(before_ref, hist_ref, sem.at[senders]))
    for copy in copies:
        copy.start()
    if first:

        def clear(b, carry):
            hist_ref[b] = jnp.zeros(hist_ref.shape[1:], jnp.float32)
            return carry

        lax.fori_loop(0, hist_ref.shape[0], clear, 0)
    for copy in copies:
        copy.wait()
    row = lax.broadcasted_iota(jnp.int32, (tile, tile), 0).astype(jnp.float32).astype(BF16)
    lane = lax.broadcasted_iota(jnp.int32, (tile, tile), 1).astype(jnp.float32).astype(BF16)

    def as_bf16(x):
        return x.astype(jnp.float32).astype(BF16)

    def load(p):
        block = list_ref[1, p]
        count = list_ref[3, p]
        values = got[pl.ds(list_ref[0, p], per_tile)].reshape(tile, tile)
        whole = as_bf16(count // tile)
        part = as_bf16(count % tile)
        low = as_bf16(list_ref[4, p])
        live = ((row < whole) | ((row == whole) & (lane < part))) & (row >= low)
        values = jnp.where(live, values, jnp.full_like(values, -1000.0))
        return block, values

    one, zero = jnp.ones((tile, tile), BF16), jnp.zeros((tile, tile), BF16)

    def pair(i, carry):
        pa = 2 * i
        pb = 2 * i + 1
        block_a, va = load(pa)
        block_b, vb = load(pb)
        left = jnp.concatenate(
            [grads_ref[0, list_ref[2, pa]], grads_ref[1, list_ref[2, pb]]], axis=1
        )
        for c in range(0, levels, 2):
            columns = []
            for d in (c, c + 1):
                cut_a = jnp.tile(cuts_ref[block_a, d], (per_tile, 1))
                cut_b = jnp.tile(cuts_ref[block_b, d], (per_tile, 1))
                columns.append(
                    jnp.concatenate(
                        [jnp.where(va > cut_a, one, zero), jnp.where(vb > cut_b, one, zero)],
                        axis=0,
                    )
                )
            sums = jnp.dot(
                left, jnp.concatenate(columns, axis=1), preferred_element_type=jnp.float32
            )
            hist_ref[block_a, c] += sums[:k_out, :tile]
            hist_ref[block_a, c + 1] += sums[:k_out, tile:]
            hist_ref[block_b, c] += sums[k_out:, :tile]
            hist_ref[block_b, c + 1] += sums[k_out:, tile:]
        return carry

    lax.fori_loop(0, (total_ref[0] + 1) // 2, pair, 0)


def add_tiles(hist, listed, total, got, grads, cuts, skip, k_out):
    first = hist is None
    senders, length, tile = got.shape[0], got.shape[1] - skip, got.shape[3]
    blocks, levels = cuts.shape[0], cuts.shape[1]
    args = [listed, total, got, grads, cuts] + ([] if first else [hist])
    return pl.pallas_call(
        functools.partial(hist_kernel, first, skip),
        out_shape=jax.ShapeDtypeStruct((blocks, levels, k_out, tile), jnp.float32),
        in_specs=[spec(SMEM), spec(SMEM), spec(HBM), spec(VMEM), spec(VMEM)]
        + ([] if first else [spec(HBM)]),
        out_specs=spec(VMEM),
        scratch_shapes=[
            VMEM((senders * length + 2 * (tile // ROWS_G), ROWS_G, tile), BF16),
            pltpu.SemaphoreType.DMA((senders + 1,)),
        ],
        compiler_params=params(40),
        cost_estimate=pl.CostEstimate(
            flops=10**10, bytes_accessed=24 << 20, transcendentals=0
        ),
    )(*args)


def close_kernel(me_ref, hist_ref, out_ref):
    slots, per = out_ref.shape[0], out_ref.shape[1]
    levels, k_out, tile = hist_ref.shape[1:]
    me = me_ref[0]

    def step(i, carry):
        slot = i // per
        at = i % per
        block = (slot ^ me) * per + at
        above = hist_ref[block]
        below = jnp.concatenate(
            [above[1:], jnp.zeros((1, k_out, tile), jnp.float32)], axis=0
        )
        out_ref[slot, at] = (above - below).reshape(levels * k_out, tile).astype(BF16)
        return carry

    lax.fori_loop(0, slots * per, step, 0)


def close(me, hist, slots):
    blocks, levels, k_out, tile = hist.shape
    return pl.pallas_call(
        close_kernel,
        out_shape=jax.ShapeDtypeStruct((slots, blocks // slots, levels * k_out, tile), BF16),
        in_specs=[spec(SMEM), spec(VMEM)],
        out_specs=spec(VMEM),
        compiler_params=params(24),
    )(me, hist)


def finish_kernel(k_out, *refs):
    parts, out_ref, scratch = refs[:-2], refs[-2], refs[-1]
    blocks, rows, tile = parts[0].shape
    levels = rows // k_out
    for b in range(blocks):
        total = parts[0][b].astype(jnp.float32)
        for part in parts[1:]:
            total = total + part[b].astype(jnp.float32)
        scratch[...] = total
        for k in range(k_out):
            out_ref[k, :, b * tile : (b + 1) * tile] = scratch[pl.ds(k, levels, stride=k_out), :]


def finish(parts, k_out):
    blocks, rows, tile = parts[0].shape
    return pl.pallas_call(
        functools.partial(finish_kernel, k_out),
        out_shape=jax.ShapeDtypeStruct((k_out, rows // k_out, blocks * tile), jnp.float32),
        in_specs=[spec(VMEM)] * len(parts),
        out_specs=spec(VMEM),
        scratch_shapes=[VMEM((rows, tile), jnp.float32)],
        compiler_params=params(16),
    )(*parts)


def reduce_rows(slots, k_out, axis):
    n = slots.shape[0]
    parts = {p: [slots[p]] for p in range(n)}
    bit = 1
    while bit < n:
        for p in sorted((p for p in parts if p & bit), reverse=True):
            have = parts.pop(p)
            if len(have) > 1:
                value = functools.reduce(jnp.add, [x.astype(jnp.float32) for x in have])
                value = value.astype(BF16)
            else:
                value = have[0]
            moved = lax.ppermute(value, axis, [(i, i ^ bit) for i in range(n)])
            parts[p ^ bit].append(moved)
        bit *= 2
    return finish(parts[0], k_out)


def shards(tile_values, tile_row, tile_block, tile_count, tile_owner, cut_index, gradients):
    owners = lax.axis_size("feat")
    row_groups = lax.axis_size("rows")
    tile_dev, tile = tile_values.shape[:2]
    levels = cut_index.shape[0] + 1
    k_out, rows_dev = gradients.shape
    row_blocks = rows_dev // tile
    fb_dev = cut_index.shape[1] // tile
    per_tile = tile // ROWS_G
    capacity = max(2, 2 * tile_dev // owners) * per_tile
    static = [capacity // 6] * 4
    turn = capacity // 12
    left = capacity - sum(static)

    owner = tile_owner[:, 0]
    meta = jnp.stack(
        [owner, tile_count // tile, tile_count % tile, tile_block, tile_row], axis=0
    )
    meta = jnp.pad(meta, ((0, ROWS_G - meta.shape[0]), (0, tile - tile_dev))).astype(BF16)
    rows_first = jnp.transpose(gradients.reshape(k_out, row_blocks, tile), (1, 0, 2))
    rows_first = rows_first.reshape(row_blocks * k_out // ROWS_G, ROWS_G, tile)
    head = jnp.concatenate([rows_first, meta[None]], axis=0)
    skip = head.shape[0]

    sent = pack(owner, tile_count, tile_values, head, static + [left], (owners, capacity))

    n = 2 * cut_index + (1 - 10 * (levels - 1))
    n = jnp.where(jnp.abs(n) > 256, n - 1, n)
    cuts = (n.astype(jnp.float32) / 128.0).astype(BF16)
    cuts = jnp.concatenate([jnp.full((1, fb_dev * tile), -500.0, BF16), cuts], axis=0)
    cuts = jnp.transpose(cuts.reshape(levels, fb_dev, tile), (1, 0, 2))
    cuts = jnp.broadcast_to(cuts[:, :, None, :], (fb_dev, levels, ROWS_G, tile))

    def exchange(x):
        return lax.all_to_all(x, "feat", split_axis=0, concat_axis=0, tiled=True)

    got = [exchange(x) for x in sent[:-1]]
    known = got[0][:, skip - 1, :5, :tile_dev].astype(jnp.int32)
    grads = got[0][:, : skip - 1].reshape(owners * row_blocks, k_out, tile)
    nothing = jnp.zeros_like(grads)
    grads = jnp.stack(
        [jnp.concatenate([grads, nothing], axis=1), jnp.concatenate([nothing, grads], axis=1)],
        axis=0,
    )
    me = lax.axis_index("feat")
    room = -(-(owners * capacity // per_tile + 2) // 128) * 128

    def listed(low, size):
        window = jnp.stack([me, low, low + size]).astype(jnp.int32)
        return list_tiles(window, known, tile, row_blocks, room)

    hist = None
    low = 0
    for number, size in enumerate(static):
        entries, total = listed(low, size)
        hist = add_tiles(
            hist, entries, total, got[number], grads, cuts, skip if number == 0 else 0, k_out
        )
        low += size
    turns = (total[1] - low + turn - 1) // turn

    def more(carry):
        return carry[0] < turns

    def step(carry):
        r, hist = carry
        piece = lax.dynamic_slice_in_dim(sent[-1], r * turn, turn, axis=1)
        entries, total = listed(low + r * turn, turn)
        hist = add_tiles(hist, entries, total, exchange(piece), grads, cuts, 0, k_out)
        return r + 1, hist

    _, hist = lax.while_loop(more, step, (jnp.int32(0), hist))
    slots = close(lax.axis_index("rows").astype(jnp.int32)[None], hist, row_groups)
    return reduce_rows(slots, k_out, "rows")


def solution(mesh):
    placed = (
        P(("grp", "feat", "rows"), None, None),
        P(("grp", "feat", "rows")),
        P(("grp", "feat", "rows")),
        P(("grp", "feat", "rows")),
        P(("grp", "feat", "rows"), None),
        P(None, ("grp", "feat")),
        P(None, ("grp", "feat", "rows")),
    )
    return jax.shard_map(
        shards,
        mesh=mesh,
        in_specs=placed,
        out_specs=P(None, None, ("grp", "feat", "rows")),
        check_vma=False,
    )
```

time: 576 us -> 242 us (0.42)
  other arithmetic: 181 us -> 4.1 us
  Pallas kernels: 0 us -> 120 us
  blocking collectives: 141 us -> 31.8 us
  matrix products: 91.7 us -> 0 us
  local copies, waits for them, and re-layouts: 93.1 us -> 26 us
  between operations: 13.5 us -> 0.92 us
  waiting for transfers between devices: 36.8 us -> 46.3 us
    all_gather x1 -> x0, blocking collectives: 141 us -> none  [shards(): lax.all_gather(gradients, 'feat', axis=1, tiled=True)]
    pallas_call x0 -> x11, Pallas kernels: none -> 120 us  [the longest x4 55 us: list_tiles(): pl.pallas_call(functools.partial(list_kernel, tile, row_blocks), out_shap...]
    dot_general x24 -> x0, matrix products: 91.7 us -> none  [step(): jnp.einsum('wki,wibj->kbwj', grad_rows, onehot, preferred_element_type=jn...]
    scatter-add x24 -> x0, other arithmetic: 91.2 us -> none  [step(): carry = carry.at[:, :, info[:, 1], :].add(sums)]
    add x49 -> x0, other arithmetic: 64.9 us -> none  [the longest x24 62.3 us: step(): level = level + (vfloat > cut_rows[c][:, None, :]).astype(jnp.int32)]
    gather x29 -> x0, local copies, waits for them, and re-layouts: 55.7 us -> none  [the longest x24 40.5 us: step(): cut_rows = jnp.take(cuts, info[:, 1], axis=1)]
    reduce_scatter x1 -> x0, waiting for transfers between devices: 36.7 us -> none  [shards(): lax.psum_scatter(hist.reshape(k_out, levels, fb_dev * tile).astype(jnp.bf...]
    all_to_all x0 -> x1, blocking collectives: none -> 31.8 us  [exchange(): return lax.all_to_all(x, 'feat', split_axis=0, concat_axis=0, tiled=True)]
  transfers between devices with their start and end apart: 3 -> 6, of which waited for: 1 -> 4; matrix products, arithmetic and copies ran while one was open for 4% -> 2% of each run, Pallas kernels for 0% -> 41%
where the time goes in v1:
time: 242 us
  Pallas kernels  120 us (50%)
  waiting for transfers between devices  46.3 us (19%)
  blocking collectives  31.8 us (13%)
  local copies, waits for them, and re-layouts  26 us (11%)
  starting transfers between devices  13.5 us (6%)
  other arithmetic  4.1 us (2%)
    pallas_call x4, Pallas kernels, list_tiles(): pl.pallas_call(functools.partial(list_kernel, tile, row_blocks), out_shap...  55 us
    pallas_call x4, Pallas kernels, add_tiles(): pl.pallas_call(functools.partial(hist_kernel, first, skip), out_shape=jax...  54.9 us
    all_to_all x1, blocking collectives, exchange(): return lax.all_to_all(x, 'feat', split_axis=0, concat_axis=0, tiled=True)  31.8 us
    all_to_all x3, waiting for transfers between devices, exchange(): return lax.all_to_all(x, 'feat', split_axis=0, concat_axis=0, tiled=True)  25.3 us
    unnamed x26, local copies, waits for them, and re-layouts  22.2 us
    ppermute x3, waiting for transfers between devices, reduce_rows(): moved = lax.ppermute(value, axis, [(i, i ^ bit) for i in range(n)])  21.1 us
    all_to_all x3, starting transfers between devices, exchange(): return lax.all_to_all(x, 'feat', split_axis=0, concat_axis=0, tiled=True)  12.5 us
  transfers between devices with their start and end apart: 6, of which 4 were waited for; matrix products, arithmetic and copies ran while one was open for 2% of the time, Pallas kernels for 41%

profile of v1, /device:TPU:0, one launch (start us, length us, event | category | flops | bytes accessed | tf_op | source)
XLA Modules:
  0.0 242.3 jit_solution(3448809590899526554)
XLA Ops:
  0.0 0.7 convert_bitcast_fusion.1
  0.7 0.7 convert_bitcast_fusion.3
  1.3 0.7 fusion.5
  2.0 0.7 pad_maximum_fusion.1.head_ref
  2.8 0.0 copy-start.4
  2.8 1.9 copy-done.4
  4.7 0.0 copy-start.5
  4.7 0.7 copy-done.5
  5.3 0.0 copy-start.6
  5.3 0.7 copy-done.6
  6.0 0.0 copy-start.12
  6.0 4.2 %shard_map.73 = (bf16[4,69,16,128]{3,2,1,0:T(8,128)(2,1)}, bf16[4,64,16,128]{3,2,1,0:T(8,128)(2,1)S(1)}, bf16[4,64,16,128]{3,2,1,0:T(8,128)(2,1)}, bf16[4,64,16,...) custom-call(s32[96]{0:T(128)S(1)} %bitcast.56, s32[96]{0:T(128)S(1)} %copy-done.5, bf16[96,128,128]{2,1,0:T(8,128)(2,1)S(1)} %copy-done.4, ...), custom_call_target="tpu_custom_call" | custom-call | bytes 8388608 | tf_op jit(solution)/shard_map/pallas_call | solution.py:76
  10.2 31.8 %all_to_all.27.got_ref = bf16[4,64,16,128]{3,2,1,0:T(8,128)(2,1)S(1)} all-to-all(bf16[4,64,16,128]{3,2,1,0:T(8,128)(2,1)S(1)} %get-tuple-element.128), channel_id=1, replica_groups=mesh['grp'=2,'feat'=4,'rows'=4] {'feat'}, dimensions={0} | all-to-all | bytes 2097152 | tf_op jit(solution)/shard_map/all_to_all | solution.py:367
  42.0 3.5 %all-to-all-start.1 = ((bf16[4,69,16,128]{3,2,1,0:T(8,128)(2,1)}), bf16[4,69,16,128]{3,2,1,0:T(8,128)(2,1)S(1)}, u32[]{:S(2)}, u32[]{:S(2)}) async-start(bf16[4,69,16,128]{3,2,1,0:T(8,128)(2,1)} %get-tuple-element.119), calls=%async_computation.1 | async-start | bytes 2260992 | tf_op jit(solution)/shard_map/all_to_all | solution.py:367
  45.6 0.0 copy-done.12
  45.6 0.3 multiply_convert_fusion
  45.8 0.1 pad_bitcast_fusion
  46.0 0.1 copy.10
  46.0 0.8 copy.8
  46.9 25.3 %all-to-all-done.1.got_ref = bf16[4,69,16,128]{3,2,1,0:T(8,128)(2,1)S(1)} async-done(((bf16[4,69,16,128]{3,2,1,0:T(8,128)(2,1)}), bf16[4,69,16,128]{3,2,1,0:T(8,128)(2,1)S(1)}, u32[]{:S(2)}, u32[]{:S(2)}) %all-to-all-start.1) | async-done | bytes 1130528 | tf_op jit(solution)/shard_map/all_to_all | solution.py:367
  72.1 3.5 %all-to-all-start.3 = ((bf16[4,64,16,128]{3,2,1,0:T(8,128)(2,1)}), bf16[4,64,16,128]{3,2,1,0:T(8,128)(2,1)S(1)}, u32[]{:S(2)}, u32[]{:S(2)}) async-start(bf16[4,64,16,128]{3,2,1,0:T(8,128)(2,1)} %get-tuple-element.125), calls=%async_computation.3 | async-start | bytes 2097152 | tf_op jit(solution)/shard_map/all_to_all | solution.py:367
  75.7 0.1 pad_add_fusion.1
  75.7 0.1 pad_add_fusion.3
  75.8 13.8 %shard_map.74 = (s32[6,256]{1,0:T(8,128)S(1)}, s32[2]{0:T(128)S(1)}) custom-call(s32[3]{0:T(128)S(1)} %get-tuple-element.186.window_ref, s32[4,5,96]{2,1,0:T(8,128)S(1)} %fusion.3.meta_ref), custom_call_target="tpu_custom_call" | custom-call | bytes 1048576 | tf_op jit(solution)/shard_map/pallas_call | solution.py:141
  89.6 0.6 slice.23
  90.8 13.8 %shard_map.77 = (s32[6,256]{1,0:T(8,128)S(1)}, s32[2]{0:T(128)S(1)}) custom-call(s32[3]{0:T(128)S(1)} %get-tuple-element.189.window_ref, s32[4,5,96]{2,1,0:T(8,128)S(1)} %fusion.3.meta_ref), custom_call_target="tpu_custom_call" | custom-call | bytes 1048576 | tf_op jit(solution)/shard_map/pallas_call | solution.py:141
  104.6 13.8 %shard_map.76 = (s32[6,256]{1,0:T(8,128)S(1)}, s32[2]{0:T(128)S(1)}) custom-call(s32[3]{0:T(128)S(1)} %get-tuple-element.188.window_ref, s32[4,5,96]{2,1,0:T(8,128)S(1)} %fusion.3.meta_ref), custom_call_target="tpu_custom_call" | custom-call | bytes 1048576 | tf_op jit(solution)/shard_map/pallas_call | solution.py:141
  118.4 13.8 %shard_map.75 = (s32[6,256]{1,0:T(8,128)S(1)}, s32[2]{0:T(128)S(1)}) custom-call(s32[3]{0:T(128)S(1)} %get-tuple-element.187.window_ref, s32[4,5,96]{2,1,0:T(8,128)S(1)} %fusion.3.meta_ref), custom_call_target="tpu_custom_call" | custom-call | bytes 1048576 | tf_op jit(solution)/shard_map/pallas_call | solution.py:141
  132.2 0.7 pad_maximum_fusion.grads_ref
  133.0 2.0 broadcast_in_dim.16.cuts_ref
  135.0 13.3 %shard_map.78.rest_0_ = f32[48,32,8,128]{3,2,1,0:T(8,128)S(1)} custom-call(s32[6,256]{1,0:T(8,128)S(1)} %get-tuple-element.129.list_ref, s32[2]{0:T(128)S(1)} %get-tuple-element.130.total_ref, bf16[4,69,16,128]{3,2,1,0:T(8,128)(2,1)S(1)} %all-to-all-done.1.got_ref, bf16[2,32,16,128]{3,2,1,0:T(8,128)(2,1)} %pad_maximum_fusion.grads_ref, ...), custom_call_target="tpu_custom_call" | custom-call | flops 10000000000 | bytes 25165824 | tf_op jit(solution)/shard_map/pallas_call | solution.py:243
  148.3 0.0 copy-start.1
  148.3 2.6 %copy-done.1 = bf16[48,32,16,128]{3,2,1,0:T(8,128)(2,1)} copy-done((bf16[48,32,16,128]{3,2,1,0:T(8,128)(2,1)}, bf16[48,32,16,128]{3,2,1,0:T(8,128)(2,1)S(1)}, u32[]{:S(2)}) %copy-start.1) | copy-done | bytes 6291480
  151.0 0.0 copy-start.7
  151.0 2.6 %copy-done.7 = f32[48,32,8,128]{3,2,1,0:T(8,128)} copy-done((f32[48,32,8,128]{3,2,1,0:T(8,128)}, f32[48,32,8,128]{3,2,1,0:T(8,128)S(1)}, u32[]{:S(2)}) %copy-start.7) | copy-done | bytes 6291480
  153.6 0.0 all-to-all-done.3.got_ref
  153.6 5.5 %all-to-all-start.2 = ((bf16[4,64,16,128]{3,2,1,0:T(8,128)(2,1)}), bf16[4,64,16,128]{3,2,1,0:T(8,128)(2,1)S(1)}, u32[]{:S(2)}, u32[]{:S(2)}) async-start(bf16[4,64,16,128]{3,2,1,0:T(8,128)(2,1)} %get-tuple-element.122), calls=%async_computation.2 | async-start | bytes 2097152 | tf_op jit(solution)/shard_map/all_to_all | solution.py:367
  159.1 0.0 copy-start.2
  159.1 2.8 %copy-done.2 = bf16[48,32,16,128]{3,2,1,0:T(8,128)(2,1)S(1)} copy-done((bf16[48,32,16,128]{3,2,1,0:T(8,128)(2,1)S(1)}, bf16[48,32,16,128]{3,2,1,0:T(8,128)(2,1)}, u32[]{:S(2)}) %copy-start.2) | copy-done | bytes 6291480
  161.9 15.2 %shard_map.79.rest_0_ = f32[48,32,8,128]{3,2,1,0:T(8,128)S(1)} custom-call(s32[6,256]{1,0:T(8,128)S(1)} %get-tuple-element.126.list_ref, s32[2]{0:T(128)S(1)} %get-tuple-element.127.total_ref, bf16[4,64,16,128]{3,2,1,0:T(8,128)(2,1)S(1)} %all_to_all.27.got_ref, bf16[2,32,16,128]{3,2,1,0:T(8,128)(2,1)} %pad_maximum_fusion.grads_ref, ...), custom_call_target="tpu_custom_call" | custom-call | flops 10000000000 | bytes 25165824 | tf_op jit(solution)/shard_map/pallas_call | solution.py:243
  177.1 0.0 copy-start.10
  177.1 2.6 %copy-done.10 = f32[48,32,8,128]{3,2,1,0:T(8,128)} copy-done((f32[48,32,8,128]{3,2,1,0:T(8,128)}, f32[48,32,8,128]{3,2,1,0:T(8,128)S(1)}, u32[]{:S(2)}) %copy-start.10) | copy-done | bytes 6291480
  179.8 16.4 %shard_map.80.rest_0_ = f32[48,32,8,128]{3,2,1,0:T(8,128)S(1)} custom-call(s32[6,256]{1,0:T(8,128)S(1)} %get-tuple-element.123.list_ref, s32[2]{0:T(128)S(1)} %get-tuple-element.124.total_ref, bf16[4,64,16,128]{3,2,1,0:T(8,128)(2,1)S(1)} %all-to-all-done.3.got_ref, bf16[2,32,16,128]{3,2,1,0:T(8,128)(2,1)} %pad_maximum_fusion.grads_ref, ...), custom_call_target="tpu_custom_call" | custom-call | flops 10000000000 | bytes 25165824 | tf_op jit(solution)/shard_map/pallas_call | solution.py:243
  196.2 0.0 copy-start.8
  196.2 2.6 %copy-done.8 = f32[48,32,8,128]{3,2,1,0:T(8,128)} copy-done((f32[48,32,8,128]{3,2,1,0:T(8,128)}, f32[48,32,8,128]{3,2,1,0:T(8,128)S(1)}, u32[]{:S(2)}) %copy-start.8) | copy-done | bytes 6291480
  198.8 0.0 all-to-all-done.2.got_ref
  198.8 0.0 copy-start.3
  198.8 2.8 %copy-done.3 = bf16[48,32,16,128]{3,2,1,0:T(8,128)(2,1)S(1)} copy-done((bf16[48,32,16,128]{3,2,1,0:T(8,128)(2,1)S(1)}, bf16[48,32,16,128]{3,2,1,0:T(8,128)(2,1)}, u32[]{:S(2)}) %copy-start.3) | copy-done | bytes 6291480
  201.6 0.0 copy-start.9
  201.6 2.8 %copy-done.9 = f32[48,32,8,128]{3,2,1,0:T(8,128)S(1)} copy-done((f32[48,32,8,128]{3,2,1,0:T(8,128)S(1)}, f32[48,32,8,128]{3,2,1,0:T(8,128)}, u32[]{:S(2)}) %copy-start.9) | copy-done | bytes 6291480
  204.4 0.0 copy-start.11
  204.4 9.9 %shard_map.81 = f32[48,32,8,128]{3,2,1,0:T(8,128)} custom-call(s32[6,256]{1,0:T(8,128)S(1)} %get-tuple-element.120.list_ref, s32[2]{0:T(128)S(1)} %get-tuple-element.121.total_ref, bf16[4,64,16,128]{3,2,1,0:T(8,128)(2,1)S(1)} %all-to-all-done.2.got_ref, bf16[2,32,16,128]{3,2,1,0:T(8,128)(2,1)} %pad_maximum_fusion.grads_ref, ...), custom_call_target="tpu_custom_call" | custom-call | flops 10000000000 | bytes 25165824 | tf_op jit(solution)/shard_map/pallas_call | solution.py:243
  214.3 0.0 copy-done.11
  214.4 3.8 %shard_map.82 = bf16[4,12,256,128]{3,2,1,0:T(8,128)(2,1)S(1)} custom-call(s32[1]{0:T(128)} %bitcast.me_ref, f32[48,32,8,128]{3,2,1,0:T(8,128)} %get-tuple-element.132.hist_ref), custom_call_target="tpu_custom_call" | custom-call | tf_op jit(solution)/shard_map/pallas_call | solution.py:281
  218.2 0.2 slice_bitcast_fusion
  218.4 0.1 collective-permute-start.1
  218.5 0.5 collective-permute-start
  218.9 1.8 collective-permute-done.1
  220.7 0.2 fusion.2
  221.0 0.3 collective-permute-start.2
  221.3 0.6 collective-permute-done.refs_1_
  221.8 18.7 %collective-permute-done.2.refs_2_ = bf16[12,256,128]{2,1,0:T(8,128)(2,1)S(1)} collective-permute-done((bf16[12,256,128]{2,1,0:T(8,128)(2,1)S(1)}, bf16[12,256,128]{2,1,0:T(8,128)(2,1)S(1)}, u32[]{:S(2)}, u32[]{:S(2)}) %collective-permute-start.2) | collective-permute-done | bytes 786464 | tf_op jit(solution)/shard_map/ppermute | solution.py:327
  240.6 1.7 shard_map.83
  (6 shorter events, 0.1 us)
Async XLA Ops:
  2.8 1.9 copy-start.4
  4.7 0.7 copy-start.5
  5.3 0.7 copy-start.6
  6.0 39.6 %copy-start.12 = (s32[31,6144]{1,0:T(8,128)S(1)}, s32[31,6144]{1,0:T(8,128)}, u32[]{:S(2)}) copy-start(s32[31,6144]{1,0:T(8,128)} %param.14) | copy-start | bytes 2285572
  42.0 30.1 %all-to-all-start.1 = ((bf16[4,69,16,128]{3,2,1,0:T(8,128)(2,1)}), bf16[4,69,16,128]{3,2,1,0:T(8,128)(2,1)S(1)}, u32[]{:S(2)}, u32[]{:S(2)}) async-start(bf16[4,69,16,128]{3,2,1,0:T(8,128)(2,1)} %get-tuple-element.119), calls=%async_computation.1 | async-start | bytes 2260992 | tf_op jit(solution)/shard_map/all_to_all | solution.py:367
  72.1 81.5 %all-to-all-start.3 = ((bf16[4,64,16,128]{3,2,1,0:T(8,128)(2,1)}), bf16[4,64,16,128]{3,2,1,0:T(8,128)(2,1)S(1)}, u32[]{:S(2)}, u32[]{:S(2)}) async-start(bf16[4,64,16,128]{3,2,1,0:T(8,128)(2,1)} %get-tuple-element.125), calls=%async_computation.3 | async-start | bytes 2097152 | tf_op jit(solution)/shard_map/all_to_all | solution.py:367
  148.3 2.6 %copy-start.1 = (bf16[48,32,16,128]{3,2,1,0:T(8,128)(2,1)}, bf16[48,32,16,128]{3,2,1,0:T(8,128)(2,1)S(1)}, u32[]{:S(2)}) copy-start(bf16[48,32,16,128]{3,2,1,0:T(8,128)(2,1)S(1)} %broadcast_in_dim.16.cuts_ref) | copy-start | bytes 18874372
  151.0 2.6 %copy-start.7 = (f32[48,32,8,128]{3,2,1,0:T(8,128)}, f32[48,32,8,128]{3,2,1,0:T(8,128)S(1)}, u32[]{:S(2)}) copy-start(f32[48,32,8,128]{3,2,1,0:T(8,128)S(1)} %shard_map.78.rest_0_) | copy-start | bytes 18874372
  153.6 45.2 %all-to-all-start.2 = ((bf16[4,64,16,128]{3,2,1,0:T(8,128)(2,1)}), bf16[4,64,16,128]{3,2,1,0:T(8,128)(2,1)S(1)}, u32[]{:S(2)}, u32[]{:S(2)}) async-start(bf16[4,64,16,128]{3,2,1,0:T(8,128)(2,1)} %get-tuple-element.122), calls=%async_computation.2 | async-start | bytes 2097152 | tf_op jit(solution)/shard_map/all_to_all | solution.py:367
  159.1 2.8 %copy-start.2 = (bf16[48,32,16,128]{3,2,1,0:T(8,128)(2,1)S(1)}, bf16[48,32,16,128]{3,2,1,0:T(8,128)(2,1)}, u32[]{:S(2)}) copy-start(bf16[48,32,16,128]{3,2,1,0:T(8,128)(2,1)} %copy-done.1) | copy-start | bytes 18874372
  177.1 2.6 %copy-start.10 = (f32[48,32,8,128]{3,2,1,0:T(8,128)}, f32[48,32,8,128]{3,2,1,0:T(8,128)S(1)}, u32[]{:S(2)}) copy-start(f32[48,32,8,128]{3,2,1,0:T(8,128)S(1)} %shard_map.79.rest_0_) | copy-start | bytes 18874372
  196.2 2.6 %copy-start.8 = (f32[48,32,8,128]{3,2,1,0:T(8,128)}, f32[48,32,8,128]{3,2,1,0:T(8,128)S(1)}, u32[]{:S(2)}) copy-start(f32[48,32,8,128]{3,2,1,0:T(8,128)S(1)} %shard_map.80.rest_0_) | copy-start | bytes 18874372
  198.8 2.8 %copy-start.3 = (bf16[48,32,16,128]{3,2,1,0:T(8,128)(2,1)S(1)}, bf16[48,32,16,128]{3,2,1,0:T(8,128)(2,1)}, u32[]{:S(2)}) copy-start(bf16[48,32,16,128]{3,2,1,0:T(8,128)(2,1)} %copy-done.1) | copy-start | bytes 18874372
  201.6 2.8 %copy-start.9 = (f32[48,32,8,128]{3,2,1,0:T(8,128)S(1)}, f32[48,32,8,128]{3,2,1,0:T(8,128)}, u32[]{:S(2)}) copy-start(f32[48,32,8,128]{3,2,1,0:T(8,128)} %copy-done.8) | copy-start | bytes 18874372
  204.4 9.9 %copy-start.11 = (bf16[48,32,128]{2,1,0:T(8,128)(2,1)S(1)}, bf16[48,32,128]{2,1,0:T(8,128)(2,1)}, u32[]{:S(2)}) copy-start(bf16[48,32,128]{2,1,0:T(8,128)(2,1)} %copy.8) | copy-start | bytes 1179652
  218.4 2.4 collective-permute-start.1
  218.5 3.4 %collective-permute-start = (bf16[12,256,128]{2,1,0:T(8,128)(2,1)S(1)}, bf16[12,256,128]{2,1,0:T(8,128)(2,1)S(1)}, u32[]{:S(2)}, u32[]{:S(2)}) collective-permute-start(bf16[12,256,128]{2,1,0:T(8,128)(2,1)S(1)} %get-tuple-element.180), channel_id=1, source_target_pairs={{0,1},{1,0},{2,3},{3,2},{4,5},{5,4},{6,7},{7,6},{8,9},{9,8},{10,11... | collective-permute-start | bytes 2359304 | tf_op jit(solution)/shard_map/ppermute | solution.py:327
  221.0 19.6 %collective-permute-start.2 = (bf16[12,256,128]{2,1,0:T(8,128)(2,1)S(1)}, bf16[12,256,128]{2,1,0:T(8,128)(2,1)S(1)}, u32[]{:S(2)}, u32[]{:S(2)}) collective-permute-start(bf16[12,256,128]{2,1,0:T(8,128)(2,1)S(1)} %fusion.2), channel_id=1, source_target_pairs={{0,2},{1,3},{2,0},{3,1},{4,6},{5,7},{6,4},{7,5},{8,10},{9,11},{10,... | collective-permute-start | bytes 2359304 | tf_op jit(solution)/shard_map/ppermute | solution.py:327

commit v2 on v0

v2 whole, which is shorter than its diff:
```python
import functools

import jax
import jax.numpy as jnp
from jax import lax
from jax.experimental import pallas as pl
from jax.experimental.pallas import tpu as pltpu
from jax.sharding import PartitionSpec as P

ROWS_G = 16
VMEM = pltpu.VMEM
SMEM = pltpu.SMEM
ANY = pl.ANY
BF16 = jnp.bfloat16
INFO = 6
PACK_MIB = 56


def params(mib):
    return pltpu.CompilerParams(vmem_limit_bytes=mib << 20)


def spec(space):
    return pl.BlockSpec(memory_space=space)


def cost(flops, mib):
    return pl.CostEstimate(flops=flops, bytes_accessed=mib << 20, transcendentals=0)


def log2(n):
    assert n & (n - 1) == 0
    return n.bit_length() - 1


def shifted(x, n):
    return lax.shift_right_logical(x, jnp.int32(log2(n)))


def wrapped(x, n):
    return jnp.where(x < 0, x + n, x)


def as_bf16(x):
    return x.astype(jnp.float32).astype(BF16)


def pack_kernel(
    sizes, unit, me_ref, owner_ref, count_ref, block_ref, row_ref, grads_hbm, values_hbm, *rest
):
    number = len(sizes)
    slots, lanes = rest[-3].shape[0], rest[-3].shape[2]
    outs, infos = rest[: number * slots], rest[number * slots : (number + 1) * slots]
    scratch, values, heads, grads, info, cursor, sem = rest[(number + 1) * slots :]
    tiles, tile = values.shape[0], values.shape[1]
    per_tile = tile // ROWS_G
    k_out, row_blocks = grads.shape[0], grads.shape[1] // tile
    parts = 4 if tiles % 4 == 0 else 1
    span = tiles // parts
    loads = [
        pltpu.make_async_copy(
            values_hbm.at[pl.ds(i * span, span)], values.at[pl.ds(i * span, span)], sem.at[i]
        )
        for i in range(parts)
    ] + [pltpu.make_async_copy(grads_hbm, grads, sem.at[parts])]
    for load in loads:
        load.start()
    me = me_ref[0]
    units = sum(sizes) // unit
    for d in range(slots):
        cursor[0, d] = 0
        cursor[1, d] = 0
        for u in range(units + 1):
            info[d, 4, u] = lanes
            info[d, 5, u] = lanes
    for i in range(parts):
        loads[i].wait()

        def place(t, carry):
            d = wrapped(owner_ref[t] - me, slots)
            at, n = cursor[0, d], cursor[1, d]
            count = count_ref[t]
            end = at + shifted(count + (ROWS_G * tile - 1), ROWS_G * tile)
            cursor[0, d] = end
            cursor[1, d] = n + 1
            scratch[d, pl.ds(at, per_tile)] = values[t].reshape(per_tile, ROWS_G, tile)
            info[d, 0, n] = at
            info[d, 1, n] = count
            info[d, 2, n] = block_ref[t]
            info[d, 3, n] = row_ref[t]
            u = shifted(end - 1, unit)
            info[d, 4, jnp.where(u * unit >= at, u, lanes - 3)] = n
            u = shifted(end, unit)
            info[d, 5, jnp.where(u * unit > at, u, lanes - 3)] = n + 1
            return carry

        lax.fori_loop(i * span, (i + 1) * span, place, 0)
    most = cursor[0, 0]
    for d in range(1, slots):
        most = jnp.maximum(most, cursor[0, d])
    for d in range(slots):
        info[d, 4, lanes - 2] = cursor[1, d]
        info[d, 4, lanes - 1] = most
    loads[parts].wait()
    lines = [grads[:, b * tile : (b + 1) * tile] for b in range(row_blocks)]
    heads[...] = jnp.concatenate(lines, axis=0).reshape(heads.shape)
    copies = []
    start, at = 0, parts + 1
    for c, size in enumerate(sizes):
        skip = heads.shape[0] if c == 0 else 0
        for d in range(slots):
            out = outs[c * slots + d]
            pairs = [(scratch.at[d, pl.ds(start, size)], out.at[pl.ds(skip, size)])]
            if skip:
                pairs += [(heads, out.at[pl.ds(0, skip)]), (info.at[d], infos[d])]
            for source, target in pairs:
                copies.append(pltpu.make_async_copy(source, target, sem.at[at]))
                at += 1
        start += size
    for copy in copies:
        copy.start()
    for copy in copies:
        copy.wait()


def pack(me, owner, count, block, row, grads, values, sizes, unit, slots):
    tiles, tile = values.shape[0], values.shape[1]
    room = sum(sizes)
    lanes = 128
    assert max(2, 2 * tiles // slots) < lanes - 3 and room // unit < lanes - 3
    head = grads.size // (ROWS_G * tile)
    shapes = [
        jax.ShapeDtypeStruct((size + (head if number == 0 else 0), ROWS_G, tile), BF16)
        for number, size in enumerate(sizes)
        for _ in range(slots)
    ] + [jax.ShapeDtypeStruct((INFO, lanes), jnp.int32)] * slots
    outs = pl.pallas_call(
        functools.partial(pack_kernel, sizes, unit),
        out_shape=shapes,
        in_specs=[spec(SMEM)] * 5 + [spec(ANY)] * 2,
        out_specs=[spec(ANY)] * len(shapes),
        scratch_shapes=[
            VMEM((slots, room, ROWS_G, tile), BF16),
            VMEM(values.shape, BF16),
            VMEM((head, ROWS_G, tile), BF16),
            VMEM(grads.shape, BF16),
            SMEM((slots, INFO, lanes), jnp.int32),
            SMEM((2, slots), jnp.int32),
            pltpu.SemaphoreType.DMA((5 + (len(sizes) + 2) * slots,)),
        ],
        compiler_params=params(PACK_MIB),
        cost_estimate=cost(0, 8),
    )(me, owner, count, block, row, grads, values)
    pieces = [list(outs[i * slots : (i + 1) * slots]) for i in range(len(sizes))]
    return pieces, list(outs[-slots:]), head


def hist_kernel(kind, skip, senders, unit, row_blocks, which_ref, info_ref, *refs):
    first, last = kind
    got_refs, (grads_ref, cuts_ref), refs = (
        refs[:senders],
        refs[senders : senders + 2],
        refs[senders + 2 :],
    )
    if not first:
        before_ref, refs = refs[0], refs[1:]
    if last:
        more_ref, out_ref, hist_ref, got, sem, extra = refs
    else:
        hist_ref, got, sem = refs
    length, tile = got_refs[0].shape[0] - skip, got_refs[0].shape[2]
    per_tile = tile // ROWS_G
    blocks, levels = cuts_ref.shape[:2]
    k_out, lanes = hist_ref.shape[2], info_ref.shape[2]
    low = which_ref[0]
    copies = [
        pltpu.make_async_copy(
            got_refs[s].at[pl.ds(skip, length)],
            got.at[pl.ds(per_tile + s * length, length)],
            sem.at[s],
        )
        for s in range(senders)
    ]
    for copy in copies:
        copy.start()

    def clear(b, carry):
        hist_ref[b] = jnp.zeros(hist_ref.shape[1:], jnp.float32)
        return carry

    def keep(b, carry):
        hist_ref[b] = before_ref[b]
        return carry

    if first:
        lax.fori_loop(0, blocks, clear, 0)
    else:
        fresh = which_ref[3] > 0
        lax.fori_loop(0, jnp.where(fresh, blocks, 0), clear, 0)
        lax.fori_loop(0, jnp.where(fresh, 0, blocks), keep, 0)
    for copy in copies:
        copy.wait()
    row = as_bf16(lax.broadcasted_iota(jnp.int32, (tile, tile), 0))
    lane = as_bf16(lax.broadcasted_iota(jnp.int32, (tile, tile), 1))
    one, zero = jnp.ones((tile, tile), BF16), jnp.zeros((tile, tile), BF16)
    per = ROWS_G * tile

    def load(s, i, end):
        at, block = info_ref[s, 0, i], info_ref[s, 2, i]
        count = jnp.where(i < end, info_ref[s, 1, i], 0)
        count = jnp.minimum(count, (low + length - at) * per)
        start = per_tile + s * length + at - low
        values = got[pl.ds(start, per_tile)].reshape(tile, tile)
        whole = as_bf16(shifted(count, tile))
        part = as_bf16(count & (tile - 1))
        above = as_bf16((low - at) * ROWS_G)
        live = ((row < whole) | ((row == whole) & (lane < part))) & (row >= above)
        values = jnp.where(live, values, jnp.full_like(values, -1000.0))
        return block, values, s * row_blocks + info_ref[s, 3, i]

    def sender(s, carry):
        tiles = info_ref[s, 4, lanes - 2]
        begin = jnp.minimum(info_ref[s, 4, shifted(low, unit)], tiles)
        end = jnp.minimum(info_ref[s, 5, shifted(low + length, unit)], tiles)

        def pair(p, carry):
            i = begin + 2 * p
            block_a, va, line_a = load(s, i, end)
            block_b, vb, line_b = load(s, jnp.minimum(i + 1, end - 1), jnp.where(i + 1 < end, end, 0))
            left = jnp.concatenate([grads_ref[0, line_a], grads_ref[1, line_b]], axis=1)
            for c in range(0, levels, 2):
                columns = []
                for d in (c, c + 1):
                    cut_a = jnp.broadcast_to(cuts_ref[block_a, d : d + 1], (tile, tile))
                    cut_b = jnp.broadcast_to(cuts_ref[block_b, d : d + 1], (tile, tile))
                    columns.append(
                        jnp.concatenate(
                            [
                                jnp.where(va > cut_a.astype(BF16), one, zero),
                                jnp.where(vb > cut_b.astype(BF16), one, zero),
                            ],
                            axis=0,
                        )
                    )
                sums = jnp.dot(
                    left, jnp.concatenate(columns, axis=1), preferred_element_type=jnp.float32
                )
                hist_ref[block_a, c] += sums[:k_out, :tile]
                hist_ref[block_a, c + 1] += sums[:k_out, tile:]
                hist_ref[block_b, c] += sums[k_out:, :tile]
                hist_ref[block_b, c + 1] += sums[k_out:, tile:]
            return carry

        lax.fori_loop(0, shifted(jnp.maximum(end - begin, 0) + 1, 2), pair, 0)
        return carry

    lax.fori_loop(0, senders, sender, 0)
    if not last:
        return

    @pl.when(which_ref[1] > 0)
    def _():
        def add(b, carry):
            copy = pltpu.make_async_copy(more_ref.at[b], extra, sem.at[senders])
            copy.start()
            copy.wait()
            hist_ref[b] += extra[...]
            return carry

        lax.fori_loop(0, blocks, add, 0)

    slots, per_slot = out_ref.shape[0], out_ref.shape[1]
    me = which_ref[2]

    def step(i, carry):
        for slot in range(slots):
            above = hist_ref[(slot ^ me) * per_slot + i]
            below = jnp.concatenate(
                [above[1:], jnp.zeros((1, k_out, tile), jnp.float32)], axis=0
            )
            out_ref[slot, i] = (above - below).reshape(levels * k_out, tile).astype(BF16)
        return carry

    lax.fori_loop(0, per_slot, step, 0)


def add_tiles(hist, which, info, got, grads, cuts, skip, unit, slots=0, more=None):
    first, last = hist is None, slots > 0
    senders, length, tile = len(got), got[0].shape[0] - skip, got[0].shape[2]
    blocks, levels = cuts.shape[0], cuts.shape[1]
    k_out = grads.shape[2] // 2
    args = [which, info, *got, grads, cuts]
    specs = [spec(SMEM)] * 2 + [spec(ANY)] * senders + [spec(VMEM)] * 2
    whole = jax.ShapeDtypeStruct((blocks, levels, k_out, tile), jnp.float32)
    outs, aliases = [whole], {}
    if last:
        outs = [jax.ShapeDtypeStruct((slots, blocks // slots, levels * k_out, tile), BF16), whole]
    if not first:
        aliases = {len(args): len(outs) - 1}
        args.append(hist)
        specs.append(spec(VMEM))
    if last:
        args.append(more)
        specs.append(spec(ANY))
    result = pl.pallas_call(
        functools.partial(
            hist_kernel, (first, last), skip, senders, unit, grads.shape[1] // senders
        ),
        out_shape=outs,
        in_specs=specs,
        out_specs=[spec(VMEM)] * len(outs),
        scratch_shapes=[
            VMEM((senders * length + 2 * (tile // ROWS_G), ROWS_G, tile), BF16),
            pltpu.SemaphoreType.DMA((senders + 1,)),
        ]
        + ([VMEM(whole.shape[1:], jnp.float32)] if last else []),
        input_output_aliases=aliases,
        compiler_params=params(28),
        cost_estimate=cost(10**10, 24),
    )(*args)
    return result[0]


def unwritten(shape):
    return pl.pallas_call(
        lambda out_ref: None,
        out_shape=jax.ShapeDtypeStruct(shape, jnp.float32),
        out_specs=spec(ANY),
        compiler_params=params(PACK_MIB),
    )()


def finish_kernel(k_out, *refs):
    parts, out_ref, scratch = refs[:-2], refs[-2], refs[-1]
    blocks, rows, tile = parts[0].shape
    levels = rows // k_out
    for b in range(blocks):
        total = parts[0][b].astype(jnp.float32)
        for part in parts[1:]:
            total = total + part[b].astype(jnp.float32)
        scratch[...] = total
        for k in range(k_out):
            out_ref[k, :, b * tile : (b + 1) * tile] = scratch[pl.ds(k, levels, stride=k_out), :]


def finish(parts, k_out):
    blocks, rows, tile = parts[0].shape
    return pl.pallas_call(
        functools.partial(finish_kernel, k_out),
        out_shape=jax.ShapeDtypeStruct((k_out, rows // k_out, blocks * tile), jnp.float32),
        in_specs=[spec(VMEM)] * len(parts),
        out_specs=spec(VMEM),
        scratch_shapes=[VMEM((rows, tile), jnp.float32)],
        compiler_params=params(16),
    )(*parts)


def reduce_rows(slots, k_out, axis):
    n = slots.shape[0]
    parts = {p: [slots[p]] for p in range(n)}
    bit = 1
    while bit < n:
        for p in sorted((p for p in parts if p & bit), reverse=True):
            have = parts.pop(p)
            if len(have) > 1:
                value = functools.reduce(jnp.add, [x.astype(jnp.float32) for x in have])
                value = value.astype(BF16)
            else:
                value = have[0]
            moved = lax.ppermute(value, axis, [(i, i ^ bit) for i in range(n)])
            parts[p ^ bit].append(moved)
        bit *= 2
    return finish(parts[0], k_out)


def shards(tile_values, tile_row, tile_block, tile_count, tile_owner, cut_index, gradients):
    owners = lax.axis_size("feat")
    row_groups = lax.axis_size("rows")
    tile_dev, tile = tile_values.shape[:2]
    levels = cut_index.shape[0] + 1
    k_out, rows_dev = gradients.shape
    row_blocks = rows_dev // tile
    fb_dev = cut_index.shape[1] // tile
    per_tile = tile // ROWS_G
    capacity = max(2, 2 * tile_dev // owners) * per_tile
    static = [capacity // 12 * i for i in (1, 2, 2, 2, 1)]
    turn = max(per_tile, capacity // 12)
    left = -(-(capacity - sum(static)) // turn) * turn
    me = lax.axis_index("feat").astype(jnp.int32)
    sent, infos, skip = pack(
        me[None], tile_owner[:, 0], tile_count, tile_block, tile_row, gradients, tile_values,
        static + [left], turn, owners,
    )

    n = 2 * cut_index + (1 - 10 * (levels - 1))
    n = jnp.where(jnp.abs(n) > 256, n - 1, n)
    cuts = n.astype(jnp.float32) / 128.0
    cuts = jnp.concatenate([jnp.full((1, fb_dev * tile), -512.0, jnp.float32), cuts], axis=0)
    cuts = jnp.transpose(cuts.reshape(levels, fb_dev, tile), (1, 0, 2))

    def exchange(pieces):
        moved = [
            lax.ppermute(pieces[d], "feat", [(i, (i + d) % owners) for i in range(owners)])
            for d in range(1, owners)
        ]
        return [pieces[0]] + moved

    info = jnp.stack(exchange(infos), axis=0)
    got = []
    for number in range(len(static)):
        pieces = sent[number]
        if number > 1:
            got[number - 2], pieces = lax.optimization_barrier((got[number - 2], pieces))
        got.append(exchange(pieces))

    grads = jnp.stack([x[:skip] for x in got[0]], axis=0)
    grads = grads.reshape(owners * row_blocks, k_out, tile)
    nothing = jnp.zeros_like(grads)
    grads = jnp.stack(
        [jnp.concatenate([grads, nothing], axis=1), jnp.concatenate([nothing, grads], axis=1)],
        axis=0,
    )
    mine = lax.axis_index("rows").astype(jnp.int32)

    most = jnp.max(info[:, 4, -1])
    turns = (most - sum(static) + turn - 1) // turn

    def which(low, fresh=0):
        return jnp.stack([jnp.asarray(x, jnp.int32) for x in (low, turns, mine, fresh)])

    def more(carry):
        return carry[0] < turns

    def step(carry):
        r, hist = carry
        pieces = [lax.dynamic_slice_in_dim(x, r * turn, turn, axis=0) for x in sent[-1]]
        hist = add_tiles(
            hist,
            which(sum(static) + r * turn, r == 0),
            info,
            exchange(pieces),
            grads,
            cuts,
            0,
            turn,
        )
        return r + 1, hist

    extra = unwritten((fb_dev, levels, k_out, tile))
    _, extra = lax.while_loop(more, step, (jnp.int32(0), extra))
    extra, grads = lax.optimization_barrier((extra, grads))
    hist, low = None, 0
    for number, size in enumerate(static):
        last = {"slots": row_groups, "more": extra} if number == len(static) - 1 else {}
        hist = add_tiles(
            hist, which(low), info, got[number], grads, cuts, 0 if number else skip, turn, **last
        )
        low += size
    return reduce_rows(hist, k_out, "rows")


def solution(mesh):
    placed = (
        P(("grp", "feat", "rows"), None, None),
        P(("grp", "feat", "rows")),
        P(("grp", "feat", "rows")),
        P(("grp", "feat", "rows")),
        P(("grp", "feat", "rows"), None),
        P(None, ("grp", "feat")),
        P(None, ("grp", "feat", "rows")),
    )
    return jax.shard_map(
        shards,
        mesh=mesh,
        in_specs=placed,
        out_specs=P(None, None, ("grp", "feat", "rows")),
        check_vma=False,
    )
```

time: 576 us -> 143 us (0.25); the launches traced: 571 us -> 144 us
  other arithmetic: 181 us -> 3.48 us
  blocking collectives: 141 us -> 0 us
  local copies, waits for them, and re-layouts: 93.1 us -> 1.31 us
  matrix products: 91.7 us -> 0 us
  Pallas kernels: 0 us -> 62.5 us
  starting transfers between devices: 11.7 us -> 42 us
  between operations: 13.5 us -> 1.09 us
    all_gather x1 -> x0, blocking collectives: 141 us -> none  [shards(): lax.all_gather(gradients, 'feat', axis=1, tiled=True)]
    dot_general x24 -> x0, matrix products: 91.7 us -> none  [step(): jnp.einsum('wki,wibj->kbwj', grad_rows, onehot, preferred_element_type=jn...]
    scatter-add x24 -> x0, other arithmetic: 91.2 us -> none  [step(): carry = carry.at[:, :, info[:, 1], :].add(sums)]
    add x49 -> x0, other arithmetic: 64.9 us -> none  [the longest x24 62.3 us: step(): level = level + (vfloat > cut_rows[c][:, None, :]).astype(jnp.int32)]
    pallas_call x0 -> x8, Pallas kernels: none -> 62.5 us  [the longest x5 54.2 us: add_tiles(): pl.pallas_call(functools.partial(hist_kernel, (first, last), skip, sender...]
    gather x29 -> x0, local copies, waits for them, and re-layouts: 55.7 us -> none  [the longest x24 40.5 us: step(): cut_rows = jnp.take(cuts, info[:, 1], axis=1)]
    ppermute x0 -> x21, starting transfers between devices: none -> 42 us  [the longest x18 40.3 us: exchange(): lax.ppermute(pieces[d], 'feat', [(i, (i + d) % owners) for i in range(own...]
    reduce_scatter x1 -> x0, waiting for transfers between devices: 36.7 us -> none  [shards(): lax.psum_scatter(hist.reshape(k_out, levels, fb_dev * tile).astype(jnp.bf...]
  transfers between devices with their start and end apart: 3 -> 21, of which waited for: 1 -> 3; matrix products, arithmetic and copies ran while one was open for 4% -> 3% of each run, Pallas kernels for 0% -> 35%
where the time goes in v2:
time: 143 us; the launch traced here: 144 us
  Pallas kernels  62.5 us (44%)
  starting transfers between devices  42 us (29%)
  waiting for transfers between devices  33.5 us (23%)
  other arithmetic  3.48 us (2%)
    pallas_call x5, Pallas kernels, add_tiles(): pl.pallas_call(functools.partial(hist_kernel, (first, last), skip, sender...  54.2 us
    ppermute x18, starting transfers between devices, exchange(): lax.ppermute(pieces[d], 'feat', [(i, (i + d) % owners) for i in range(own...  40.3 us
    ppermute x3, waiting for transfers between devices, reduce_rows(): moved = lax.ppermute(value, axis, [(i, i ^ bit) for i in range(n)])  20.2 us
    ppermute x18, waiting for transfers between devices, exchange(): lax.ppermute(pieces[d], 'feat', [(i, (i + d) % owners) for i in range(own...  13.2 us
    pallas_call x1, Pallas kernels, pack(): pl.pallas_call(functools.partial(pack_kernel, sizes, unit), out_shape=sha...  6.55 us
  transfers between devices with their start and end apart: 21, of which 3 were waited for; matrix products, arithmetic and copies ran while one was open for 3% of the time, Pallas kernels for 35%

profile of v2, /device:TPU:0, one launch (start us, length us, event | category | flops | bytes accessed | tf_op | source)
XLA Modules:
  0.0 143.9 jit_solution(3328552602463187736)
XLA Ops:
  0.0 6.5 %shard_map.73 = (bf16[36,16,128]{2,1,0:T(8,128)(2,1)}, bf16[36,16,128]{2,1,0:T(8,128)(2,1)}, bf16[36,16,128]{2,1,0:T(8,128)(2,1)}, bf16[36,16,128]{2,1,0:T(8,128...) custom-call(s32[1]{0:T(128)} %bitcast.4.me_ref, ...), custom_call_target="tpu_custom_call" | custom-call | bytes 8388608 | tf_op jit(solution)/shard_map/pallas_call | solution.py:137
  6.6 3.1 %collective-permute-start.6 = (bf16[36,16,128]{2,1,0:T(8,128)(2,1)}, bf16[36,16,128]{2,1,0:T(8,128)(2,1)S(1)}, u32[]{:S(2)}, u32[]{:S(2)}) collective-permute-start(bf16[36,16,128]{2,1,0:T(8,128)(2,1)} %get-tuple-element.123), channel_id=1, source_target_pairs={{0,4},{4,8},{8,12},{12,0},{1,5},{5,9},{9,13},{13,1},{2,6},{6,10},{... | collective-permute-start | bytes 442376 | tf_op jit(solution)/shard_map/ppermute | solution.py:403
  9.7 1.6 %collective-permute-start.3 = (s32[6,128]{1,0:T(8,128)}, s32[6,128]{1,0:T(8,128)S(1)}, u32[]{:S(2)}, u32[]{:S(2)}) collective-permute-start(s32[6,128]{1,0:T(8,128)} %get-tuple-element.119), channel_id=1, source_target_pairs={{0,4},{4,8},{8,12},{12,0},{1,5},{5,9},{9,13},{13,1},{2,6},{6,10},{... | collective-permute-start | bytes 9224 | tf_op jit(solution)/shard_map/ppermute | solution.py:403
  11.3 1.1 collective-permute-start.4
  12.3 2.9 %collective-permute-start.5 = (s32[6,128]{1,0:T(8,128)}, s32[6,128]{1,0:T(8,128)S(1)}, u32[]{:S(2)}, u32[]{:S(2)}) collective-permute-start(s32[6,128]{1,0:T(8,128)} %get-tuple-element.121), channel_id=1, source_target_pairs={{0,12},{4,0},{8,4},{12,8},{1,13},{5,1},{9,5},{13,9},{2,14},{6,2},{... | collective-permute-start | bytes 9224 | tf_op jit(solution)/shard_map/ppermute | solution.py:403
  15.2 1.4 convert_multiply_fusion
  16.6 1.0 bitcast_bitcast_fusion.refs_5_
  17.6 0.3 collective-permute-start.7
  17.9 0.0 collective-permute-done.3
  17.9 1.2 collective-permute-start.8
  19.1 0.0 collective-permute-done.4
  19.1 0.8 collective-permute-start.15
  19.9 0.0 collective-permute-done.5
  20.0 0.7 slice_reduce_fusion
  21.4 2.7 %collective-permute-start.16 = (bf16[64,16,128]{2,1,0:T(8,128)(2,1)}, bf16[64,16,128]{2,1,0:T(8,128)(2,1)S(1)}, u32[]{:S(2)}, u32[]{:S(2)}) collective-permute-start(bf16[64,16,128]{2,1,0:T(8,128)(2,1)} %get-tuple-element.154), channel_id=1, source_target_pairs={{0,8},{4,12},{8,0},{12,4},{1,9},{5,13},{9,1},{13,5},{2,10},{6,14},... | collective-permute-start | bytes 786440 | tf_op jit(solution)/shard_map/ppermute | solution.py:403
  24.0 0.0 collective-permute-done.6.refs_1_
  24.0 13.2 %collective-permute-done.7.refs_2_ = bf16[36,16,128]{2,1,0:T(8,128)(2,1)S(1)} collective-permute-done((bf16[36,16,128]{2,1,0:T(8,128)(2,1)S(1)}, bf16[36,16,128]{2,1,0:T(8,128)(2,1)S(1)}, u32[]{:S(2)}, u32[]{:S(2)}) %collective-permute-start.7) | collective-permute-done | bytes 147488 | tf_op jit(solution)/shard_map/ppermute | solution.py:403
  37.2 0.0 collective-permute-done.8.refs_3_
  37.3 0.7 pad_maximum_fusion.refs_4_
  38.0 0.0 collective-permute-start.17
  38.0 0.1 pad_add_fusion.2.which_ref
  38.1 0.1 pad_add_fusion.3.which_ref
  38.2 0.1 pad_add_fusion.4.which_ref
  38.3 0.1 pad_add_fusion.5.which_ref
  38.4 0.1 pad_add_fusion.6.which_ref
  38.4 0.0 copy-start.3
  38.5 0.0 copy-start.5
  38.5 5.2 %collective-permute-start.10 = (bf16[64,16,128]{2,1,0:T(8,128)(2,1)}, bf16[64,16,128]{2,1,0:T(8,128)(2,1)S(1)}, u32[]{:S(2)}, u32[]{:S(2)}) collective-permute-start(bf16[64,16,128]{2,1,0:T(8,128)(2,1)} %get-tuple-element.132), channel_id=1, source_target_pairs={{0,8},{4,12},{8,0},{12,4},{1,9},{5,13},{9,1},{13,5},{2,10},{6,14},... | collective-permute-start | bytes 786440 | tf_op jit(solution)/shard_map/ppermute | solution.py:403
  43.7 0.9 collective-permute-start.11
  44.6 8.2 %shard_map.75.refs_6_ = f32[48,32,8,128]{3,2,1,0:T(8,128)S(1)} custom-call(s32[4]{0:T(128)S(1)} %pad_add_fusion.2.which_ref, s32[4,6,128]{2,1,0:T(8,128)S(1)} %get-tuple-element.350, bf16[36,16,128]{2,1,0:T(8,128)(2,1)S(1)} %copy-done, bf16[36,16,128]{2,1,0:T(8,128)(2,1)S(1)} %collective-permute-done.6.refs_1_, ...), custom_call_target="tpu_custom_call" | custom-call | flops 10000000000 | bytes 25165824 | tf_op jit(solution)/shard_map/pallas_call | solution.py:305
  52.8 0.0 collective-permute-done.15.refs_1_
  52.9 2.8 %collective-permute-start.9 = (bf16[64,16,128]{2,1,0:T(8,128)(2,1)S(1)}, bf16[64,16,128]{2,1,0:T(8,128)(2,1)S(1)}, u32[]{:S(2)}, u32[]{:S(2)}) collective-permute-start(bf16[64,16,128]{2,1,0:T(8,128)(2,1)S(1)} %copy-done.11), channel_id=1, source_target_pairs={{0,4},{4,8},{8,12},{12,0},{1,5},{5,9},{9,13},{13,1},{2,6},{6,10},{... | collective-permute-start | bytes 786440 | tf_op jit(solution)/shard_map/ppermute | solution.py:403
  55.6 0.0 collective-permute-done.16.refs_2_
  55.6 0.0 collective-permute-done.17.refs_3_
  55.7 6.0 %collective-permute-start.18 = (bf16[64,16,128]{2,1,0:T(8,128)(2,1)S(1)}, bf16[64,16,128]{2,1,0:T(8,128)(2,1)S(1)}, u32[]{:S(2)}, u32[]{:S(2)}) collective-permute-start(bf16[64,16,128]{2,1,0:T(8,128)(2,1)S(1)} %copy-done.10), channel_id=1, source_target_pairs={{0,4},{4,8},{8,12},{12,0},{1,5},{5,9},{9,13},{13,1},{2,6},{6,10},{... | collective-permute-start | bytes 786440 | tf_op jit(solution)/shard_map/ppermute | solution.py:403
  61.7 3.3 %collective-permute-start.19 = (bf16[64,16,128]{2,1,0:T(8,128)(2,1)S(1)}, bf16[64,16,128]{2,1,0:T(8,128)(2,1)S(1)}, u32[]{:S(2)}, u32[]{:S(2)}) collective-permute-start(bf16[64,16,128]{2,1,0:T(8,128)(2,1)S(1)} %copy-done.9), channel_id=1, source_target_pairs={{0,8},{4,12},{8,0},{12,4},{1,9},{5,13},{9,1},{13,5},{2,10},{6,14},... | collective-permute-start | bytes 786440 | tf_op jit(solution)/shard_map/ppermute | solution.py:403
  65.0 15.3 %shard_map.76.refs_6_ = f32[48,32,8,128]{3,2,1,0:T(8,128)S(1)} custom-call(s32[4]{0:T(128)S(1)} %pad_add_fusion.3.which_ref, s32[4,6,128]{2,1,0:T(8,128)S(1)} %get-tuple-element.350, bf16[64,16,128]{2,1,0:T(8,128)(2,1)S(1)} %copy-done.3, bf16[64,16,128]{2,1,0:T(8,128)(2,1)S(1)} %collective-permute-done.15.refs_1_, ...), custom_call_target="tpu_custom_call", output_to_operand_aliasing={{}: (8, {})} | custom-call | flops 10000000000 | bytes 25165824 | tf_op jit(solution)/shard_map/pallas_call | solution.py:305
  80.4 0.0 collective-permute-done.10.refs_2_
  80.4 0.1 collective-permute-start.20
  80.4 0.0 collective-permute-done.11.refs_3_
  80.5 0.0 collective-permute-done.9.refs_1_
  80.5 8.3 %collective-permute-start.12 = (bf16[32,16,128]{2,1,0:T(8,128)(2,1)S(1)}, bf16[32,16,128]{2,1,0:T(8,128)(2,1)S(1)}, u32[]{:S(2)}, u32[]{:S(2)}) collective-permute-start(bf16[32,16,128]{2,1,0:T(8,128)(2,1)S(1)} %copy-done.16), channel_id=1, source_target_pairs={{0,4},{4,8},{8,12},{12,0},{1,5},{5,9},{9,13},{13,1},{2,6},{6,10},{... | collective-permute-start | bytes 393224 | tf_op jit(solution)/shard_map/ppermute | solution.py:403
  88.8 0.0 collective-permute-start.13
  88.8 0.0 slice-start
  88.8 13.7 %shard_map.77.refs_6_ = f32[48,32,8,128]{3,2,1,0:T(8,128)S(1)} custom-call(s32[4]{0:T(128)S(1)} %pad_add_fusion.4.which_ref, s32[4,6,128]{2,1,0:T(8,128)S(1)} %get-tuple-element.350, bf16[64,16,128]{2,1,0:T(8,128)(2,1)S(1)} %copy-done.2, bf16[64,16,128]{2,1,0:T(8,128)(2,1)S(1)} %collective-permute-done.9.refs_1_, ...), custom_call_target="tpu_custom_call", output_to_operand_aliasing={{}: (8, {})} | custom-call | flops 10000000000 | bytes 25165824 | tf_op jit(solution)/shard_map/pallas_call | solution.py:305
  102.6 0.0 slice-start.1
  102.6 0.0 collective-permute-done.18.refs_1_
  102.6 0.1 collective-permute-start.14
  102.7 0.0 collective-permute-done.19.refs_2_
  102.7 0.0 collective-permute-done.20.refs_3_
  102.7 12.9 %shard_map.78.refs_6_ = f32[48,32,8,128]{3,2,1,0:T(8,128)S(1)} custom-call(s32[4]{0:T(128)S(1)} %pad_add_fusion.5.which_ref, s32[4,6,128]{2,1,0:T(8,128)S(1)} %get-tuple-element.350, bf16[64,16,128]{2,1,0:T(8,128)(2,1)S(1)} %copy-done.1, bf16[64,16,128]{2,1,0:T(8,128)(2,1)S(1)} %collective-permute-done.18.refs_1_, ...), custom_call_target="tpu_custom_call", output_to_operand_aliasing={{}: (8, {})} | custom-call | flops 10000000000 | bytes 25165824 | tf_op jit(solution)/shard_map/pallas_call | solution.py:305
  115.6 0.0 collective-permute-done.12.refs_1_
  115.6 0.0 collective-permute-done.13.refs_2_
  115.6 0.0 collective-permute-done.14.refs_3_
  115.6 4.1 %shard_map.79 = (bf16[4,12,256,128]{3,2,1,0:T(8,128)(2,1)S(1)}, f32[48,32,8,128]{3,2,1,0:T(8,128)S(1)}) custom-call(s32[4]{0:T(128)S(1)} %pad_add_fusion.6.which_ref, s32[4,6,128]{2,1,0:T(8,128)S(1)} %get-tuple-element.350, bf16[32,16,128]{2,1,0:T(8,128)(2,1)S(1)} %copy-done.4, ...), custom_call_target="tpu_custom_call", output_to_operand_aliasing={{1}: (8, {})} | custom-call | flops 10000000000 | bytes 25165824 | tf_op jit(solution)/shard_map/pallas_call | solution.py:305
  119.8 0.2 slice_bitcast_fusion
  120.0 0.1 collective-permute-start.22
  120.0 0.5 collective-permute-start.21
  120.5 1.8 %collective-permute-done.22 = bf16[12,256,128]{2,1,0:T(8,128)(2,1)S(1)} collective-permute-done((bf16[12,256,128]{2,1,0:T(8,128)(2,1)S(1)}, bf16[12,256,128]{2,1,0:T(8,128)(2,1)S(1)}, u32[]{:S(2)}, u32[]{:S(2)}) %collective-permute-start.22) | collective-permute-done | bytes 786464 | tf_op jit(solution)/shard_map/ppermute | solution.py:370
  122.3 0.2 fusion
  122.5 1.2 collective-permute-start.23
  123.7 0.0 collective-permute-done.21.refs_1_
  123.7 18.5 %collective-permute-done.23.refs_2_ = bf16[12,256,128]{2,1,0:T(8,128)(2,1)S(1)} collective-permute-done((bf16[12,256,128]{2,1,0:T(8,128)(2,1)S(1)}, bf16[12,256,128]{2,1,0:T(8,128)(2,1)S(1)}, u32[]{:S(2)}, u32[]{:S(2)}) %collective-permute-start.23) | collective-permute-done | bytes 786464 | tf_op jit(solution)/shard_map/ppermute | solution.py:370
  142.2 1.7 %shard_map.80 = f32[8,32,1536]{2,1,0:T(8,128)} custom-call(bf16[12,256,128]{2,1,0:T(8,128)(2,1)S(1)} %get-tuple-element.198.refs_0_, bf16[12,256,128]{2,1,0:T(8,128)(2,1)S(1)} %collective-permute-done.21.refs_1_, bf16[12,256,128]{2,1,0:T(8,128)(2,1)S(1)} %collective-permute-done.23.refs_2_), custom_call_target="tpu_custom_call" | custom-call | tf_op jit(solution)/shard_map/pallas_call | solution.py:348
  (42 shorter events, 0.1 us)
Async XLA Ops:
  6.6 11.0 %copy-start.13 = (bf16[36,16,128]{2,1,0:T(8,128)(2,1)S(1)}, bf16[36,16,128]{2,1,0:T(8,128)(2,1)}, u32[]{:S(2)}) copy-start(bf16[36,16,128]{2,1,0:T(8,128)(2,1)} %get-tuple-element.124) | copy-start | bytes 442372
  6.6 11.3 %copy-start.12 = (bf16[36,16,128]{2,1,0:T(8,128)(2,1)S(1)}, bf16[36,16,128]{2,1,0:T(8,128)(2,1)}, u32[]{:S(2)}) copy-start(bf16[36,16,128]{2,1,0:T(8,128)(2,1)} %get-tuple-element.125) | copy-start | bytes 442372
  6.6 13.4 %copy-start.7 = (s32[6,128]{1,0:T(8,128)S(1)}, s32[6,128]{1,0:T(8,128)}, u32[]{:S(2)}) copy-start(s32[6,128]{1,0:T(8,128)} %get-tuple-element.118) | copy-start | bytes 9220
  6.6 30.6 %copy-start = (bf16[36,16,128]{2,1,0:T(8,128)(2,1)S(1)}, bf16[36,16,128]{2,1,0:T(8,128)(2,1)}, u32[]{:S(2)}) copy-start(bf16[36,16,128]{2,1,0:T(8,128)(2,1)} %get-tuple-element.146.refs_0_) | copy-start | bytes 442372
  6.6 17.4 %collective-permute-start.6 = (bf16[36,16,128]{2,1,0:T(8,128)(2,1)}, bf16[36,16,128]{2,1,0:T(8,128)(2,1)S(1)}, u32[]{:S(2)}, u32[]{:S(2)}) collective-permute-start(bf16[36,16,128]{2,1,0:T(8,128)(2,1)} %get-tuple-element.123), channel_id=1, source_target_pairs={{0,4},{4,8},{8,12},{12,0},{1,5},{5,9},{9,13},{13,1},{2,6},{6,10},{... | collective-permute-start | bytes 442376 | tf_op jit(solution)/shard_map/ppermute | solution.py:403
  9.7 8.2 %collective-permute-start.3 = (s32[6,128]{1,0:T(8,128)}, s32[6,128]{1,0:T(8,128)S(1)}, u32[]{:S(2)}, u32[]{:S(2)}) collective-permute-start(s32[6,128]{1,0:T(8,128)} %get-tuple-element.119), channel_id=1, source_target_pairs={{0,4},{4,8},{8,12},{12,0},{1,5},{5,9},{9,13},{13,1},{2,6},{6,10},{... | collective-permute-start | bytes 9224 | tf_op jit(solution)/shard_map/ppermute | solution.py:403
  11.3 7.9 %collective-permute-start.4 = (s32[6,128]{1,0:T(8,128)}, s32[6,128]{1,0:T(8,128)S(1)}, u32[]{:S(2)}, u32[]{:S(2)}) collective-permute-start(s32[6,128]{1,0:T(8,128)} %get-tuple-element.120), channel_id=1, source_target_pairs={{0,8},{4,12},{8,0},{12,4},{1,9},{5,13},{9,1},{13,5},{2,10},{6,14},... | collective-permute-start | bytes 9224 | tf_op jit(solution)/shard_map/ppermute | solution.py:403
  12.3 7.6 %collective-permute-start.5 = (s32[6,128]{1,0:T(8,128)}, s32[6,128]{1,0:T(8,128)S(1)}, u32[]{:S(2)}, u32[]{:S(2)}) collective-permute-start(s32[6,128]{1,0:T(8,128)} %get-tuple-element.121), channel_id=1, source_target_pairs={{0,12},{4,0},{8,4},{12,8},{1,13},{5,1},{9,5},{13,9},{2,14},{6,2},{... | collective-permute-start | bytes 9224 | tf_op jit(solution)/shard_map/ppermute | solution.py:403
  17.6 19.6 %collective-permute-start.7 = (bf16[36,16,128]{2,1,0:T(8,128)(2,1)S(1)}, bf16[36,16,128]{2,1,0:T(8,128)(2,1)S(1)}, u32[]{:S(2)}, u32[]{:S(2)}) collective-permute-start(bf16[36,16,128]{2,1,0:T(8,128)(2,1)S(1)} %copy-done.13), channel_id=1, source_target_pairs={{0,8},{4,12},{8,0},{12,4},{1,9},{5,13},{9,1},{13,5},{2,10},{6,14},... | collective-permute-start | bytes 442376 | tf_op jit(solution)/shard_map/ppermute | solution.py:403
  17.9 19.3 %collective-permute-start.8 = (bf16[36,16,128]{2,1,0:T(8,128)(2,1)S(1)}, bf16[36,16,128]{2,1,0:T(8,128)(2,1)S(1)}, u32[]{:S(2)}, u32[]{:S(2)}) collective-permute-start(bf16[36,16,128]{2,1,0:T(8,128)(2,1)S(1)} %copy-done.12), channel_id=1, source_target_pairs={{0,12},{4,0},{8,4},{12,8},{1,13},{5,1},{9,5},{13,9},{2,14},{6,2},{... | collective-permute-start | bytes 442376 | tf_op jit(solution)/shard_map/ppermute | solution.py:403
  19.1 33.7 %collective-permute-start.15 = (bf16[64,16,128]{2,1,0:T(8,128)(2,1)}, bf16[64,16,128]{2,1,0:T(8,128)(2,1)S(1)}, u32[]{:S(2)}, u32[]{:S(2)}) collective-permute-start(bf16[64,16,128]{2,1,0:T(8,128)(2,1)} %get-tuple-element.153), channel_id=1, source_target_pairs={{0,4},{4,8},{8,12},{12,0},{1,5},{5,9},{9,13},{13,1},{2,6},{6,10},{... | collective-permute-start | bytes 786440 | tf_op jit(solution)/shard_map/ppermute | solution.py:403
  21.4 34.3 %collective-permute-start.16 = (bf16[64,16,128]{2,1,0:T(8,128)(2,1)}, bf16[64,16,128]{2,1,0:T(8,128)(2,1)S(1)}, u32[]{:S(2)}, u32[]{:S(2)}) collective-permute-start(bf16[64,16,128]{2,1,0:T(8,128)(2,1)} %get-tuple-element.154), channel_id=1, source_target_pairs={{0,8},{4,12},{8,0},{12,4},{1,9},{5,13},{9,1},{13,5},{2,10},{6,14},... | collective-permute-start | bytes 786440 | tf_op jit(solution)/shard_map/ppermute | solution.py:403
  38.0 17.6 %collective-permute-start.17 = (bf16[64,16,128]{2,1,0:T(8,128)(2,1)}, bf16[64,16,128]{2,1,0:T(8,128)(2,1)S(1)}, u32[]{:S(2)}, u32[]{:S(2)}) collective-permute-start(bf16[64,16,128]{2,1,0:T(8,128)(2,1)} %get-tuple-element.155), channel_id=1, source_target_pairs={{0,12},{4,0},{8,4},{12,8},{1,13},{5,1},{9,5},{13,9},{2,14},{6,2},{... | collective-permute-start | bytes 786440 | tf_op jit(solution)/shard_map/ppermute | solution.py:403
  38.4 14.4 %copy-start.11 = (bf16[64,16,128]{2,1,0:T(8,128)(2,1)S(1)}, bf16[64,16,128]{2,1,0:T(8,128)(2,1)}, u32[]{:S(2)}) copy-start(bf16[64,16,128]{2,1,0:T(8,128)(2,1)} %get-tuple-element.131) | copy-start | bytes 786436
  38.4 17.2 %copy-start.10 = (bf16[64,16,128]{2,1,0:T(8,128)(2,1)S(1)}, bf16[64,16,128]{2,1,0:T(8,128)(2,1)}, u32[]{:S(2)}) copy-start(bf16[64,16,128]{2,1,0:T(8,128)(2,1)} %get-tuple-element.161) | copy-start | bytes 786436
  38.4 23.2 %copy-start.9 = (bf16[64,16,128]{2,1,0:T(8,128)(2,1)S(1)}, bf16[64,16,128]{2,1,0:T(8,128)(2,1)}, u32[]{:S(2)}) copy-start(bf16[64,16,128]{2,1,0:T(8,128)(2,1)} %get-tuple-element.162) | copy-start | bytes 786436
  38.4 26.6 %copy-start.3 = (bf16[64,16,128]{2,1,0:T(8,128)(2,1)S(1)}, bf16[64,16,128]{2,1,0:T(8,128)(2,1)}, u32[]{:S(2)}) copy-start(bf16[64,16,128]{2,1,0:T(8,128)(2,1)} %get-tuple-element.168.refs_0_) | copy-start | bytes 786436
  38.5 26.6 %copy-start.5 = (f32[48,32,128]{2,1,0:T(8,128)S(1)}, f32[48,32,128]{2,1,0:T(8,128)}, u32[]{:S(2)}) copy-start(f32[48,32,128]{2,1,0:T(8,128)} %get-tuple-element.346) | copy-start | bytes 2359300
  38.5 26.6 %copy-start.6 = (bf16[2,32,16,128]{3,2,1,0:T(8,128)(2,1)S(1)}, bf16[2,32,16,128]{3,2,1,0:T(8,128)(2,1)}, u32[]{:S(2)}) copy-start(bf16[2,32,16,128]{3,2,1,0:T(8,128)(2,1)} %get-tuple-element.349) | copy-start | bytes 786436
  38.5 41.9 %collective-permute-start.10 = (bf16[64,16,128]{2,1,0:T(8,128)(2,1)}, bf16[64,16,128]{2,1,0:T(8,128)(2,1)S(1)}, u32[]{:S(2)}, u32[]{:S(2)}) collective-permute-start(bf16[64,16,128]{2,1,0:T(8,128)(2,1)} %get-tuple-element.132), channel_id=1, source_target_pairs={{0,8},{4,12},{8,0},{12,4},{1,9},{5,13},{9,1},{13,5},{2,10},{6,14},... | collective-permute-start | bytes 786440 | tf_op jit(solution)/shard_map/ppermute | solution.py:403
  43.7 36.7 %collective-permute-start.11 = (bf16[64,16,128]{2,1,0:T(8,128)(2,1)}, bf16[64,16,128]{2,1,0:T(8,128)(2,1)S(1)}, u32[]{:S(2)}, u32[]{:S(2)}) collective-permute-start(bf16[64,16,128]{2,1,0:T(8,128)(2,1)} %get-tuple-element.133), channel_id=1, source_target_pairs={{0,12},{4,0},{8,4},{12,8},{1,13},{5,1},{9,5},{13,9},{2,14},{6,2},{... | collective-permute-start | bytes 786440 | tf_op jit(solution)/shard_map/ppermute | solution.py:403
  52.9 27.6 %collective-permute-start.9 = (bf16[64,16,128]{2,1,0:T(8,128)(2,1)S(1)}, bf16[64,16,128]{2,1,0:T(8,128)(2,1)S(1)}, u32[]{:S(2)}, u32[]{:S(2)}) collective-permute-start(bf16[64,16,128]{2,1,0:T(8,128)(2,1)S(1)} %copy-done.11), channel_id=1, source_target_pairs={{0,4},{4,8},{8,12},{12,0},{1,5},{5,9},{9,13},{13,1},{2,6},{6,10},{... | collective-permute-start | bytes 786440 | tf_op jit(solution)/shard_map/ppermute | solution.py:403
  55.6 24.7 %copy-start.8 = (bf16[64,16,128]{2,1,0:T(8,128)(2,1)S(1)}, bf16[64,16,128]{2,1,0:T(8,128)(2,1)}, u32[]{:S(2)}) copy-start(bf16[64,16,128]{2,1,0:T(8,128)(2,1)} %get-tuple-element.163) | copy-start | bytes 786436
  55.7 24.8 %copy-start.16 = (bf16[32,16,128]{2,1,0:T(8,128)(2,1)S(1)}, bf16[32,16,128]{2,1,0:T(8,128)(2,1)}, u32[]{:S(2)}) copy-start(bf16[32,16,128]{2,1,0:T(8,128)(2,1)} %get-tuple-element.139) | copy-start | bytes 393220
  55.7 33.1 %copy-start.15 = (bf16[32,16,128]{2,1,0:T(8,128)(2,1)S(1)}, bf16[32,16,128]{2,1,0:T(8,128)(2,1)}, u32[]{:S(2)}) copy-start(bf16[32,16,128]{2,1,0:T(8,128)(2,1)} %get-tuple-element.140) | copy-start | bytes 393220
  55.7 33.1 %copy-start.2 = (bf16[64,16,128]{2,1,0:T(8,128)(2,1)S(1)}, bf16[64,16,128]{2,1,0:T(8,128)(2,1)}, u32[]{:S(2)}) copy-start(bf16[64,16,128]{2,1,0:T(8,128)(2,1)} %get-tuple-element.164.refs_0_) | copy-start | bytes 786436
  55.7 46.9 %collective-permute-start.18 = (bf16[64,16,128]{2,1,0:T(8,128)(2,1)S(1)}, bf16[64,16,128]{2,1,0:T(8,128)(2,1)S(1)}, u32[]{:S(2)}, u32[]{:S(2)}) collective-permute-start(bf16[64,16,128]{2,1,0:T(8,128)(2,1)S(1)} %copy-done.10), channel_id=1, source_target_pairs={{0,4},{4,8},{8,12},{12,0},{1,5},{5,9},{9,13},{13,1},{2,6},{6,10},{... | collective-permute-start | bytes 786440 | tf_op jit(solution)/shard_map/ppermute | solution.py:403
  61.7 41.0 %collective-permute-start.19 = (bf16[64,16,128]{2,1,0:T(8,128)(2,1)S(1)}, bf16[64,16,128]{2,1,0:T(8,128)(2,1)S(1)}, u32[]{:S(2)}, u32[]{:S(2)}) collective-permute-start(bf16[64,16,128]{2,1,0:T(8,128)(2,1)S(1)} %copy-done.9), channel_id=1, source_target_pairs={{0,8},{4,12},{8,0},{12,4},{1,9},{5,13},{9,1},{13,5},{2,10},{6,14},... | collective-permute-start | bytes 786440 | tf_op jit(solution)/shard_map/ppermute | solution.py:403
  80.4 22.3 %collective-permute-start.20 = (bf16[64,16,128]{2,1,0:T(8,128)(2,1)S(1)}, bf16[64,16,128]{2,1,0:T(8,128)(2,1)S(1)}, u32[]{:S(2)}, u32[]{:S(2)}) collective-permute-start(bf16[64,16,128]{2,1,0:T(8,128)(2,1)S(1)} %copy-done.8), channel_id=1, source_target_pairs={{0,12},{4,0},{8,4},{12,8},{1,13},{5,1},{9,5},{13,9},{2,14},{6,2},{... | collective-permute-start | bytes 786440 | tf_op jit(solution)/shard_map/ppermute | solution.py:403
  80.5 22.1 %copy-start.14 = (bf16[32,16,128]{2,1,0:T(8,128)(2,1)S(1)}, bf16[32,16,128]{2,1,0:T(8,128)(2,1)}, u32[]{:S(2)}) copy-start(bf16[32,16,128]{2,1,0:T(8,128)(2,1)} %get-tuple-element.141) | copy-start | bytes 393220
  80.5 22.2 %copy-start.1 = (bf16[64,16,128]{2,1,0:T(8,128)(2,1)S(1)}, bf16[64,16,128]{2,1,0:T(8,128)(2,1)}, u32[]{:S(2)}) copy-start(bf16[64,16,128]{2,1,0:T(8,128)(2,1)} %get-tuple-element.160.refs_0_) | copy-start | bytes 786436
  80.5 35.1 %collective-permute-start.12 = (bf16[32,16,128]{2,1,0:T(8,128)(2,1)S(1)}, bf16[32,16,128]{2,1,0:T(8,128)(2,1)S(1)}, u32[]{:S(2)}, u32[]{:S(2)}) collective-permute-start(bf16[32,16,128]{2,1,0:T(8,128)(2,1)S(1)} %copy-done.16), channel_id=1, source_target_pairs={{0,4},{4,8},{8,12},{12,0},{1,5},{5,9},{9,13},{13,1},{2,6},{6,10},{... | collective-permute-start | bytes 393224 | tf_op jit(solution)/shard_map/ppermute | solution.py:403
  88.8 26.8 %collective-permute-start.13 = (bf16[32,16,128]{2,1,0:T(8,128)(2,1)S(1)}, bf16[32,16,128]{2,1,0:T(8,128)(2,1)S(1)}, u32[]{:S(2)}, u32[]{:S(2)}) collective-permute-start(bf16[32,16,128]{2,1,0:T(8,128)(2,1)S(1)} %copy-done.15), channel_id=1, source_target_pairs={{0,8},{4,12},{8,0},{12,4},{1,9},{5,13},{9,1},{13,5},{2,10},{6,14},... | collective-permute-start | bytes 393224 | tf_op jit(solution)/shard_map/ppermute | solution.py:403
  88.8 26.8 %slice-start = ((s8[6291456]{0:T(1024)(128)(4,1)}), s8[4194304]{0:T(1024)(128)(4,1)S(1)}, s32[]{:S(2)}) async-start(s8[6291456]{0:T(1024)(128)(4,1)} %bitcast.49), calls=%async_computation | async-start | bytes 8388608
  102.5 13.1 %copy-start.4 = (bf16[32,16,128]{2,1,0:T(8,128)(2,1)S(1)}, bf16[32,16,128]{2,1,0:T(8,128)(2,1)}, u32[]{:S(2)}) copy-start(bf16[32,16,128]{2,1,0:T(8,128)(2,1)} %get-tuple-element.138.refs_0_) | copy-start | bytes 393220
  102.6 13.1 %slice-start.1 = ((s8[6291456]{0:T(1024)(128)(4,1)}), s8[2097152]{0:T(1024)(128)(4,1)S(1)}, s32[]{:S(2)}) async-start(s8[6291456]{0:T(1024)(128)(4,1)} %bitcast.49), calls=%async_computation.1 | async-start | bytes 4194304
  102.6 13.0 %collective-permute-start.14 = (bf16[32,16,128]{2,1,0:T(8,128)(2,1)S(1)}, bf16[32,16,128]{2,1,0:T(8,128)(2,1)S(1)}, u32[]{:S(2)}, u32[]{:S(2)}) collective-permute-start(bf16[32,16,128]{2,1,0:T(8,128)(2,1)S(1)} %copy-done.14), channel_id=1, source_target_pairs={{0,12},{4,0},{8,4},{12,8},{1,13},{5,1},{9,5},{13,9},{2,14},{6,2},{... | collective-permute-start | bytes 393224 | tf_op jit(solution)/shard_map/ppermute | solution.py:403
  120.0 2.4 %collective-permute-start.22 = (bf16[12,256,128]{2,1,0:T(8,128)(2,1)S(1)}, bf16[12,256,128]{2,1,0:T(8,128)(2,1)S(1)}, u32[]{:S(2)}, u32[]{:S(2)}) collective-permute-start(bf16[12,256,128]{2,1,0:T(8,128)(2,1)S(1)} %get-tuple-element.196), channel_id=1, source_target_pairs={{0,1},{1,0},{2,3},{3,2},{4,5},{5,4},{6,7},{7,6},{8,9},{9,8},{10,11... | collective-permute-start | bytes 2359304 | tf_op jit(solution)/shard_map/ppermute | solution.py:370
  120.0 3.7 %collective-permute-start.21 = (bf16[12,256,128]{2,1,0:T(8,128)(2,1)S(1)}, bf16[12,256,128]{2,1,0:T(8,128)(2,1)S(1)}, u32[]{:S(2)}, u32[]{:S(2)}) collective-permute-start(bf16[12,256,128]{2,1,0:T(8,128)(2,1)S(1)} %get-tuple-element.197), channel_id=1, source_target_pairs={{0,1},{1,0},{2,3},{3,2},{4,5},{5,4},{6,7},{7,6},{8,9},{9,8},{10,11... | collective-permute-start | bytes 2359304 | tf_op jit(solution)/shard_map/ppermute | solution.py:370
  122.5 19.6 %collective-permute-start.23 = (bf16[12,256,128]{2,1,0:T(8,128)(2,1)S(1)}, bf16[12,256,128]{2,1,0:T(8,128)(2,1)S(1)}, u32[]{:S(2)}, u32[]{:S(2)}) collective-permute-start(bf16[12,256,128]{2,1,0:T(8,128)(2,1)S(1)} %fusion), channel_id=1, source_target_pairs={{0,2},{1,3},{2,0},{3,1},{4,6},{5,7},{6,4},{7,5},{8,10},{9,11},{10,... | collective-permute-start | bytes 2359304 | tf_op jit(solution)/shard_map/ppermute | solution.py:370

commit v3 on v2

--- a/solution.py
+++ b/solution.py
@@ -7,12 +7,17 @@
 from jax.experimental.pallas import tpu as pltpu
 from jax.sharding import PartitionSpec as P
 
-ROWS_G = 16
+ROWS_G = 8
+PACKED = 16
 VMEM = pltpu.VMEM
 SMEM = pltpu.SMEM
 ANY = pl.ANY
 BF16 = jnp.bfloat16
-INFO = 6
+INFO = 8
+CHUNKS = (2, 6, 7, 7, 5, 4)
+TURN = 4
+AT_ONCE = 4
+DIGIT = 256
 PACK_MIB = 56
 
 
@@ -49,11 +54,10 @@
     sizes, unit, me_ref, owner_ref, count_ref, block_ref, row_ref, grads_hbm, values_hbm, *rest
 ):
     number = len(sizes)
-    slots, lanes = rest[-3].shape[0], rest[-3].shape[2]
-    outs, infos = rest[: number * slots], rest[number * slots : (number + 1) * slots]
-    scratch, values, heads, grads, info, cursor, sem = rest[(number + 1) * slots :]
-    tiles, tile = values.shape[0], values.shape[1]
-    per_tile = tile // ROWS_G
+    slots, lanes = rest[-4].shape[0], rest[-4].shape[2]
+    outs = rest[: number * slots]
+    scratch, values, heads, grads, info, lines, cursor, sem = rest[number * slots :]
+    tiles, per_tile, _, tile = values.shape
     k_out, row_blocks = grads.shape[0], grads.shape[1] // tile
     parts = 4 if tiles % 4 == 0 else 1
     span = tiles // parts
@@ -83,7 +87,7 @@
             end = at + shifted(count + (ROWS_G * tile - 1), ROWS_G * tile)
             cursor[0, d] = end
             cursor[1, d] = n + 1
-            scratch[d, pl.ds(at, per_tile)] = values[t].reshape(per_tile, ROWS_G, tile)
+            scratch[d, pl.ds(at, per_tile)] = values[t]
             info[d, 0, n] = at
             info[d, 1, n] = count
             info[d, 2, n] = block_ref[t]
@@ -101,39 +105,57 @@
     for d in range(slots):
         info[d, 4, lanes - 2] = cursor[1, d]
         info[d, 4, lanes - 1] = most
+    listed = pltpu.make_async_copy(info, lines, sem.at[parts + 1])
+    listed.start()
     loads[parts].wait()
-    lines = [grads[:, b * tile : (b + 1) * tile] for b in range(row_blocks)]
-    heads[...] = jnp.concatenate(lines, axis=0).reshape(heads.shape)
+    stack = [grads[:, b * tile : (b + 1) * tile] for b in range(row_blocks)]
+    listed.wait()
+    for d in range(slots):
+        for b in range(row_blocks):
+            heads[d, b] = stack[b]
+        heads[d, row_blocks] = as_bf16(shifted(lines[d], DIGIT))
+        heads[d, row_blocks + 1] = as_bf16(lines[d] & (DIGIT - 1))
     copies = []
-    start, at = 0, parts + 1
+    start, at = 0, parts + 2
     for c, size in enumerate(sizes):
-        skip = heads.shape[0] if c == 0 else 0
+        skip = heads.shape[1] if c == 0 else 0
         for d in range(slots):
             out = outs[c * slots + d]
             pairs = [(scratch.at[d, pl.ds(start, size)], out.at[pl.ds(skip, size)])]
             if skip:
-                pairs += [(heads, out.at[pl.ds(0, skip)]), (info.at[d], infos[d])]
+                pairs += [(heads.at[d], out.at[pl.ds(0, skip)])]
             for source, target in pairs:
                 copies.append(pltpu.make_async_copy(source, target, sem.at[at]))
                 at += 1
         start += size
-    for copy in copies:
+    always, rare = copies[:-slots], copies[-slots:]
+    for copy in always:
         copy.start()
-    for copy in copies:
+
+    @pl.when(most > start - sizes[-1])
+    def _():
+        for copy in rare:
+            copy.start()
+        for copy in rare:
+            copy.wait()
+
+    for copy in always:
         copy.wait()
 
 
 def pack(me, owner, count, block, row, grads, values, sizes, unit, slots):
     tiles, tile = values.shape[0], values.shape[1]
+    values = values.reshape(tiles, tile // ROWS_G, ROWS_G, tile)
     room = sum(sizes)
     lanes = 128
     assert max(2, 2 * tiles // slots) < lanes - 3 and room // unit < lanes - 3
-    head = grads.size // (ROWS_G * tile)
+    assert lanes == tile and INFO == ROWS_G == grads.shape[0]
+    head = grads.size // (ROWS_G * tile) + 2
     shapes = [
         jax.ShapeDtypeStruct((size + (head if number == 0 else 0), ROWS_G, tile), BF16)
         for number, size in enumerate(sizes)
         for _ in range(slots)
-    ] + [jax.ShapeDtypeStruct((INFO, lanes), jnp.int32)] * slots
+    ]
     outs = pl.pallas_call(
         functools.partial(pack_kernel, sizes, unit),
         out_shape=shapes,
@@ -142,17 +164,18 @@
         scratch_shapes=[
             VMEM((slots, room, ROWS_G, tile), BF16),
             VMEM(values.shape, BF16),
-            VMEM((head, ROWS_G, tile), BF16),
+            VMEM((slots, head, ROWS_G, tile), BF16),
             VMEM(grads.shape, BF16),
             SMEM((slots, INFO, lanes), jnp.int32),
+            VMEM((slots, INFO, lanes), jnp.int32),
             SMEM((2, slots), jnp.int32),
-            pltpu.SemaphoreType.DMA((5 + (len(sizes) + 2) * slots,)),
+            pltpu.SemaphoreType.DMA((6 + (len(sizes) + 1) * slots,)),
         ],
         compiler_params=params(PACK_MIB),
         cost_estimate=cost(0, 8),
     )(me, owner, count, block, row, grads, values)
     pieces = [list(outs[i * slots : (i + 1) * slots]) for i in range(len(sizes))]
-    return pieces, list(outs[-slots:]), head
+    return pieces, head
 
 
 def hist_kernel(kind, skip, senders, unit, row_blocks, which_ref, info_ref, *refs):
@@ -165,9 +188,9 @@
     if not first:
         before_ref, refs = refs[0], refs[1:]
     if last:
-        more_ref, out_ref, hist_ref, got, sem, extra = refs
+        more_ref, out_ref, hist_ref, got, list_ref, sem, extra = refs
     else:
-        hist_ref, got, sem = refs
+        hist_ref, got, list_ref, sem = refs
     length, tile = got_refs[0].shape[0] - skip, got_refs[0].shape[2]
     per_tile = tile // ROWS_G
     blocks, levels = cuts_ref.shape[:2]
@@ -183,6 +206,19 @@
     ]
     for copy in copies:
         copy.start()
+    found = jnp.int32(0)
+    for s in range(senders):
+        tiles = info_ref[s, 4, lanes - 2]
+        begin = jnp.minimum(info_ref[s, 4, shifted(low, unit)], tiles)
+        end = jnp.minimum(info_ref[s, 5, shifted(low + length, unit)], tiles)
+
+        def put(i, at, s=s):
+            list_ref[at] = s * lanes + i
+            return at + 1
+
+        found = lax.fori_loop(begin, end, put, found)
+    for i in range(AT_ONCE - 1):
+        list_ref[found + i] = -1
 
     def clear(b, carry):
         hist_ref[b] = jnp.zeros(hist_ref.shape[1:], jnp.float32)
@@ -205,56 +241,57 @@
     one, zero = jnp.ones((tile, tile), BF16), jnp.zeros((tile, tile), BF16)
     per = ROWS_G * tile
 
-    def load(s, i, end):
-        at, block = info_ref[s, 0, i], info_ref[s, 2, i]
-        count = jnp.where(i < end, info_ref[s, 1, i], 0)
-        count = jnp.minimum(count, (low + length - at) * per)
-        start = per_tile + s * length + at - low
+    def entry(p):
+        e = list_ref[p]
+        s, i, real = e >> log2(lanes), e & (lanes - 1), e >= 0
+        at = jnp.where(real, info_ref[s & (senders - 1), 0, i], low)
+        block = jnp.where(real, info_ref[s & (senders - 1), 2, i], 0)
+        count = jnp.where(real, info_ref[s & (senders - 1), 1, i], 0)
+        line = jnp.where(real, s * row_blocks + info_ref[s & (senders - 1), 3, i], 0)
+        start = per_tile + jnp.where(real, s, 0) * length + at - low
+        return start, block, jnp.minimum(count, (low + length - at) * per), (low - at) * ROWS_G, line
+
+    def load(p):
+        start, block, count, above, line = entry(p)
         values = got[pl.ds(start, per_tile)].reshape(tile, tile)
         whole = as_bf16(shifted(count, tile))
         part = as_bf16(count & (tile - 1))
-        above = as_bf16((low - at) * ROWS_G)
-        live = ((row < whole) | ((row == whole) & (lane < part))) & (row >= above)
+        live = ((row < whole) | ((row == whole) & (lane < part))) & (row >= as_bf16(above))
         values = jnp.where(live, values, jnp.full_like(values, -1000.0))
-        return block, values, s * row_blocks + info_ref[s, 3, i]
-
-    def sender(s, carry):
-        tiles = info_ref[s, 4, lanes - 2]
-        begin = jnp.minimum(info_ref[s, 4, shifted(low, unit)], tiles)
-        end = jnp.minimum(info_ref[s, 5, shifted(low + length, unit)], tiles)
-
-        def pair(p, carry):
-            i = begin + 2 * p
-            block_a, va, line_a = load(s, i, end)
-            block_b, vb, line_b = load(s, jnp.minimum(i + 1, end - 1), jnp.where(i + 1 < end, end, 0))
-            left = jnp.concatenate([grads_ref[0, line_a], grads_ref[1, line_b]], axis=1)
-            for c in range(0, levels, 2):
-                columns = []
-                for d in (c, c + 1):
-                    cut_a = jnp.broadcast_to(cuts_ref[block_a, d : d + 1], (tile, tile))
-                    cut_b = jnp.broadcast_to(cuts_ref[block_b, d : d + 1], (tile, tile))
-                    columns.append(
-                        jnp.concatenate(
-                            [
-                                jnp.where(va > cut_a.astype(BF16), one, zero),
-                                jnp.where(vb > cut_b.astype(BF16), one, zero),
-                            ],
-                            axis=0,
-                        )
+        return block, values, line
+
+    def pair(p):
+        block_a, va, line_a = load(p)
+        block_b, vb, line_b = load(p + 1)
+        left = jnp.concatenate([grads_ref[0, line_a], grads_ref[1, line_b]], axis=1)
+        for c in range(0, levels, 2):
+            columns = []
+            for d in (c, c + 1):
+                cut_a = jnp.broadcast_to(cuts_ref[block_a, d : d + 1], (tile, tile))
+                cut_b = jnp.broadcast_to(cuts_ref[block_b, d : d + 1], (tile, tile))
+                columns.append(
+                    jnp.concatenate(
+                        [
+                            jnp.where(va > cut_a.astype(BF16), one, zero),
+                            jnp.where(vb > cut_b.astype(BF16), one, zero),
+                        ],
+                        axis=0,
                     )
-                sums = jnp.dot(
-                    left, jnp.concatenate(columns, axis=1), preferred_element_type=jnp.float32
                 )
-                hist_ref[block_a, c] += sums[:k_out, :tile]
-                hist_ref[block_a, c + 1] += sums[:k_out, tile:]
-                hist_ref[block_b, c] += sums[k_out:, :tile]
-                hist_ref[block_b, c + 1] += sums[k_out:, tile:]
-            return carry
-
-        lax.fori_loop(0, shifted(jnp.maximum(end - begin, 0) + 1, 2), pair, 0)
+            sums = jnp.dot(
+                left, jnp.concatenate(columns, axis=1), preferred_element_type=jnp.float32
+            )
+            hist_ref[block_a, c] += sums[:k_out, :tile]
+            hist_ref[block_a, c + 1] += sums[:k_out, tile:]
+            hist_ref[block_b, c] += sums[k_out:, :tile]
+            hist_ref[block_b, c + 1] += sums[k_out:, tile:]
+
+    def group(i, carry):
+        for j in range(0, AT_ONCE, 2):
+            pair(AT_ONCE * i + j)
         return carry
 
-    lax.fori_loop(0, senders, sender, 0)
+    lax.fori_loop(0, (found + AT_ONCE - 1) >> log2(AT_ONCE), group, 0)
     if not last:
         return
 
@@ -311,6 +348,7 @@
         out_specs=[spec(VMEM)] * len(outs),
         scratch_shapes=[
             VMEM((senders * length + 2 * (tile // ROWS_G), ROWS_G, tile), BF16),
+            SMEM((senders * (length + 1) + AT_ONCE,), jnp.int32),
             pltpu.SemaphoreType.DMA((senders + 1,)),
         ]
         + ([VMEM(whole.shape[1:], jnp.float32)] if last else []),
@@ -383,13 +421,17 @@
     fb_dev = cut_index.shape[1] // tile
     per_tile = tile // ROWS_G
     capacity = max(2, 2 * tile_dev // owners) * per_tile
-    static = [capacity // 12 * i for i in (1, 2, 2, 2, 1)]
-    turn = max(per_tile, capacity // 12)
+    unit = per_tile
+    units = capacity // unit
+    static = [max(1, units * i // 48) * unit for i in CHUNKS]
+    while sum(static) >= capacity:
+        static.pop()
+    turn = min(TURN, capacity // per_tile // 12 + 1) * unit
     left = -(-(capacity - sum(static)) // turn) * turn
     me = lax.axis_index("feat").astype(jnp.int32)
-    sent, infos, skip = pack(
+    sent, skip = pack(
         me[None], tile_owner[:, 0], tile_count, tile_block, tile_row, gradients, tile_values,
-        static + [left], turn, owners,
+        static + [left], unit, owners,
     )
 
     n = 2 * cut_index + (1 - 10 * (levels - 1))
@@ -405,7 +447,6 @@
         ]
         return [pieces[0]] + moved
 
-    info = jnp.stack(exchange(infos), axis=0)
     got = []
     for number in range(len(static)):
         pieces = sent[number]
@@ -413,8 +454,10 @@
             got[number - 2], pieces = lax.optimization_barrier((got[number - 2], pieces))
         got.append(exchange(pieces))
 
-    grads = jnp.stack([x[:skip] for x in got[0]], axis=0)
-    grads = grads.reshape(owners * row_blocks, k_out, tile)
+    heads = jnp.stack([x[:skip] for x in got[0]], axis=0)
+    digits = heads[:, skip - 2 :].astype(jnp.int32)
+    info = digits[:, 0] * DIGIT + digits[:, 1]
+    grads = heads[:, : skip - 2].reshape(owners * row_blocks, k_out, tile)
     nothing = jnp.zeros_like(grads)
     grads = jnp.stack(
         [jnp.concatenate([grads, nothing], axis=1), jnp.concatenate([nothing, grads], axis=1)],
@@ -442,7 +485,7 @@
             grads,
             cuts,
             0,
-            turn,
+            unit,
         )
         return r + 1, hist
 
@@ -453,7 +496,7 @@
     for number, size in enumerate(static):
         last = {"slots": row_groups, "more": extra} if number == len(static) - 1 else {}
         hist = add_tiles(
-            hist, which(low), info, got[number], grads, cuts, 0 if number else skip, turn, **last
+            hist, which(low), info, got[number], grads, cuts, 0 if number else skip, unit, **last
         )
         low += size
     return reduce_rows(hist, k_out, "rows")

time: 143 us -> 137 us (0.958)
  the two profiles are of different devices: /device:TPU:0 before, /device:TPU:8 now
where the time goes in v3:
time: 137 us
  Pallas kernels  63.7 us (46%)
  waiting for transfers between devices  47.8 us (35%)
  starting transfers between devices  22.3 us (16%)
  other arithmetic  1.79 us (1%)
    pallas_call x6, Pallas kernels, add_tiles(): pl.pallas_call(functools.partial(hist_kernel, (first, last), skip, sender...  54.7 us
    ppermute x18, waiting for transfers between devices, exchange(): lax.ppermute(pieces[d], 'feat', [(i, (i + d) % owners) for i in range(own...  28.2 us
    ppermute x3, waiting for transfers between devices, reduce_rows(): moved = lax.ppermute(value, axis, [(i, i ^ bit) for i in range(n)])  19.6 us
    ppermute x18, starting transfers between devices, exchange(): lax.ppermute(pieces[d], 'feat', [(i, (i + d) % owners) for i in range(own...  19.4 us
    pallas_call x1, Pallas kernels, pack(): pl.pallas_call(functools.partial(pack_kernel, sizes, unit), out_shape=sha...  7.32 us
    ppermute x3, starting transfers between devices, reduce_rows(): moved = lax.ppermute(value, axis, [(i, i ^ bit) for i in range(n)])  2.9 us
  transfers between devices with their start and end apart: 21, of which 8 were waited for; matrix products, arithmetic and copies ran while one was open for 1% of the time, Pallas kernels for 37%

profile of v3, /device:TPU:8, one launch (start us, length us, event | category | flops | bytes accessed | tf_op | source)
XLA Modules:
  0.0 137.2 jit_solution(4606099581059497529)
XLA Ops:
  0.0 7.3 %shard_map.73 = (bf16[42,8,128]{2,1,0:T(8,128)(2,1)}, bf16[42,8,128]{2,1,0:T(8,128)(2,1)}, bf16[42,8,128]{2,1,0:T(8,128)(2,1)}, bf16[42,8,128]{2,1,0:T(8,128)(2,...) custom-call(s32[1]{0:T(128)} %bitcast.4.me_ref, ...), custom_call_target="tpu_custom_call" | custom-call | bytes 8388608 | tf_op jit(solution)/shard_map/pallas_call | solution.py:159
  7.3 1.6 %collective-permute-start.3 = (bf16[42,8,128]{2,1,0:T(8,128)(2,1)}, bf16[42,8,128]{2,1,0:T(8,128)(2,1)S(1)}, u32[]{:S(2)}, u32[]{:S(2)}) collective-permute-start(bf16[42,8,128]{2,1,0:T(8,128)(2,1)} %get-tuple-element.127), channel_id=1, source_target_pairs={{0,4},{4,8},{8,12},{12,0},{1,5},{5,9},{9,13},{13,1},{2,6},{6,10},{... | collective-permute-start | bytes 258056 | tf_op jit(solution)/shard_map/ppermute | solution.py:445
  9.0 1.1 collective-permute-start.4
  10.1 1.9 %collective-permute-start.5 = (bf16[42,8,128]{2,1,0:T(8,128)(2,1)}, bf16[42,8,128]{2,1,0:T(8,128)(2,1)S(1)}, u32[]{:S(2)}, u32[]{:S(2)}) collective-permute-start(bf16[42,8,128]{2,1,0:T(8,128)(2,1)} %get-tuple-element.129), channel_id=1, source_target_pairs={{0,12},{4,0},{8,4},{12,8},{1,13},{5,1},{9,5},{13,9},{2,14},{6,2},{... | collective-permute-start | bytes 258056 | tf_op jit(solution)/shard_map/ppermute | solution.py:445
  12.0 0.1 collective-permute-start.6
  12.1 0.3 convert_multiply_fusion
  12.4 0.1 bitcast_bitcast_fusion.refs_5_
  12.5 3.7 %collective-permute-start.7 = (bf16[96,8,128]{2,1,0:T(8,128)(2,1)}, bf16[96,8,128]{2,1,0:T(8,128)(2,1)S(1)}, u32[]{:S(2)}, u32[]{:S(2)}) collective-permute-start(bf16[96,8,128]{2,1,0:T(8,128)(2,1)} %get-tuple-element.140), channel_id=1, source_target_pairs={{0,8},{4,12},{8,0},{12,4},{1,9},{5,13},{9,1},{13,5},{2,10},{6,14},... | collective-permute-start | bytes 589832 | tf_op jit(solution)/shard_map/ppermute | solution.py:445
  16.2 0.0 collective-permute-done.3.refs_1_
  16.2 1.6 %collective-permute-done.4.refs_2_ = bf16[42,8,128]{2,1,0:T(8,128)(2,1)S(1)} collective-permute-done((bf16[42,8,128]{2,1,0:T(8,128)(2,1)}, bf16[42,8,128]{2,1,0:T(8,128)(2,1)S(1)}, u32[]{:S(2)}, u32[]{:S(2)}) %collective-permute-start.4) | collective-permute-done | bytes 86048 | tf_op jit(solution)/shard_map/ppermute | solution.py:445
  17.7 9.1 %collective-permute-done.5.refs_3_ = bf16[42,8,128]{2,1,0:T(8,128)(2,1)S(1)} collective-permute-done((bf16[42,8,128]{2,1,0:T(8,128)(2,1)}, bf16[42,8,128]{2,1,0:T(8,128)(2,1)S(1)}, u32[]{:S(2)}, u32[]{:S(2)}) %collective-permute-start.5) | collective-permute-done | bytes 86048 | tf_op jit(solution)/shard_map/ppermute | solution.py:445
  26.8 0.0 copy-done
  26.9 0.8 slice_reduce_fusion
  28.5 0.1 collective-permute-start.8
  28.6 0.1 pad_add_fusion.1.which_ref
  28.7 0.1 pad_add_fusion.2.which_ref
  28.8 2.0 %collective-permute-start.15 = (bf16[112,8,128]{2,1,0:T(8,128)(2,1)}, bf16[112,8,128]{2,1,0:T(8,128)(2,1)S(1)}, u32[]{:S(2)}, u32[]{:S(2)}) collective-permute-start(bf16[112,8,128]{2,1,0:T(8,128)(2,1)} %get-tuple-element.165), channel_id=1, source_target_pairs={{0,4},{4,8},{8,12},{12,0},{1,5},{5,9},{9,13},{13,1},{2,6},{6,10},{... | collective-permute-start | bytes 688136 | tf_op jit(solution)/shard_map/ppermute | solution.py:445
  30.8 0.0 collective-permute-start.16
  30.8 0.1 pad_add_fusion.3.which_ref
  30.9 0.1 pad_add_fusion.4.which_ref
  31.0 5.3 %shard_map.75.refs_6_ = f32[48,32,8,128]{3,2,1,0:T(8,128)S(1)} custom-call(s32[4]{0:T(128)S(1)} %pad_add_fusion.1.which_ref, s32[4,8,128]{2,1,0:T(8,128)S(1)} %get-tuple-element.369, bf16[42,8,128]{2,1,0:T(8,128)(2,1)S(1)} %copy-done, bf16[42,8,128]{2,1,0:T(8,128)(2,1)S(1)} %collective-permute-done.3.refs_1_, ...), custom_call_target="tpu_custom_call" | custom-call | flops 10000000000 | bytes 25165824 | tf_op jit(solution)/shard_map/pallas_call | solution.py:342
  36.3 0.1 pad_add_fusion.5.which_ref
  36.4 0.1 pad_add_fusion.6.which_ref
  36.4 0.0 collective-permute-done.6.refs_1_
  36.4 1.6 %collective-permute-start.17 = (bf16[112,8,128]{2,1,0:T(8,128)(2,1)S(1)}, bf16[112,8,128]{2,1,0:T(8,128)(2,1)S(1)}, u32[]{:S(2)}, u32[]{:S(2)}) collective-permute-start(bf16[112,8,128]{2,1,0:T(8,128)(2,1)S(1)} %copy-done.10), channel_id=1, source_target_pairs={{0,12},{4,0},{8,4},{12,8},{1,13},{5,1},{9,5},{13,9},{2,14},{6,2},{... | collective-permute-start | bytes 688136 | tf_op jit(solution)/shard_map/ppermute | solution.py:445
  38.0 0.0 collective-permute-done.7.refs_2_
  38.0 8.4 %collective-permute-done.8.refs_3_ = bf16[96,8,128]{2,1,0:T(8,128)(2,1)S(1)} collective-permute-done((bf16[96,8,128]{2,1,0:T(8,128)(2,1)}, bf16[96,8,128]{2,1,0:T(8,128)(2,1)S(1)}, u32[]{:S(2)}, u32[]{:S(2)}) %collective-permute-start.8) | collective-permute-done | bytes 196640 | tf_op jit(solution)/shard_map/ppermute | solution.py:445
  46.4 0.1 collective-permute-start.10
  46.5 1.1 collective-permute-start.11
  47.6 11.4 %shard_map.76.refs_6_ = f32[48,32,8,128]{3,2,1,0:T(8,128)S(1)} custom-call(s32[4]{0:T(128)S(1)} %pad_add_fusion.2.which_ref, s32[4,8,128]{2,1,0:T(8,128)S(1)} %get-tuple-element.369, bf16[96,8,128]{2,1,0:T(8,128)(2,1)S(1)} %copy-done.3, bf16[96,8,128]{2,1,0:T(8,128)(2,1)S(1)} %collective-permute-done.6.refs_1_, ...), custom_call_target="tpu_custom_call", output_to_operand_aliasing={{}: (8, {})} | custom-call | flops 10000000000 | bytes 25165824 | tf_op jit(solution)/shard_map/pallas_call | solution.py:342
  59.0 0.2 collective-permute-done.15.refs_1_
  59.2 2.4 %collective-permute-start.9 = (bf16[112,8,128]{2,1,0:T(8,128)(2,1)S(1)}, bf16[112,8,128]{2,1,0:T(8,128)(2,1)S(1)}, u32[]{:S(2)}, u32[]{:S(2)}) collective-permute-start(bf16[112,8,128]{2,1,0:T(8,128)(2,1)S(1)} %copy-done.7), channel_id=1, source_target_pairs={{0,4},{4,8},{8,12},{12,0},{1,5},{5,9},{9,13},{13,1},{2,6},{6,10},{... | collective-permute-start | bytes 688136 | tf_op jit(solution)/shard_map/ppermute | solution.py:445
  61.6 2.5 %collective-permute-done.16.refs_2_ = bf16[112,8,128]{2,1,0:T(8,128)(2,1)S(1)} collective-permute-done((bf16[112,8,128]{2,1,0:T(8,128)(2,1)S(1)}, bf16[112,8,128]{2,1,0:T(8,128)(2,1)S(1)}, u32[]{:S(2)}, u32[]{:S(2)}) %collective-permute-start.16) | collective-permute-done | bytes 229408 | tf_op jit(solution)/shard_map/ppermute | solution.py:445
  64.1 0.0 collective-permute-done.17.refs_3_
  64.1 0.1 collective-permute-start.18
  64.2 3.5 %collective-permute-start.19 = (bf16[80,8,128]{2,1,0:T(8,128)(2,1)S(1)}, bf16[80,8,128]{2,1,0:T(8,128)(2,1)S(1)}, u32[]{:S(2)}, u32[]{:S(2)}) collective-permute-start(bf16[80,8,128]{2,1,0:T(8,128)(2,1)S(1)} %copy-done.13), channel_id=1, source_target_pairs={{0,8},{4,12},{8,0},{12,4},{1,9},{5,13},{9,1},{13,5},{2,10},{6,14},... | collective-permute-start | bytes 491528 | tf_op jit(solution)/shard_map/ppermute | solution.py:445
  67.7 13.0 %shard_map.77.refs_6_ = f32[48,32,8,128]{3,2,1,0:T(8,128)S(1)} custom-call(s32[4]{0:T(128)S(1)} %pad_add_fusion.3.which_ref, s32[4,8,128]{2,1,0:T(8,128)S(1)} %get-tuple-element.369, bf16[112,8,128]{2,1,0:T(8,128)(2,1)S(1)} %copy-done.2, bf16[112,8,128]{2,1,0:T(8,128)(2,1)S(1)} %collective-permute-done.15.refs_1_, ...), custom_call_target="tpu_custom_call", output_to_operand_aliasing={{}: (8, {})} | custom-call | flops 10000000000 | bytes 25165824 | tf_op jit(solution)/shard_map/pallas_call | solution.py:342
  80.7 0.0 collective-permute-done.10.refs_2_
  80.7 0.1 collective-permute-start.20
  80.8 6.4 %collective-permute-done.11.refs_3_ = bf16[112,8,128]{2,1,0:T(8,128)(2,1)S(1)} collective-permute-done((bf16[112,8,128]{2,1,0:T(8,128)(2,1)S(1)}, bf16[112,8,128]{2,1,0:T(8,128)(2,1)S(1)}, u32[]{:S(2)}, u32[]{:S(2)}) %collective-permute-start.11) | collective-permute-done | bytes 229408 | tf_op jit(solution)/shard_map/ppermute | solution.py:445
  87.2 0.0 collective-permute-done.9.refs_1_
  87.2 0.1 collective-permute-start.12
  87.3 0.1 collective-permute-start.13
  87.4 0.0 slice-start
  87.4 14.5 %shard_map.78.refs_6_ = f32[48,32,8,128]{3,2,1,0:T(8,128)S(1)} custom-call(s32[4]{0:T(128)S(1)} %pad_add_fusion.4.which_ref, s32[4,8,128]{2,1,0:T(8,128)S(1)} %get-tuple-element.369, bf16[112,8,128]{2,1,0:T(8,128)(2,1)S(1)} %copy-done.1, bf16[112,8,128]{2,1,0:T(8,128)(2,1)S(1)} %collective-permute-done.9.refs_1_, ...), custom_call_target="tpu_custom_call", output_to_operand_aliasing={{}: (8, {})} | custom-call | flops 10000000000 | bytes 25165824 | tf_op jit(solution)/shard_map/pallas_call | solution.py:342
  101.9 0.0 slice-start.1
  101.9 0.0 collective-permute-done.18.refs_1_
  101.9 0.1 collective-permute-start.14
  102.0 0.0 collective-permute-done.19.refs_2_
  102.0 0.0 collective-permute-done.20.refs_3_
  102.0 6.9 %shard_map.79.refs_6_ = f32[48,32,8,128]{3,2,1,0:T(8,128)S(1)} custom-call(s32[4]{0:T(128)S(1)} %pad_add_fusion.5.which_ref, s32[4,8,128]{2,1,0:T(8,128)S(1)} %get-tuple-element.369, bf16[80,8,128]{2,1,0:T(8,128)(2,1)S(1)} %copy-done.4, bf16[80,8,128]{2,1,0:T(8,128)(2,1)S(1)} %collective-permute-done.18.refs_1_, ...), custom_call_target="tpu_custom_call", output_to_operand_aliasing={{}: (8, {})} | custom-call | flops 10000000000 | bytes 25165824 | tf_op jit(solution)/shard_map/pallas_call | solution.py:342
  108.9 0.0 collective-permute-done.12.refs_1_
  108.9 0.0 collective-permute-done.13.refs_2_
  108.9 0.0 collective-permute-done.14.refs_3_
  109.0 3.6 %shard_map.80 = (bf16[4,12,256,128]{3,2,1,0:T(8,128)(2,1)S(1)}, f32[48,32,8,128]{3,2,1,0:T(8,128)S(1)}) custom-call(s32[4]{0:T(128)S(1)} %pad_add_fusion.6.which_ref, s32[4,8,128]{2,1,0:T(8,128)S(1)} %get-tuple-element.369, bf16[64,8,128]{2,1,0:T(8,128)(2,1)S(1)} %copy-done.5, ...), custom_call_target="tpu_custom_call", output_to_operand_aliasing={{1}: (8, {})} | custom-call | flops 10000000000 | bytes 25165824 | tf_op jit(solution)/shard_map/pallas_call | solution.py:342
  112.6 0.2 slice_bitcast_fusion
  112.7 0.1 collective-permute-start.22
  112.8 0.5 collective-permute-start.21
  113.3 1.8 %collective-permute-done.22 = bf16[12,256,128]{2,1,0:T(8,128)(2,1)S(1)} collective-permute-done((bf16[12,256,128]{2,1,0:T(8,128)(2,1)S(1)}, bf16[12,256,128]{2,1,0:T(8,128)(2,1)S(1)}, u32[]{:S(2)}, u32[]{:S(2)}) %collective-permute-start.22) | collective-permute-done | bytes 786464 | tf_op jit(solution)/shard_map/ppermute | solution.py:408
  115.1 0.2 fusion
  115.3 2.3 %collective-permute-start.23 = (bf16[12,256,128]{2,1,0:T(8,128)(2,1)S(1)}, bf16[12,256,128]{2,1,0:T(8,128)(2,1)S(1)}, u32[]{:S(2)}, u32[]{:S(2)}) collective-permute-start(bf16[12,256,128]{2,1,0:T(8,128)(2,1)S(1)} %fusion), channel_id=1, source_target_pairs={{0,2},{1,3},{2,0},{3,1},{4,6},{5,7},{6,4},{7,5},{8,10},{9,11},{10,... | collective-permute-start | bytes 2359304 | tf_op jit(solution)/shard_map/ppermute | solution.py:408
  117.6 0.0 collective-permute-done.21.refs_1_
  117.6 17.8 %collective-permute-done.23.refs_2_ = bf16[12,256,128]{2,1,0:T(8,128)(2,1)S(1)} collective-permute-done((bf16[12,256,128]{2,1,0:T(8,128)(2,1)S(1)}, bf16[12,256,128]{2,1,0:T(8,128)(2,1)S(1)}, u32[]{:S(2)}, u32[]{:S(2)}) %collective-permute-start.23) | collective-permute-done | bytes 786464 | tf_op jit(solution)/shard_map/ppermute | solution.py:408
  135.5 1.7 %shard_map.81 = f32[8,32,1536]{2,1,0:T(8,128)} custom-call(bf16[12,256,128]{2,1,0:T(8,128)(2,1)S(1)} %get-tuple-element.214.refs_0_, bf16[12,256,128]{2,1,0:T(8,128)(2,1)S(1)} %collective-permute-done.21.refs_1_, bf16[12,256,128]{2,1,0:T(8,128)(2,1)S(1)} %collective-permute-done.23.refs_2_), custom_call_target="tpu_custom_call" | custom-call | tf_op jit(solution)/shard_map/pallas_call | solution.py:386
  (48 shorter events, 0.2 us)
Async XLA Ops:
  0.0 12.1 %copy-start.6 = (s32[31,6144]{1,0:T(8,128)S(1)}, s32[31,6144]{1,0:T(8,128)}, u32[]{:S(2)}) copy-start(s32[31,6144]{1,0:T(8,128)} %param.14) | copy-start | bytes 2285572
  7.3 19.5 %copy-start = (bf16[42,8,128]{2,1,0:T(8,128)(2,1)S(1)}, bf16[42,8,128]{2,1,0:T(8,128)(2,1)}, u32[]{:S(2)}) copy-start(bf16[42,8,128]{2,1,0:T(8,128)(2,1)} %get-tuple-element.134.refs_0_) | copy-start | bytes 258052
  7.3 8.8 %collective-permute-start.3 = (bf16[42,8,128]{2,1,0:T(8,128)(2,1)}, bf16[42,8,128]{2,1,0:T(8,128)(2,1)S(1)}, u32[]{:S(2)}, u32[]{:S(2)}) collective-permute-start(bf16[42,8,128]{2,1,0:T(8,128)(2,1)} %get-tuple-element.127), channel_id=1, source_target_pairs={{0,4},{4,8},{8,12},{12,0},{1,5},{5,9},{9,13},{13,1},{2,6},{6,10},{... | collective-permute-start | bytes 258056 | tf_op jit(solution)/shard_map/ppermute | solution.py:445
  9.0 8.8 %collective-permute-start.4 = (bf16[42,8,128]{2,1,0:T(8,128)(2,1)}, bf16[42,8,128]{2,1,0:T(8,128)(2,1)S(1)}, u32[]{:S(2)}, u32[]{:S(2)}) collective-permute-start(bf16[42,8,128]{2,1,0:T(8,128)(2,1)} %get-tuple-element.128), channel_id=1, source_target_pairs={{0,8},{4,12},{8,0},{12,4},{1,9},{5,13},{9,1},{13,5},{2,10},{6,14},... | collective-permute-start | bytes 258056 | tf_op jit(solution)/shard_map/ppermute | solution.py:445
  10.1 16.8 %collective-permute-start.5 = (bf16[42,8,128]{2,1,0:T(8,128)(2,1)}, bf16[42,8,128]{2,1,0:T(8,128)(2,1)S(1)}, u32[]{:S(2)}, u32[]{:S(2)}) collective-permute-start(bf16[42,8,128]{2,1,0:T(8,128)(2,1)} %get-tuple-element.129), channel_id=1, source_target_pairs={{0,12},{4,0},{8,4},{12,8},{1,13},{5,1},{9,5},{13,9},{2,14},{6,2},{... | collective-permute-start | bytes 258056 | tf_op jit(solution)/shard_map/ppermute | solution.py:445
  12.0 24.4 %collective-permute-start.6 = (bf16[96,8,128]{2,1,0:T(8,128)(2,1)}, bf16[96,8,128]{2,1,0:T(8,128)(2,1)S(1)}, u32[]{:S(2)}, u32[]{:S(2)}) collective-permute-start(bf16[96,8,128]{2,1,0:T(8,128)(2,1)} %get-tuple-element.139), channel_id=1, source_target_pairs={{0,4},{4,8},{8,12},{12,0},{1,5},{5,9},{9,13},{13,1},{2,6},{6,10},{... | collective-permute-start | bytes 589832 | tf_op jit(solution)/shard_map/ppermute | solution.py:445
  12.5 25.5 %collective-permute-start.7 = (bf16[96,8,128]{2,1,0:T(8,128)(2,1)}, bf16[96,8,128]{2,1,0:T(8,128)(2,1)S(1)}, u32[]{:S(2)}, u32[]{:S(2)}) collective-permute-start(bf16[96,8,128]{2,1,0:T(8,128)(2,1)} %get-tuple-element.140), channel_id=1, source_target_pairs={{0,8},{4,12},{8,0},{12,4},{1,9},{5,13},{9,1},{13,5},{2,10},{6,14},... | collective-permute-start | bytes 589832 | tf_op jit(solution)/shard_map/ppermute | solution.py:445
  28.5 2.3 %copy-start.11 = (bf16[112,8,128]{2,1,0:T(8,128)(2,1)S(1)}, bf16[112,8,128]{2,1,0:T(8,128)(2,1)}, u32[]{:S(2)}) copy-start(bf16[112,8,128]{2,1,0:T(8,128)(2,1)} %get-tuple-element.166) | copy-start | bytes 688132
  28.5 17.9 %collective-permute-start.8 = (bf16[96,8,128]{2,1,0:T(8,128)(2,1)}, bf16[96,8,128]{2,1,0:T(8,128)(2,1)S(1)}, u32[]{:S(2)}, u32[]{:S(2)}) collective-permute-start(bf16[96,8,128]{2,1,0:T(8,128)(2,1)} %get-tuple-element.141), channel_id=1, source_target_pairs={{0,12},{4,0},{8,4},{12,8},{1,13},{5,1},{9,5},{13,9},{2,14},{6,2},{... | collective-permute-start | bytes 589832 | tf_op jit(solution)/shard_map/ppermute | solution.py:445
  28.8 30.4 %collective-permute-start.15 = (bf16[112,8,128]{2,1,0:T(8,128)(2,1)}, bf16[112,8,128]{2,1,0:T(8,128)(2,1)S(1)}, u32[]{:S(2)}, u32[]{:S(2)}) collective-permute-start(bf16[112,8,128]{2,1,0:T(8,128)(2,1)} %get-tuple-element.165), channel_id=1, source_target_pairs={{0,4},{4,8},{8,12},{12,0},{1,5},{5,9},{9,13},{13,1},{2,6},{6,10},{... | collective-permute-start | bytes 688136 | tf_op jit(solution)/shard_map/ppermute | solution.py:445
  30.8 33.3 %collective-permute-start.16 = (bf16[112,8,128]{2,1,0:T(8,128)(2,1)S(1)}, bf16[112,8,128]{2,1,0:T(8,128)(2,1)S(1)}, u32[]{:S(2)}, u32[]{:S(2)}) collective-permute-start(bf16[112,8,128]{2,1,0:T(8,128)(2,1)S(1)} %copy-done.11), channel_id=1, source_target_pairs={{0,8},{4,12},{8,0},{12,4},{1,9},{5,13},{9,1},{13,5},{2,10},{6,14},... | collective-permute-start | bytes 688136 | tf_op jit(solution)/shard_map/ppermute | solution.py:445
  30.9 5.5 %copy-start.10 = (bf16[112,8,128]{2,1,0:T(8,128)(2,1)S(1)}, bf16[112,8,128]{2,1,0:T(8,128)(2,1)}, u32[]{:S(2)}) copy-start(bf16[112,8,128]{2,1,0:T(8,128)(2,1)} %get-tuple-element.167) | copy-start | bytes 688132
  30.9 15.5 %copy-start.9 = (bf16[112,8,128]{2,1,0:T(8,128)(2,1)S(1)}, bf16[112,8,128]{2,1,0:T(8,128)(2,1)}, u32[]{:S(2)}) copy-start(bf16[112,8,128]{2,1,0:T(8,128)(2,1)} %get-tuple-element.148) | copy-start | bytes 688132
  30.9 15.6 %copy-start.8 = (bf16[112,8,128]{2,1,0:T(8,128)(2,1)S(1)}, bf16[112,8,128]{2,1,0:T(8,128)(2,1)}, u32[]{:S(2)}) copy-start(bf16[112,8,128]{2,1,0:T(8,128)(2,1)} %get-tuple-element.149) | copy-start | bytes 688132
  30.9 16.7 %copy-start.3 = (bf16[96,8,128]{2,1,0:T(8,128)(2,1)S(1)}, bf16[96,8,128]{2,1,0:T(8,128)(2,1)}, u32[]{:S(2)}) copy-start(bf16[96,8,128]{2,1,0:T(8,128)(2,1)} %get-tuple-element.184.refs_0_) | copy-start | bytes 589828
  36.4 27.6 %collective-permute-start.17 = (bf16[112,8,128]{2,1,0:T(8,128)(2,1)S(1)}, bf16[112,8,128]{2,1,0:T(8,128)(2,1)S(1)}, u32[]{:S(2)}, u32[]{:S(2)}) collective-permute-start(bf16[112,8,128]{2,1,0:T(8,128)(2,1)S(1)} %copy-done.10), channel_id=1, source_target_pairs={{0,12},{4,0},{8,4},{12,8},{1,13},{5,1},{9,5},{13,9},{2,14},{6,2},{... | collective-permute-start | bytes 688136 | tf_op jit(solution)/shard_map/ppermute | solution.py:445
  46.4 12.8 %copy-start.7 = (bf16[112,8,128]{2,1,0:T(8,128)(2,1)S(1)}, bf16[112,8,128]{2,1,0:T(8,128)(2,1)}, u32[]{:S(2)}) copy-start(bf16[112,8,128]{2,1,0:T(8,128)(2,1)} %get-tuple-element.147) | copy-start | bytes 688132
  46.4 17.7 %copy-start.14 = (bf16[80,8,128]{2,1,0:T(8,128)(2,1)S(1)}, bf16[80,8,128]{2,1,0:T(8,128)(2,1)}, u32[]{:S(2)}) copy-start(bf16[80,8,128]{2,1,0:T(8,128)(2,1)} %get-tuple-element.173) | copy-start | bytes 491524
  46.4 17.7 %copy-start.13 = (bf16[80,8,128]{2,1,0:T(8,128)(2,1)S(1)}, bf16[80,8,128]{2,1,0:T(8,128)(2,1)}, u32[]{:S(2)}) copy-start(bf16[80,8,128]{2,1,0:T(8,128)(2,1)} %get-tuple-element.174) | copy-start | bytes 491524
  46.4 21.3 %copy-start.2 = (bf16[112,8,128]{2,1,0:T(8,128)(2,1)S(1)}, bf16[112,8,128]{2,1,0:T(8,128)(2,1)}, u32[]{:S(2)}) copy-start(bf16[112,8,128]{2,1,0:T(8,128)(2,1)} %get-tuple-element.180.refs_0_) | copy-start | bytes 688132
  46.4 34.3 %collective-permute-start.10 = (bf16[112,8,128]{2,1,0:T(8,128)(2,1)S(1)}, bf16[112,8,128]{2,1,0:T(8,128)(2,1)S(1)}, u32[]{:S(2)}, u32[]{:S(2)}) collective-permute-start(bf16[112,8,128]{2,1,0:T(8,128)(2,1)S(1)} %copy-done.9), channel_id=1, source_target_pairs={{0,8},{4,12},{8,0},{12,4},{1,9},{5,13},{9,1},{13,5},{2,10},{6,14},... | collective-permute-start | bytes 688136 | tf_op jit(solution)/shard_map/ppermute | solution.py:445
  46.5 40.7 %collective-permute-start.11 = (bf16[112,8,128]{2,1,0:T(8,128)(2,1)S(1)}, bf16[112,8,128]{2,1,0:T(8,128)(2,1)S(1)}, u32[]{:S(2)}, u32[]{:S(2)}) collective-permute-start(bf16[112,8,128]{2,1,0:T(8,128)(2,1)S(1)} %copy-done.8), channel_id=1, source_target_pairs={{0,12},{4,0},{8,4},{12,8},{1,13},{5,1},{9,5},{13,9},{2,14},{6,2},{... | collective-permute-start | bytes 688136 | tf_op jit(solution)/shard_map/ppermute | solution.py:445
  59.2 28.0 %collective-permute-start.9 = (bf16[112,8,128]{2,1,0:T(8,128)(2,1)S(1)}, bf16[112,8,128]{2,1,0:T(8,128)(2,1)S(1)}, u32[]{:S(2)}, u32[]{:S(2)}) collective-permute-start(bf16[112,8,128]{2,1,0:T(8,128)(2,1)S(1)} %copy-done.7), channel_id=1, source_target_pairs={{0,4},{4,8},{8,12},{12,0},{1,5},{5,9},{9,13},{13,1},{2,6},{6,10},{... | collective-permute-start | bytes 688136 | tf_op jit(solution)/shard_map/ppermute | solution.py:445
  64.1 16.6 %copy-start.12 = (bf16[80,8,128]{2,1,0:T(8,128)(2,1)S(1)}, bf16[80,8,128]{2,1,0:T(8,128)(2,1)}, u32[]{:S(2)}) copy-start(bf16[80,8,128]{2,1,0:T(8,128)(2,1)} %get-tuple-element.175) | copy-start | bytes 491524
  64.1 23.1 %copy-start.17 = (bf16[64,8,128]{2,1,0:T(8,128)(2,1)S(1)}, bf16[64,8,128]{2,1,0:T(8,128)(2,1)}, u32[]{:S(2)}) copy-start(bf16[64,8,128]{2,1,0:T(8,128)(2,1)} %get-tuple-element.155) | copy-start | bytes 393220
  64.1 23.2 %copy-start.16 = (bf16[64,8,128]{2,1,0:T(8,128)(2,1)S(1)}, bf16[64,8,128]{2,1,0:T(8,128)(2,1)}, u32[]{:S(2)}) copy-start(bf16[64,8,128]{2,1,0:T(8,128)(2,1)} %get-tuple-element.156) | copy-start | bytes 393220
  64.1 23.3 %copy-start.1 = (bf16[112,8,128]{2,1,0:T(8,128)(2,1)S(1)}, bf16[112,8,128]{2,1,0:T(8,128)(2,1)}, u32[]{:S(2)}) copy-start(bf16[112,8,128]{2,1,0:T(8,128)(2,1)} %get-tuple-element.176.refs_0_) | copy-start | bytes 688132
  64.1 37.8 %collective-permute-start.18 = (bf16[80,8,128]{2,1,0:T(8,128)(2,1)S(1)}, bf16[80,8,128]{2,1,0:T(8,128)(2,1)S(1)}, u32[]{:S(2)}, u32[]{:S(2)}) collective-permute-start(bf16[80,8,128]{2,1,0:T(8,128)(2,1)S(1)} %copy-done.14), channel_id=1, source_target_pairs={{0,4},{4,8},{8,12},{12,0},{1,5},{5,9},{9,13},{13,1},{2,6},{6,10},{... | collective-permute-start | bytes 491528 | tf_op jit(solution)/shard_map/ppermute | solution.py:445
  64.2 37.8 %collective-permute-start.19 = (bf16[80,8,128]{2,1,0:T(8,128)(2,1)S(1)}, bf16[80,8,128]{2,1,0:T(8,128)(2,1)S(1)}, u32[]{:S(2)}, u32[]{:S(2)}) collective-permute-start(bf16[80,8,128]{2,1,0:T(8,128)(2,1)S(1)} %copy-done.13), channel_id=1, source_target_pairs={{0,8},{4,12},{8,0},{12,4},{1,9},{5,13},{9,1},{13,5},{2,10},{6,14},... | collective-permute-start | bytes 491528 | tf_op jit(solution)/shard_map/ppermute | solution.py:445
  80.7 21.3 %collective-permute-start.20 = (bf16[80,8,128]{2,1,0:T(8,128)(2,1)S(1)}, bf16[80,8,128]{2,1,0:T(8,128)(2,1)S(1)}, u32[]{:S(2)}, u32[]{:S(2)}) collective-permute-start(bf16[80,8,128]{2,1,0:T(8,128)(2,1)S(1)} %copy-done.12), channel_id=1, source_target_pairs={{0,12},{4,0},{8,4},{12,8},{1,13},{5,1},{9,5},{13,9},{2,14},{6,2},{... | collective-permute-start | bytes 491528 | tf_op jit(solution)/shard_map/ppermute | solution.py:445
  87.2 14.7 %copy-start.15 = (bf16[64,8,128]{2,1,0:T(8,128)(2,1)S(1)}, bf16[64,8,128]{2,1,0:T(8,128)(2,1)}, u32[]{:S(2)}) copy-start(bf16[64,8,128]{2,1,0:T(8,128)(2,1)} %get-tuple-element.157) | copy-start | bytes 393220
  87.2 14.8 %copy-start.4 = (bf16[80,8,128]{2,1,0:T(8,128)(2,1)S(1)}, bf16[80,8,128]{2,1,0:T(8,128)(2,1)}, u32[]{:S(2)}) copy-start(bf16[80,8,128]{2,1,0:T(8,128)(2,1)} %get-tuple-element.172.refs_0_) | copy-start | bytes 491524
  87.2 21.7 %collective-permute-start.12 = (bf16[64,8,128]{2,1,0:T(8,128)(2,1)S(1)}, bf16[64,8,128]{2,1,0:T(8,128)(2,1)S(1)}, u32[]{:S(2)}, u32[]{:S(2)}) collective-permute-start(bf16[64,8,128]{2,1,0:T(8,128)(2,1)S(1)} %copy-done.17), channel_id=1, source_target_pairs={{0,4},{4,8},{8,12},{12,0},{1,5},{5,9},{9,13},{13,1},{2,6},{6,10},{... | collective-permute-start | bytes 393224 | tf_op jit(solution)/shard_map/ppermute | solution.py:445
  87.3 21.6 %collective-permute-start.13 = (bf16[64,8,128]{2,1,0:T(8,128)(2,1)S(1)}, bf16[64,8,128]{2,1,0:T(8,128)(2,1)S(1)}, u32[]{:S(2)}, u32[]{:S(2)}) collective-permute-start(bf16[64,8,128]{2,1,0:T(8,128)(2,1)S(1)} %copy-done.16), channel_id=1, source_target_pairs={{0,8},{4,12},{8,0},{12,4},{1,9},{5,13},{9,1},{13,5},{2,10},{6,14},... | collective-permute-start | bytes 393224 | tf_op jit(solution)/shard_map/ppermute | solution.py:445
  87.4 21.6 %slice-start = ((s8[6291456]{0:T(1024)(128)(4,1)}), s8[4194304]{0:T(1024)(128)(4,1)S(1)}, s32[]{:S(2)}) async-start(s8[6291456]{0:T(1024)(128)(4,1)} %bitcast.48), calls=%async_computation | async-start | bytes 8388608
  101.9 7.1 %copy-start.5 = (bf16[64,8,128]{2,1,0:T(8,128)(2,1)S(1)}, bf16[64,8,128]{2,1,0:T(8,128)(2,1)}, u32[]{:S(2)}) copy-start(bf16[64,8,128]{2,1,0:T(8,128)(2,1)} %get-tuple-element.154.refs_0_) | copy-start | bytes 393220
  101.9 7.1 %slice-start.1 = ((s8[6291456]{0:T(1024)(128)(4,1)}), s8[2097152]{0:T(1024)(128)(4,1)S(1)}, s32[]{:S(2)}) async-start(s8[6291456]{0:T(1024)(128)(4,1)} %bitcast.48), calls=%async_computation.1 | async-start | bytes 4194304
  101.9 7.0 %collective-permute-start.14 = (bf16[64,8,128]{2,1,0:T(8,128)(2,1)S(1)}, bf16[64,8,128]{2,1,0:T(8,128)(2,1)S(1)}, u32[]{:S(2)}, u32[]{:S(2)}) collective-permute-start(bf16[64,8,128]{2,1,0:T(8,128)(2,1)S(1)} %copy-done.15), channel_id=1, source_target_pairs={{0,12},{4,0},{8,4},{12,8},{1,13},{5,1},{9,5},{13,9},{2,14},{6,2},{... | collective-permute-start | bytes 393224 | tf_op jit(solution)/shard_map/ppermute | solution.py:445
  112.7 2.4 %collective-permute-start.22 = (bf16[12,256,128]{2,1,0:T(8,128)(2,1)S(1)}, bf16[12,256,128]{2,1,0:T(8,128)(2,1)S(1)}, u32[]{:S(2)}, u32[]{:S(2)}) collective-permute-start(bf16[12,256,128]{2,1,0:T(8,128)(2,1)S(1)} %get-tuple-element.212), channel_id=1, source_target_pairs={{0,1},{1,0},{2,3},{3,2},{4,5},{5,4},{6,7},{7,6},{8,9},{9,8},{10,11... | collective-permute-start | bytes 2359304 | tf_op jit(solution)/shard_map/ppermute | solution.py:408
  112.8 4.8 %collective-permute-start.21 = (bf16[12,256,128]{2,1,0:T(8,128)(2,1)S(1)}, bf16[12,256,128]{2,1,0:T(8,128)(2,1)S(1)}, u32[]{:S(2)}, u32[]{:S(2)}) collective-permute-start(bf16[12,256,128]{2,1,0:T(8,128)(2,1)S(1)} %get-tuple-element.213), channel_id=1, source_target_pairs={{0,1},{1,0},{2,3},{3,2},{4,5},{5,4},{6,7},{7,6},{8,9},{9,8},{10,11... | collective-permute-start | bytes 2359304 | tf_op jit(solution)/shard_map/ppermute | solution.py:408
  115.3 20.2 %collective-permute-start.23 = (bf16[12,256,128]{2,1,0:T(8,128)(2,1)S(1)}, bf16[12,256,128]{2,1,0:T(8,128)(2,1)S(1)}, u32[]{:S(2)}, u32[]{:S(2)}) collective-permute-start(bf16[12,256,128]{2,1,0:T(8,128)(2,1)S(1)} %fusion), channel_id=1, source_target_pairs={{0,2},{1,3},{2,0},{3,1},{4,6},{5,7},{6,4},{7,5},{8,10},{9,11},{10,... | collective-permute-start | bytes 2359304 | tf_op jit(solution)/shard_map/ppermute | solution.py:408

commit v4 on v3

--- a/solution.py
+++ b/solution.py
@@ -14,9 +14,9 @@
 ANY = pl.ANY
 BF16 = jnp.bfloat16
 INFO = 8
-CHUNKS = (2, 6, 7, 7, 5, 4)
+CHUNKS = (3, 7, 6, 5, 5, 5)
 TURN = 4
-AT_ONCE = 4
+AT_ONCE = 8
 DIGIT = 256
 PACK_MIB = 56
 
@@ -217,8 +217,7 @@
             return at + 1
 
         found = lax.fori_loop(begin, end, put, found)
-    for i in range(AT_ONCE - 1):
-        list_ref[found + i] = -1
+    list_ref[found] = -1
 
     def clear(b, carry):
         hist_ref[b] = jnp.zeros(hist_ref.shape[1:], jnp.float32)
@@ -291,7 +290,14 @@
             pair(AT_ONCE * i + j)
         return carry
 
-    lax.fori_loop(0, (found + AT_ONCE - 1) >> log2(AT_ONCE), group, 0)
+    whole_groups = found >> log2(AT_ONCE)
+    lax.fori_loop(0, whole_groups, group, 0)
+
+    def single(i, carry):
+        pair(2 * i)
+        return carry
+
+    lax.fori_loop(whole_groups * (AT_ONCE // 2), (found + 1) >> 1, single, 0)
     if not last:
         return
 

time: 137 us -> 131 us (0.956)
  the two profiles are of different devices: /device:TPU:8 before, /device:TPU:12 now
where the time goes in v4:
time: 131 us; the launch traced here: 133 us
  Pallas kernels  62 us (47%)
  waiting for transfers between devices  50.9 us (39%)
  starting transfers between devices  16.3 us (12%)
  other arithmetic  1.79 us (1%)
    pallas_call x6, Pallas kernels, add_tiles(): pl.pallas_call(functools.partial(hist_kernel, (first, last), skip, sender...  53 us
    ppermute x18, waiting for transfers between devices, exchange(): lax.ppermute(pieces[d], 'feat', [(i, (i + d) % owners) for i in range(own...  29.5 us
    ppermute x3, waiting for transfers between devices, reduce_rows(): moved = lax.ppermute(value, axis, [(i, i ^ bit) for i in range(n)])  21.3 us
    ppermute x18, starting transfers between devices, exchange(): lax.ppermute(pieces[d], 'feat', [(i, (i + d) % owners) for i in range(own...  15.6 us
    pallas_call x1, Pallas kernels, pack(): pl.pallas_call(functools.partial(pack_kernel, sizes, unit), out_shape=sha...  7.35 us
  transfers between devices with their start and end apart: 21, of which 11 were waited for; matrix products, arithmetic and copies ran while one was open for 1% of the time, Pallas kernels for 36%

profile of v4, /device:TPU:12, one launch (start us, length us, event | category | flops | bytes accessed | tf_op | source)
XLA Modules:
  0.0 132.5 jit_solution(10835313646243326458)
XLA Ops:
  0.0 7.3 %shard_map.73 = (bf16[58,8,128]{2,1,0:T(8,128)(2,1)}, bf16[58,8,128]{2,1,0:T(8,128)(2,1)}, bf16[58,8,128]{2,1,0:T(8,128)(2,1)}, bf16[58,8,128]{2,1,0:T(8,128)(2,...) custom-call(s32[1]{0:T(128)} %bitcast.4.me_ref, ...), custom_call_target="tpu_custom_call" | custom-call | bytes 8388608 | tf_op jit(solution)/shard_map/pallas_call | solution.py:159
  7.4 1.6 %collective-permute-start.3 = (bf16[58,8,128]{2,1,0:T(8,128)(2,1)}, bf16[58,8,128]{2,1,0:T(8,128)(2,1)S(1)}, u32[]{:S(2)}, u32[]{:S(2)}) collective-permute-start(bf16[58,8,128]{2,1,0:T(8,128)(2,1)} %get-tuple-element.127), channel_id=1, source_target_pairs={{0,4},{4,8},{8,12},{12,0},{1,5},{5,9},{9,13},{13,1},{2,6},{6,10},{... | collective-permute-start | bytes 356360 | tf_op jit(solution)/shard_map/ppermute | solution.py:451
  9.0 1.2 collective-permute-start.4
  10.2 1.8 %collective-permute-start.5 = (bf16[58,8,128]{2,1,0:T(8,128)(2,1)}, bf16[58,8,128]{2,1,0:T(8,128)(2,1)S(1)}, u32[]{:S(2)}, u32[]{:S(2)}) collective-permute-start(bf16[58,8,128]{2,1,0:T(8,128)(2,1)} %get-tuple-element.129), channel_id=1, source_target_pairs={{0,12},{4,0},{8,4},{12,8},{1,13},{5,1},{9,5},{13,9},{2,14},{6,2},{... | collective-permute-start | bytes 356360 | tf_op jit(solution)/shard_map/ppermute | solution.py:451
  12.0 0.2 collective-permute-start.6
  12.3 0.0 copy-done.6
  12.3 0.3 convert_multiply_fusion
  12.5 0.1 bitcast_bitcast_fusion.refs_5_
  12.6 3.6 %collective-permute-start.7 = (bf16[112,8,128]{2,1,0:T(8,128)(2,1)}, bf16[112,8,128]{2,1,0:T(8,128)(2,1)S(1)}, u32[]{:S(2)}, u32[]{:S(2)}) collective-permute-start(bf16[112,8,128]{2,1,0:T(8,128)(2,1)} %get-tuple-element.140), channel_id=1, source_target_pairs={{0,8},{4,12},{8,0},{12,4},{1,9},{5,13},{9,1},{13,5},{2,10},{6,14},... | collective-permute-start | bytes 688136 | tf_op jit(solution)/shard_map/ppermute | solution.py:451
  16.2 1.3 %collective-permute-done.3.refs_1_ = bf16[58,8,128]{2,1,0:T(8,128)(2,1)S(1)} collective-permute-done((bf16[58,8,128]{2,1,0:T(8,128)(2,1)}, bf16[58,8,128]{2,1,0:T(8,128)(2,1)S(1)}, u32[]{:S(2)}, u32[]{:S(2)}) %collective-permute-start.3) | collective-permute-done | bytes 118816 | tf_op jit(solution)/shard_map/ppermute | solution.py:451
  17.5 3.2 %collective-permute-done.4.refs_2_ = bf16[58,8,128]{2,1,0:T(8,128)(2,1)S(1)} collective-permute-done((bf16[58,8,128]{2,1,0:T(8,128)(2,1)}, bf16[58,8,128]{2,1,0:T(8,128)(2,1)S(1)}, u32[]{:S(2)}, u32[]{:S(2)}) %collective-permute-start.4) | collective-permute-done | bytes 118816 | tf_op jit(solution)/shard_map/ppermute | solution.py:451
  20.7 10.3 %collective-permute-done.5.refs_3_ = bf16[58,8,128]{2,1,0:T(8,128)(2,1)S(1)} collective-permute-done((bf16[58,8,128]{2,1,0:T(8,128)(2,1)}, bf16[58,8,128]{2,1,0:T(8,128)(2,1)S(1)}, u32[]{:S(2)}, u32[]{:S(2)}) %collective-permute-start.5) | collective-permute-done | bytes 118816 | tf_op jit(solution)/shard_map/ppermute | solution.py:451
  31.1 0.8 slice_reduce_fusion
  32.8 0.1 collective-permute-start.8
  32.8 0.1 pad_add_fusion.1.which_ref
  32.9 0.1 pad_add_fusion.5.which_ref
  33.0 0.1 pad_add_fusion.4.which_ref
  33.1 0.1 pad_add_fusion.3.which_ref
  33.1 0.0 copy-start.1
  33.2 2.1 %collective-permute-start.15 = (bf16[96,8,128]{2,1,0:T(8,128)(2,1)}, bf16[96,8,128]{2,1,0:T(8,128)(2,1)S(1)}, u32[]{:S(2)}, u32[]{:S(2)}) collective-permute-start(bf16[96,8,128]{2,1,0:T(8,128)(2,1)} %get-tuple-element.165), channel_id=1, source_target_pairs={{0,4},{4,8},{8,12},{12,0},{1,5},{5,9},{9,13},{13,1},{2,6},{6,10},{... | collective-permute-start | bytes 589832 | tf_op jit(solution)/shard_map/ppermute | solution.py:451
  35.2 0.0 collective-permute-start.16
  35.2 6.2 %shard_map.75.refs_6_ = f32[48,32,8,128]{3,2,1,0:T(8,128)S(1)} custom-call(s32[4]{0:T(128)S(1)} %pad_add_fusion.1.which_ref, s32[4,8,128]{2,1,0:T(8,128)S(1)} %get-tuple-element.369, bf16[58,8,128]{2,1,0:T(8,128)(2,1)S(1)} %copy-done, bf16[58,8,128]{2,1,0:T(8,128)(2,1)S(1)} %collective-permute-done.3.refs_1_, ...), custom_call_target="tpu_custom_call" | custom-call | flops 10000000000 | bytes 25165824 | tf_op jit(solution)/shard_map/pallas_call | solution.py:348
  41.4 0.1 pad_add_fusion.2.which_ref
  41.5 0.1 pad_add_fusion.6.which_ref
  41.6 0.0 collective-permute-done.6.refs_1_
  41.6 0.7 collective-permute-start.17
  42.3 2.2 %collective-permute-done.7.refs_2_ = bf16[112,8,128]{2,1,0:T(8,128)(2,1)S(1)} collective-permute-done((bf16[112,8,128]{2,1,0:T(8,128)(2,1)}, bf16[112,8,128]{2,1,0:T(8,128)(2,1)S(1)}, u32[]{:S(2)}, u32[]{:S(2)}) %collective-permute-start.7) | collective-permute-done | bytes 229408 | tf_op jit(solution)/shard_map/ppermute | solution.py:451
  44.5 5.5 %collective-permute-done.8.refs_3_ = bf16[112,8,128]{2,1,0:T(8,128)(2,1)S(1)} collective-permute-done((bf16[112,8,128]{2,1,0:T(8,128)(2,1)}, bf16[112,8,128]{2,1,0:T(8,128)(2,1)S(1)}, u32[]{:S(2)}, u32[]{:S(2)}) %collective-permute-start.8) | collective-permute-done | bytes 229408 | tf_op jit(solution)/shard_map/ppermute | solution.py:451
  50.0 0.1 collective-permute-start.9
  50.1 0.1 collective-permute-start.10
  50.2 11.6 %shard_map.76.refs_6_ = f32[48,32,8,128]{3,2,1,0:T(8,128)S(1)} custom-call(s32[4]{0:T(128)S(1)} %pad_add_fusion.2.which_ref, s32[4,8,128]{2,1,0:T(8,128)S(1)} %get-tuple-element.369, bf16[112,8,128]{2,1,0:T(8,128)(2,1)S(1)} %copy-done.1, bf16[112,8,128]{2,1,0:T(8,128)(2,1)S(1)} %collective-permute-done.6.refs_1_, ...), custom_call_target="tpu_custom_call", output_to_operand_aliasing={{}: (8, {})} | custom-call | flops 10000000000 | bytes 25165824 | tf_op jit(solution)/shard_map/pallas_call | solution.py:348
  61.8 0.0 collective-permute-done.15.refs_1_
  61.8 1.1 collective-permute-start.11
  62.9 0.0 collective-permute-done.16.refs_2_
  62.9 2.5 %collective-permute-done.17.refs_3_ = bf16[96,8,128]{2,1,0:T(8,128)(2,1)S(1)} collective-permute-done((bf16[96,8,128]{2,1,0:T(8,128)(2,1)S(1)}, bf16[96,8,128]{2,1,0:T(8,128)(2,1)S(1)}, u32[]{:S(2)}, u32[]{:S(2)}) %collective-permute-start.17) | collective-permute-done | bytes 196640 | tf_op jit(solution)/shard_map/ppermute | solution.py:451
  65.5 0.1 collective-permute-start.18
  65.5 2.7 %collective-permute-start.19 = (bf16[80,8,128]{2,1,0:T(8,128)(2,1)S(1)}, bf16[80,8,128]{2,1,0:T(8,128)(2,1)S(1)}, u32[]{:S(2)}, u32[]{:S(2)}) collective-permute-start(bf16[80,8,128]{2,1,0:T(8,128)(2,1)S(1)} %copy-done.12), channel_id=1, source_target_pairs={{0,8},{4,12},{8,0},{12,4},{1,9},{5,13},{9,1},{13,5},{2,10},{6,14},... | collective-permute-start | bytes 491528 | tf_op jit(solution)/shard_map/ppermute | solution.py:451
  68.2 10.9 %shard_map.77.refs_6_ = f32[48,32,8,128]{3,2,1,0:T(8,128)S(1)} custom-call(s32[4]{0:T(128)S(1)} %pad_add_fusion.3.which_ref, s32[4,8,128]{2,1,0:T(8,128)S(1)} %get-tuple-element.369, bf16[96,8,128]{2,1,0:T(8,128)(2,1)S(1)} %copy-done.2, bf16[96,8,128]{2,1,0:T(8,128)(2,1)S(1)} %collective-permute-done.15.refs_1_, ...), custom_call_target="tpu_custom_call", output_to_operand_aliasing={{}: (8, {})} | custom-call | flops 10000000000 | bytes 25165824 | tf_op jit(solution)/shard_map/pallas_call | solution.py:348
  79.2 0.0 collective-permute-done.9.refs_1_
  79.2 0.1 collective-permute-start.20
  79.2 0.0 collective-permute-done.10.refs_2_
  79.2 2.0 %collective-permute-done.11.refs_3_ = bf16[80,8,128]{2,1,0:T(8,128)(2,1)S(1)} collective-permute-done((bf16[80,8,128]{2,1,0:T(8,128)(2,1)S(1)}, bf16[80,8,128]{2,1,0:T(8,128)(2,1)S(1)}, u32[]{:S(2)}, u32[]{:S(2)}) %collective-permute-start.11) | collective-permute-done | bytes 163872 | tf_op jit(solution)/shard_map/ppermute | solution.py:451
  81.3 0.0 collective-permute-start.12
  81.3 0.3 collective-permute-start.13
  81.6 9.5 %shard_map.78.refs_6_ = f32[48,32,8,128]{3,2,1,0:T(8,128)S(1)} custom-call(s32[4]{0:T(128)S(1)} %pad_add_fusion.4.which_ref, s32[4,8,128]{2,1,0:T(8,128)S(1)} %get-tuple-element.369, bf16[80,8,128]{2,1,0:T(8,128)(2,1)S(1)} %copy-done.5, bf16[80,8,128]{2,1,0:T(8,128)(2,1)S(1)} %collective-permute-done.9.refs_1_, ...), custom_call_target="tpu_custom_call", output_to_operand_aliasing={{}: (8, {})} | custom-call | flops 10000000000 | bytes 25165824 | tf_op jit(solution)/shard_map/pallas_call | solution.py:348
  91.1 0.0 slice-start.1
  91.1 0.0 collective-permute-done.18.refs_1_
  91.1 0.1 collective-permute-start.14
  91.2 0.0 collective-permute-done.19.refs_2_
  91.2 2.4 %collective-permute-done.20.refs_3_ = bf16[80,8,128]{2,1,0:T(8,128)(2,1)S(1)} collective-permute-done((bf16[80,8,128]{2,1,0:T(8,128)(2,1)S(1)}, bf16[80,8,128]{2,1,0:T(8,128)(2,1)S(1)}, u32[]{:S(2)}, u32[]{:S(2)}) %collective-permute-start.20) | collective-permute-done | bytes 163872 | tf_op jit(solution)/shard_map/ppermute | solution.py:451
  93.6 9.2 %shard_map.79.refs_6_ = f32[48,32,8,128]{3,2,1,0:T(8,128)S(1)} custom-call(s32[4]{0:T(128)S(1)} %pad_add_fusion.5.which_ref, s32[4,8,128]{2,1,0:T(8,128)S(1)} %get-tuple-element.369, bf16[80,8,128]{2,1,0:T(8,128)(2,1)S(1)} %copy-done.4, bf16[80,8,128]{2,1,0:T(8,128)(2,1)S(1)} %collective-permute-done.18.refs_1_, ...), custom_call_target="tpu_custom_call", output_to_operand_aliasing={{}: (8, {})} | custom-call | flops 10000000000 | bytes 25165824 | tf_op jit(solution)/shard_map/pallas_call | solution.py:348
  102.8 0.0 collective-permute-done.12.refs_1_
  102.8 0.0 collective-permute-done.13.refs_2_
  102.8 0.0 collective-permute-done.14.refs_3_
  102.9 5.6 %shard_map.80 = (bf16[4,12,256,128]{3,2,1,0:T(8,128)(2,1)S(1)}, f32[48,32,8,128]{3,2,1,0:T(8,128)S(1)}) custom-call(s32[4]{0:T(128)S(1)} %pad_add_fusion.6.which_ref, s32[4,8,128]{2,1,0:T(8,128)S(1)} %get-tuple-element.369, bf16[80,8,128]{2,1,0:T(8,128)(2,1)S(1)} %copy-done.3, ...), custom_call_target="tpu_custom_call", output_to_operand_aliasing={{1}: (8, {})} | custom-call | flops 10000000000 | bytes 25165824 | tf_op jit(solution)/shard_map/pallas_call | solution.py:348
  108.5 0.2 slice_bitcast_fusion
  108.6 0.1 collective-permute-start.22
  108.7 0.5 collective-permute-start.21
  109.2 1.8 %collective-permute-done.22 = bf16[12,256,128]{2,1,0:T(8,128)(2,1)S(1)} collective-permute-done((bf16[12,256,128]{2,1,0:T(8,128)(2,1)S(1)}, bf16[12,256,128]{2,1,0:T(8,128)(2,1)S(1)}, u32[]{:S(2)}, u32[]{:S(2)}) %collective-permute-start.22) | collective-permute-done | bytes 786464 | tf_op jit(solution)/shard_map/ppermute | solution.py:414
  111.0 0.2 fusion
  111.2 0.1 collective-permute-start.23
  111.3 0.8 collective-permute-done.21.refs_1_
  112.1 18.7 %collective-permute-done.23.refs_2_ = bf16[12,256,128]{2,1,0:T(8,128)(2,1)S(1)} collective-permute-done((bf16[12,256,128]{2,1,0:T(8,128)(2,1)S(1)}, bf16[12,256,128]{2,1,0:T(8,128)(2,1)S(1)}, u32[]{:S(2)}, u32[]{:S(2)}) %collective-permute-start.23) | collective-permute-done | bytes 786464 | tf_op jit(solution)/shard_map/ppermute | solution.py:414
  130.8 1.7 %shard_map.81 = f32[8,32,1536]{2,1,0:T(8,128)} custom-call(bf16[12,256,128]{2,1,0:T(8,128)(2,1)S(1)} %get-tuple-element.214.refs_0_, bf16[12,256,128]{2,1,0:T(8,128)(2,1)S(1)} %collective-permute-done.21.refs_1_, bf16[12,256,128]{2,1,0:T(8,128)(2,1)S(1)} %collective-permute-done.23.refs_2_), custom_call_target="tpu_custom_call" | custom-call | tf_op jit(solution)/shard_map/pallas_call | solution.py:392
  (46 shorter events, 0.2 us)
Async XLA Ops:
  0.0 12.3 %copy-start.6 = (s32[31,6144]{1,0:T(8,128)S(1)}, s32[31,6144]{1,0:T(8,128)}, u32[]{:S(2)}) copy-start(s32[31,6144]{1,0:T(8,128)} %param.14) | copy-start | bytes 2285572
  7.4 23.7 %copy-start = (bf16[58,8,128]{2,1,0:T(8,128)(2,1)S(1)}, bf16[58,8,128]{2,1,0:T(8,128)(2,1)}, u32[]{:S(2)}) copy-start(bf16[58,8,128]{2,1,0:T(8,128)(2,1)} %get-tuple-element.134.refs_0_) | copy-start | bytes 356356
  7.4 10.2 %collective-permute-start.3 = (bf16[58,8,128]{2,1,0:T(8,128)(2,1)}, bf16[58,8,128]{2,1,0:T(8,128)(2,1)S(1)}, u32[]{:S(2)}, u32[]{:S(2)}) collective-permute-start(bf16[58,8,128]{2,1,0:T(8,128)(2,1)} %get-tuple-element.127), channel_id=1, source_target_pairs={{0,4},{4,8},{8,12},{12,0},{1,5},{5,9},{9,13},{13,1},{2,6},{6,10},{... | collective-permute-start | bytes 356360 | tf_op jit(solution)/shard_map/ppermute | solution.py:451
  9.0 11.7 %collective-permute-start.4 = (bf16[58,8,128]{2,1,0:T(8,128)(2,1)}, bf16[58,8,128]{2,1,0:T(8,128)(2,1)S(1)}, u32[]{:S(2)}, u32[]{:S(2)}) collective-permute-start(bf16[58,8,128]{2,1,0:T(8,128)(2,1)} %get-tuple-element.128), channel_id=1, source_target_pairs={{0,8},{4,12},{8,0},{12,4},{1,9},{5,13},{9,1},{13,5},{2,10},{6,14},... | collective-permute-start | bytes 356360 | tf_op jit(solution)/shard_map/ppermute | solution.py:451
  10.2 20.8 %collective-permute-start.5 = (bf16[58,8,128]{2,1,0:T(8,128)(2,1)}, bf16[58,8,128]{2,1,0:T(8,128)(2,1)S(1)}, u32[]{:S(2)}, u32[]{:S(2)}) collective-permute-start(bf16[58,8,128]{2,1,0:T(8,128)(2,1)} %get-tuple-element.129), channel_id=1, source_target_pairs={{0,12},{4,0},{8,4},{12,8},{1,13},{5,1},{9,5},{13,9},{2,14},{6,2},{... | collective-permute-start | bytes 356360 | tf_op jit(solution)/shard_map/ppermute | solution.py:451
  12.0 29.5 %collective-permute-start.6 = (bf16[112,8,128]{2,1,0:T(8,128)(2,1)}, bf16[112,8,128]{2,1,0:T(8,128)(2,1)S(1)}, u32[]{:S(2)}, u32[]{:S(2)}) collective-permute-start(bf16[112,8,128]{2,1,0:T(8,128)(2,1)} %get-tuple-element.139), channel_id=1, source_target_pairs={{0,4},{4,8},{8,12},{12,0},{1,5},{5,9},{9,13},{13,1},{2,6},{6,10},{... | collective-permute-start | bytes 688136 | tf_op jit(solution)/shard_map/ppermute | solution.py:451
  12.6 31.9 %collective-permute-start.7 = (bf16[112,8,128]{2,1,0:T(8,128)(2,1)}, bf16[112,8,128]{2,1,0:T(8,128)(2,1)S(1)}, u32[]{:S(2)}, u32[]{:S(2)}) collective-permute-start(bf16[112,8,128]{2,1,0:T(8,128)(2,1)} %get-tuple-element.140), channel_id=1, source_target_pairs={{0,8},{4,12},{8,0},{12,4},{1,9},{5,13},{9,1},{13,5},{2,10},{6,14},... | collective-permute-start | bytes 688136 | tf_op jit(solution)/shard_map/ppermute | solution.py:451
  32.8 17.2 %collective-permute-start.8 = (bf16[112,8,128]{2,1,0:T(8,128)(2,1)}, bf16[112,8,128]{2,1,0:T(8,128)(2,1)S(1)}, u32[]{:S(2)}, u32[]{:S(2)}) collective-permute-start(bf16[112,8,128]{2,1,0:T(8,128)(2,1)} %get-tuple-element.141), channel_id=1, source_target_pairs={{0,12},{4,0},{8,4},{12,8},{1,13},{5,1},{9,5},{13,9},{2,14},{6,2},{... | collective-permute-start | bytes 688136 | tf_op jit(solution)/shard_map/ppermute | solution.py:451
  33.1 8.4 %copy-start.7 = (bf16[96,8,128]{2,1,0:T(8,128)(2,1)S(1)}, bf16[96,8,128]{2,1,0:T(8,128)(2,1)}, u32[]{:S(2)}) copy-start(bf16[96,8,128]{2,1,0:T(8,128)(2,1)} %get-tuple-element.167) | copy-start | bytes 589828
  33.1 16.9 %copy-start.16 = (bf16[80,8,128]{2,1,0:T(8,128)(2,1)S(1)}, bf16[80,8,128]{2,1,0:T(8,128)(2,1)}, u32[]{:S(2)}) copy-start(bf16[80,8,128]{2,1,0:T(8,128)(2,1)} %get-tuple-element.147) | copy-start | bytes 491524
  33.1 16.9 %copy-start.15 = (bf16[80,8,128]{2,1,0:T(8,128)(2,1)S(1)}, bf16[80,8,128]{2,1,0:T(8,128)(2,1)}, u32[]{:S(2)}) copy-start(bf16[80,8,128]{2,1,0:T(8,128)(2,1)} %get-tuple-element.148) | copy-start | bytes 491524
  33.1 17.0 %copy-start.1 = (bf16[112,8,128]{2,1,0:T(8,128)(2,1)S(1)}, bf16[112,8,128]{2,1,0:T(8,128)(2,1)}, u32[]{:S(2)}) copy-start(bf16[112,8,128]{2,1,0:T(8,128)(2,1)} %get-tuple-element.184.refs_0_) | copy-start | bytes 688132
  33.2 28.6 %collective-permute-start.15 = (bf16[96,8,128]{2,1,0:T(8,128)(2,1)}, bf16[96,8,128]{2,1,0:T(8,128)(2,1)S(1)}, u32[]{:S(2)}, u32[]{:S(2)}) collective-permute-start(bf16[96,8,128]{2,1,0:T(8,128)(2,1)} %get-tuple-element.165), channel_id=1, source_target_pairs={{0,4},{4,8},{8,12},{12,0},{1,5},{5,9},{9,13},{13,1},{2,6},{6,10},{... | collective-permute-start | bytes 589832 | tf_op jit(solution)/shard_map/ppermute | solution.py:451
  35.2 27.7 %collective-permute-start.16 = (bf16[96,8,128]{2,1,0:T(8,128)(2,1)}, bf16[96,8,128]{2,1,0:T(8,128)(2,1)S(1)}, u32[]{:S(2)}, u32[]{:S(2)}) collective-permute-start(bf16[96,8,128]{2,1,0:T(8,128)(2,1)} %get-tuple-element.166), channel_id=1, source_target_pairs={{0,8},{4,12},{8,0},{12,4},{1,9},{5,13},{9,1},{13,5},{2,10},{6,14},... | collective-permute-start | bytes 589832 | tf_op jit(solution)/shard_map/ppermute | solution.py:451
  41.6 23.9 %collective-permute-start.17 = (bf16[96,8,128]{2,1,0:T(8,128)(2,1)S(1)}, bf16[96,8,128]{2,1,0:T(8,128)(2,1)S(1)}, u32[]{:S(2)}, u32[]{:S(2)}) collective-permute-start(bf16[96,8,128]{2,1,0:T(8,128)(2,1)S(1)} %copy-done.7), channel_id=1, source_target_pairs={{0,12},{4,0},{8,4},{12,8},{1,13},{5,1},{9,5},{13,9},{2,14},{6,2},{... | collective-permute-start | bytes 589832 | tf_op jit(solution)/shard_map/ppermute | solution.py:451
  50.0 11.8 %copy-start.14 = (bf16[80,8,128]{2,1,0:T(8,128)(2,1)S(1)}, bf16[80,8,128]{2,1,0:T(8,128)(2,1)}, u32[]{:S(2)}) copy-start(bf16[80,8,128]{2,1,0:T(8,128)(2,1)} %get-tuple-element.149) | copy-start | bytes 491524
  50.0 15.4 %copy-start.13 = (bf16[80,8,128]{2,1,0:T(8,128)(2,1)S(1)}, bf16[80,8,128]{2,1,0:T(8,128)(2,1)}, u32[]{:S(2)}) copy-start(bf16[80,8,128]{2,1,0:T(8,128)(2,1)} %get-tuple-element.173) | copy-start | bytes 491524
  50.0 15.5 %copy-start.12 = (bf16[80,8,128]{2,1,0:T(8,128)(2,1)S(1)}, bf16[80,8,128]{2,1,0:T(8,128)(2,1)}, u32[]{:S(2)}) copy-start(bf16[80,8,128]{2,1,0:T(8,128)(2,1)} %get-tuple-element.174) | copy-start | bytes 491524
  50.0 18.2 %copy-start.2 = (bf16[96,8,128]{2,1,0:T(8,128)(2,1)S(1)}, bf16[96,8,128]{2,1,0:T(8,128)(2,1)}, u32[]{:S(2)}) copy-start(bf16[96,8,128]{2,1,0:T(8,128)(2,1)} %get-tuple-element.180.refs_0_) | copy-start | bytes 589828
  50.0 29.1 %collective-permute-start.9 = (bf16[80,8,128]{2,1,0:T(8,128)(2,1)S(1)}, bf16[80,8,128]{2,1,0:T(8,128)(2,1)S(1)}, u32[]{:S(2)}, u32[]{:S(2)}) collective-permute-start(bf16[80,8,128]{2,1,0:T(8,128)(2,1)S(1)} %copy-done.16), channel_id=1, source_target_pairs={{0,4},{4,8},{8,12},{12,0},{1,5},{5,9},{9,13},{13,1},{2,6},{6,10},{... | collective-permute-start | bytes 491528 | tf_op jit(solution)/shard_map/ppermute | solution.py:451
  50.1 29.1 %collective-permute-start.10 = (bf16[80,8,128]{2,1,0:T(8,128)(2,1)S(1)}, bf16[80,8,128]{2,1,0:T(8,128)(2,1)S(1)}, u32[]{:S(2)}, u32[]{:S(2)}) collective-permute-start(bf16[80,8,128]{2,1,0:T(8,128)(2,1)S(1)} %copy-done.15), channel_id=1, source_target_pairs={{0,8},{4,12},{8,0},{12,4},{1,9},{5,13},{9,1},{13,5},{2,10},{6,14},... | collective-permute-start | bytes 491528 | tf_op jit(solution)/shard_map/ppermute | solution.py:451
  61.8 19.5 %collective-permute-start.11 = (bf16[80,8,128]{2,1,0:T(8,128)(2,1)S(1)}, bf16[80,8,128]{2,1,0:T(8,128)(2,1)S(1)}, u32[]{:S(2)}, u32[]{:S(2)}) collective-permute-start(bf16[80,8,128]{2,1,0:T(8,128)(2,1)S(1)} %copy-done.14), channel_id=1, source_target_pairs={{0,12},{4,0},{8,4},{12,8},{1,13},{5,1},{9,5},{13,9},{2,14},{6,2},{... | collective-permute-start | bytes 491528 | tf_op jit(solution)/shard_map/ppermute | solution.py:451
  65.4 13.7 %copy-start.11 = (bf16[80,8,128]{2,1,0:T(8,128)(2,1)S(1)}, bf16[80,8,128]{2,1,0:T(8,128)(2,1)}, u32[]{:S(2)}) copy-start(bf16[80,8,128]{2,1,0:T(8,128)(2,1)} %get-tuple-element.175) | copy-start | bytes 491524
  65.4 15.8 %copy-start.10 = (bf16[80,8,128]{2,1,0:T(8,128)(2,1)S(1)}, bf16[80,8,128]{2,1,0:T(8,128)(2,1)}, u32[]{:S(2)}) copy-start(bf16[80,8,128]{2,1,0:T(8,128)(2,1)} %get-tuple-element.155) | copy-start | bytes 491524
  65.4 15.9 %copy-start.9 = (bf16[80,8,128]{2,1,0:T(8,128)(2,1)S(1)}, bf16[80,8,128]{2,1,0:T(8,128)(2,1)}, u32[]{:S(2)}) copy-start(bf16[80,8,128]{2,1,0:T(8,128)(2,1)} %get-tuple-element.156) | copy-start | bytes 491524
  65.5 16.2 %copy-start.5 = (bf16[80,8,128]{2,1,0:T(8,128)(2,1)S(1)}, bf16[80,8,128]{2,1,0:T(8,128)(2,1)}, u32[]{:S(2)}) copy-start(bf16[80,8,128]{2,1,0:T(8,128)(2,1)} %get-tuple-element.176.refs_0_) | copy-start | bytes 491524
  65.5 25.6 %collective-permute-start.18 = (bf16[80,8,128]{2,1,0:T(8,128)(2,1)S(1)}, bf16[80,8,128]{2,1,0:T(8,128)(2,1)S(1)}, u32[]{:S(2)}, u32[]{:S(2)}) collective-permute-start(bf16[80,8,128]{2,1,0:T(8,128)(2,1)S(1)} %copy-done.13), channel_id=1, source_target_pairs={{0,4},{4,8},{8,12},{12,0},{1,5},{5,9},{9,13},{13,1},{2,6},{6,10},{... | collective-permute-start | bytes 491528 | tf_op jit(solution)/shard_map/ppermute | solution.py:451
  65.5 25.7 %collective-permute-start.19 = (bf16[80,8,128]{2,1,0:T(8,128)(2,1)S(1)}, bf16[80,8,128]{2,1,0:T(8,128)(2,1)S(1)}, u32[]{:S(2)}, u32[]{:S(2)}) collective-permute-start(bf16[80,8,128]{2,1,0:T(8,128)(2,1)S(1)} %copy-done.12), channel_id=1, source_target_pairs={{0,8},{4,12},{8,0},{12,4},{1,9},{5,13},{9,1},{13,5},{2,10},{6,14},... | collective-permute-start | bytes 491528 | tf_op jit(solution)/shard_map/ppermute | solution.py:451
  79.2 14.4 %collective-permute-start.20 = (bf16[80,8,128]{2,1,0:T(8,128)(2,1)S(1)}, bf16[80,8,128]{2,1,0:T(8,128)(2,1)S(1)}, u32[]{:S(2)}, u32[]{:S(2)}) collective-permute-start(bf16[80,8,128]{2,1,0:T(8,128)(2,1)S(1)} %copy-done.11), channel_id=1, source_target_pairs={{0,12},{4,0},{8,4},{12,8},{1,13},{5,1},{9,5},{13,9},{2,14},{6,2},{... | collective-permute-start | bytes 491528 | tf_op jit(solution)/shard_map/ppermute | solution.py:451
  81.3 9.8 %copy-start.8 = (bf16[80,8,128]{2,1,0:T(8,128)(2,1)S(1)}, bf16[80,8,128]{2,1,0:T(8,128)(2,1)}, u32[]{:S(2)}) copy-start(bf16[80,8,128]{2,1,0:T(8,128)(2,1)} %get-tuple-element.157) | copy-start | bytes 491524
  81.3 12.3 %copy-start.4 = (bf16[80,8,128]{2,1,0:T(8,128)(2,1)S(1)}, bf16[80,8,128]{2,1,0:T(8,128)(2,1)}, u32[]{:S(2)}) copy-start(bf16[80,8,128]{2,1,0:T(8,128)(2,1)} %get-tuple-element.172.refs_0_) | copy-start | bytes 491524
  81.3 21.5 %collective-permute-start.12 = (bf16[80,8,128]{2,1,0:T(8,128)(2,1)S(1)}, bf16[80,8,128]{2,1,0:T(8,128)(2,1)S(1)}, u32[]{:S(2)}, u32[]{:S(2)}) collective-permute-start(bf16[80,8,128]{2,1,0:T(8,128)(2,1)S(1)} %copy-done.10), channel_id=1, source_target_pairs={{0,4},{4,8},{8,12},{12,0},{1,5},{5,9},{9,13},{13,1},{2,6},{6,10},{... | collective-permute-start | bytes 491528 | tf_op jit(solution)/shard_map/ppermute | solution.py:451
  81.3 21.5 %collective-permute-start.13 = (bf16[80,8,128]{2,1,0:T(8,128)(2,1)S(1)}, bf16[80,8,128]{2,1,0:T(8,128)(2,1)S(1)}, u32[]{:S(2)}, u32[]{:S(2)}) collective-permute-start(bf16[80,8,128]{2,1,0:T(8,128)(2,1)S(1)} %copy-done.9), channel_id=1, source_target_pairs={{0,8},{4,12},{8,0},{12,4},{1,9},{5,13},{9,1},{13,5},{2,10},{6,14},... | collective-permute-start | bytes 491528 | tf_op jit(solution)/shard_map/ppermute | solution.py:451
  81.6 21.2 %slice-start = ((s8[6291456]{0:T(1024)(128)(4,1)}), s8[4194304]{0:T(1024)(128)(4,1)S(1)}, s32[]{:S(2)}) async-start(s8[6291456]{0:T(1024)(128)(4,1)} %bitcast.48), calls=%async_computation | async-start | bytes 8388608
  91.1 11.8 %copy-start.3 = (bf16[80,8,128]{2,1,0:T(8,128)(2,1)S(1)}, bf16[80,8,128]{2,1,0:T(8,128)(2,1)}, u32[]{:S(2)}) copy-start(bf16[80,8,128]{2,1,0:T(8,128)(2,1)} %get-tuple-element.154.refs_0_) | copy-start | bytes 491524
  91.1 11.8 %slice-start.1 = ((s8[6291456]{0:T(1024)(128)(4,1)}), s8[2097152]{0:T(1024)(128)(4,1)S(1)}, s32[]{:S(2)}) async-start(s8[6291456]{0:T(1024)(128)(4,1)} %bitcast.48), calls=%async_computation.1 | async-start | bytes 4194304
  91.1 11.7 %collective-permute-start.14 = (bf16[80,8,128]{2,1,0:T(8,128)(2,1)S(1)}, bf16[80,8,128]{2,1,0:T(8,128)(2,1)S(1)}, u32[]{:S(2)}, u32[]{:S(2)}) collective-permute-start(bf16[80,8,128]{2,1,0:T(8,128)(2,1)S(1)} %copy-done.8), channel_id=1, source_target_pairs={{0,12},{4,0},{8,4},{12,8},{1,13},{5,1},{9,5},{13,9},{2,14},{6,2},{... | collective-permute-start | bytes 491528 | tf_op jit(solution)/shard_map/ppermute | solution.py:451
  108.6 2.4 %collective-permute-start.22 = (bf16[12,256,128]{2,1,0:T(8,128)(2,1)S(1)}, bf16[12,256,128]{2,1,0:T(8,128)(2,1)S(1)}, u32[]{:S(2)}, u32[]{:S(2)}) collective-permute-start(bf16[12,256,128]{2,1,0:T(8,128)(2,1)S(1)} %get-tuple-element.212), channel_id=1, source_target_pairs={{0,1},{1,0},{2,3},{3,2},{4,5},{5,4},{6,7},{7,6},{8,9},{9,8},{10,11... | collective-permute-start | bytes 2359304 | tf_op jit(solution)/shard_map/ppermute | solution.py:414
  108.7 3.4 %collective-permute-start.21 = (bf16[12,256,128]{2,1,0:T(8,128)(2,1)S(1)}, bf16[12,256,128]{2,1,0:T(8,128)(2,1)S(1)}, u32[]{:S(2)}, u32[]{:S(2)}) collective-permute-start(bf16[12,256,128]{2,1,0:T(8,128)(2,1)S(1)} %get-tuple-element.213), channel_id=1, source_target_pairs={{0,1},{1,0},{2,3},{3,2},{4,5},{5,4},{6,7},{7,6},{8,9},{9,8},{10,11... | collective-permute-start | bytes 2359304 | tf_op jit(solution)/shard_map/ppermute | solution.py:414
  111.2 19.6 %collective-permute-start.23 = (bf16[12,256,128]{2,1,0:T(8,128)(2,1)S(1)}, bf16[12,256,128]{2,1,0:T(8,128)(2,1)S(1)}, u32[]{:S(2)}, u32[]{:S(2)}) collective-permute-start(bf16[12,256,128]{2,1,0:T(8,128)(2,1)S(1)} %fusion), channel_id=1, source_target_pairs={{0,2},{1,3},{2,0},{3,1},{4,6},{5,7},{6,4},{7,5},{8,10},{9,11},{10,... | collective-permute-start | bytes 2359304 | tf_op jit(solution)/shard_map/ppermute | solution.py:414
